TPU v7x, 128 devices: a whole 4x4x4 slice. The times are simulated.
128 devices in a mesh: req: 32 (over x, y, z_hi), rep: 4 (over z_lo, core).
Axes of the slice: x: 4, y: 4, z: 4 (z_hi: 2, z_lo: 2; z = z_hi * 2 + z_lo), core: 2. Of those that a mesh axis runs over, the one named last changes fastest.
Arguments:
- tokens: bfloat16 [128, 2, 2048], P('req'), may hold values from -6 to 6
- norm_gains: float32 [2, 2048], replicated, may hold values from 0.1 to 1.9
- w_kv: bfloat16 [2048, 2, 2048], P(None, None, 'rep'), may hold values from -0.125 to 0.125
- w_query: bfloat16 [32, 2048, 512], P('req', None, 'rep'), may hold values from -0.125 to 0.125
- w_out: bfloat16 [32, 512, 2048], P('req', 'rep'), may hold values from -0.5 to 0.5
- w_gate: bfloat16 [32, 2048, 1408], P('req', None, 'rep'), may hold values from -0.125 to 0.125
- w_up: bfloat16 [32, 2048, 1408], P('req', None, 'rep'), may hold values from -0.125 to 0.125
- w_down: bfloat16 [32, 1408, 2048], P('req', 'rep'), may hold values from -0.078125 to 0.078125
- kv_pages: bfloat16 [8192, 16, 2, 2048], P('req', None, None, 'rep'), may hold values from -80 to 80
- page_table: int32 [128, 64], P('req'), may hold values from 0 to 255, as said below
- cache_len: int32 [128], P('req'), may hold values from 1 to 1024
- route_ids: int32 [128, 2, 2, 2], P('req'), may hold values from 0 to 7, all different within a row
- route_gates: bfloat16 [128, 2, 2, 2], P('req'), may hold values from 0.19921875 to 1
- new_slot: int32 [128], P('req'), may hold values from 0 to 127, each once
Outputs:
- layer_out: bfloat16 [128, 2, 2048], P('req')
Inputs may be any that keep to these rules, and one draw needn't show every extreme that they name: `page_table`: row i lists 64 distinct pages of the pool of the device that holds request i; two requests of one device share no page.
All inputs are finite; a program needn't handle non-finite values.
Results may differ from a plain program's by a relative error of at most 0.022.
Values may be sent and summed in bfloat16 or wider, within the bound.
No kernel may reach another device: no remote copies, remote signals or barrier semaphores. Data moves between devices by JAX's collectives and lax.ppermute only.
A program may use at most 128 MiB of HBM per device.

v0:
```python
import functools
import math

import jax
import jax.numpy as jnp
from jax import lax
from jax.experimental import pallas as pl
from jax.experimental.pallas import tpu as pltpu
from jax.sharding import PartitionSpec as P

HD = 128
EXPERTS = 8
SPAN = 256
EPSILON = 1e-06
MASKED = -1e30
F32 = jnp.float32
BF16 = jnp.bfloat16
VM = pl.BlockSpec(memory_space=pltpu.VMEM)
SM = pl.BlockSpec(memory_space=pltpu.SMEM)
FAR = pl.BlockSpec(memory_space=pltpu.HBM)
ROWS_BY_ROWS = (((1,), (1,)), ((), ()))


def dot(a, b):
    return jnp.dot(a, b, preferred_element_type=F32)


def dot_rows(a, b):
    return lax.dot_general(a, b, ROWS_BY_ROWS, preferred_element_type=F32)


def call(body, out, ins, scratch=(), limit=12, outs=None):
    many = isinstance(out, (list, tuple))
    return pl.pallas_call(
        body,
        out_shape=out,
        in_specs=ins,
        out_specs=outs or ([VM] * len(out) if many else VM),
        scratch_shapes=scratch,
        compiler_params=pltpu.CompilerParams(vmem_limit_bytes=limit << 20),
    )


def in_hbm(value):
    return pltpu.with_memory_space_constraint(value, pltpu.HBM)


def in_vmem(value):
    return pltpu.with_memory_space_constraint(value, pltpu.VMEM)


def shape_of(shape, dtype=BF16):
    return jax.ShapeDtypeStruct(shape, dtype)


def message_kernel(slots_far, ids_far, tokens_far, gains_far, out, slots, ids, tokens, gains, sems):
    pairs = ((slots_far, slots), (ids_far, ids), (tokens_far, tokens), (gains_far, gains))
    copies = [pltpu.make_async_copy(a, b, sems.at[i]) for i, (a, b) in enumerate(pairs)]
    for copy in copies:
        copy.start()
    for copy in copies:
        copy.wait()
    count, _, width = tokens.shape
    rows = 2 * count
    half = width // 2
    rank, core = lax.axis_index("req"), lax.axis_index("rep") % 2
    x = tokens[...].reshape(rows, width).astype(F32)
    scaling = lax.rsqrt(jnp.mean(x * x, axis=1, keepdims=True) + EPSILON)
    normed = (x * scaling * gains[0:1]).astype(BF16)
    out[0, :, :half] = jnp.where(core == 0, normed[:, :half], normed[:, half:])
    row = lax.broadcasted_iota(jnp.int32, (rows, HD), 0)
    lane = lax.broadcasted_iota(jnp.int32, (rows, HD), 1)
    notes = jnp.zeros((rows, HD), jnp.int32)
    for j in range(count):
        for s in range(2):
            here = row == 2 * j + s
            source = 2 * (rank * count + j) if s == 0 else 2 * slots[j] + 1
            notes = jnp.where(here & (lane == 0), source, notes)
            for k in range(2):
                notes = jnp.where(here & (lane == 1 + k), ids[0, s, k, j], notes)
    out[0, :, half:] = notes.astype(F32).astype(BF16)
    message = out[0]
    for r in range(1, out.shape[0]):
        out[r] = message


def order_of(near):
    peers, rows, wide = near.shape
    source = near[:, :, wide - HD :].reshape(peers * rows, HD)[:, :1]
    column = lax.broadcasted_iota(jnp.int32, (peers * rows, peers * rows), 1)
    return (source.astype(jnp.int32) == column).astype(BF16)


def query_kernel(near, far, wq, out):
    peers, rows, wide = near.shape
    half = wide - HD
    core = lax.axis_index("rep") % 2
    a = near[:, :, :half].reshape(peers * rows, half)
    b = far[:, :, :half].reshape(peers * rows, half)
    q = dot(a, wq[0, pl.ds(pl.multiple_of(core * half, half), half)])
    q = q + dot(b, wq[0, pl.ds(pl.multiple_of((1 - core) * half, half), half)])
    out[...] = dot(order_of(near), q.astype(BF16)).astype(BF16).reshape(out.shape)


def own_kernel(near, far, wkv, sel, fresh):
    peers, rows, wide = near.shape
    half = wide - HD
    rank, core = lax.axis_index("req"), lax.axis_index("rep") % 2
    source = near[rank][:, half : half + 1]
    column = lax.broadcasted_iota(jnp.int32, (rows, peers * rows), 1)
    order = (source.astype(jnp.int32) == column).astype(BF16)
    a = dot(order, near[...].reshape(peers * rows, wide))
    b = dot(order, far[:, :, :half].reshape(peers * rows, half)).astype(BF16)
    sel[...] = a[:, half:]
    a = a[:, :half].astype(BF16)
    parts = (jnp.where(core == 0, a, b), jnp.where(core == 0, b, a))
    spans = half // HD
    chunks = [part[:, c * HD : (c + 1) * HD] for part in parts for c in range(spans)]
    twice = (HD, 2 * HD)
    feature = lax.broadcasted_iota(jnp.int32, twice, 1) // 2
    doubling = (lax.broadcasted_iota(jnp.int32, twice, 0) == feature).astype(BF16)
    doubled = dot(jnp.concatenate(chunks, axis=0), doubling)
    even = lax.broadcasted_iota(jnp.int32, (rows, 2 * HD), 1) % 2 == 0
    total = jnp.zeros(fresh.shape, F32)
    for c in range(2 * spans):
        v = doubled[c * rows : (c + 1) * rows]
        v = jnp.concatenate([jnp.where(even, v, 0.0), jnp.where(even, 0.0, v)], axis=0)
        w = wkv[c * HD : (c + 1) * HD].reshape(2 * HD, fresh.shape[1])
        total = total + dot(v.astype(BF16), w)
    fresh[...] = total.astype(BF16)


def page_kernel(table_far, lens_far, pool, out, table, lens, staged, sems, back, small):
    first = pltpu.make_async_copy(table_far, table, small.at[0])
    second = pltpu.make_async_copy(lens_far, lens, small.at[1])
    first.start()
    second.start()
    first.wait()
    second.wait()
    count, length = out.shape[:2]
    page = pool.shape[1]
    chunks = length // SPAN

    def each(act):
        for j in range(count):
            for c in range(chunks):
                pl.when(c * SPAN < lens[j])(functools.partial(act, j, c))

    def start(j, c):
        for p in range(SPAN // page):
            pltpu.make_async_copy(
                pool.at[table[j, c * (SPAN // page) + p]],
                staged.at[j, pl.ds(c * SPAN + p * page, page)],
                sems.at[j, c],
            ).start()

    def write(j, c):
        span = pl.ds(c * SPAN, SPAN)
        return pltpu.make_async_copy(staged.at[j, span], out.at[j, span], back.at[j, c])

    def forward(j, c):
        block = staged.at[j, pl.ds(c * SPAN, SPAN)]
        pltpu.make_async_copy(block, block, sems.at[j, c]).wait()
        write(j, c).start()

    def finish(j, c):
        write(j, c).wait()

    each(start)
    each(forward)
    each(finish)


def attention_kernel(lens, sel, arrived, fresh, cache_far, out, cache, qs, os, sc, ef, sems):
    def copy_of(j, c):
        span = pl.ds(c * SPAN, SPAN)
        return pltpu.make_async_copy(cache_far.at[j, span], cache.at[j, span], sems.at[j, c])

    for c in range(cache.shape[1] // SPAN):
        for j in range(cache.shape[0]):

            @pl.when(c * SPAN < lens[j])
            def _(j=j, c=c):
                copy_of(j, c).start()

    peers, rows, _ = arrived.shape
    count, _, _, wide = cache.shape
    heads = wide // HD
    group = 2 * heads
    inv_scale = 1.0 / math.sqrt(HD)
    picks = sel[...]
    masks = [[picks[:, 1 + k : 2 + k] == float(e) for e in range(EXPERTS)] for k in range(2)]
    for h in range(heads):
        values = [arrived[e * heads + h].astype(F32) for e in range(EXPERTS)]
        for k in range(2):
            total = jnp.where(masks[k][0], values[0], 0.0)
            for e in range(1, EXPERTS):
                total = total + jnp.where(masks[k][e], values[e], 0.0)
            qs[k * heads + h] = total
    ef[...] = jnp.zeros_like(ef)
    ef[0 : 2 * rows] = fresh[...]
    extra = ef[...]
    big = (2 * group, wide)
    block_row = lax.broadcasted_iota(jnp.int32, big, 0) % heads
    diagonal = block_row == lax.broadcasted_iota(jnp.int32, big, 1) // HD
    scores_shape = (2 * group, 2 * SPAN)
    column = lax.broadcasted_iota(jnp.int32, scores_shape, 1)
    keys = column % 2 == 0
    e_col = lax.broadcasted_iota(jnp.int32, (2 * group, HD), 1)
    e_row = lax.broadcasted_iota(jnp.int32, (2 * group, HD), 0)
    requests = range(count)

    def block(j, c):
        return cache[j, pl.ds(c * SPAN, SPAN)].reshape(2 * SPAN, wide)

    def masked_scores(q, j, c):
        copy_of(j, c).wait()
        s = dot_rows(q, block(j, c)) * inv_scale
        return jnp.where(keys & (column < 2 * (lens[j] - c * SPAN)), s, MASKED)

    def highest(s):
        return jnp.max(s, axis=1, keepdims=True)

    def added(p):
        return jnp.sum(p, axis=1, keepdims=True)

    def onto_values(p, distance=1):
        return pltpu.roll(p, distance, 1).astype(BF16)

    chunks = [(lens[j] + SPAN - 1) // SPAN for j in requests]
    queries, extras, firsts, tops = [], [], [], []
    for j in requests:
        q = jnp.concatenate([qs[:, 2 * j, :], qs[:, 2 * j + 1, :]], axis=0)
        q = jnp.where(diagonal, jnp.concatenate([q] * heads, axis=1), 0.0).astype(BF16)
        live = (e_col == 2 * j) | ((e_col == 2 * j + 1) & (e_row >= group))
        e = jnp.where(live, dot_rows(q, extra) * inv_scale, MASKED)
        s = masked_scores(q, j, 0)
        queries.append(q)
        extras.append(e)
        firsts.append(s)
        tops.append(jnp.maximum(highest(e), highest(s)))

    for j in requests:

        def score(c, top, j=j):
            s = masked_scores(queries[j], j, c)
            sc[j, c] = s
            return jnp.maximum(top, highest(s))

        tops[j] = lax.fori_loop(1, chunks[j], score, tops[j])

    extras = [jnp.exp(extras[j] - tops[j]) for j in requests]
    firsts = [jnp.exp(firsts[j] - tops[j]) for j in requests]
    sums = [added(extras[j]) + added(firsts[j]) for j in requests]
    for j in requests:

        def weigh(c, total, j=j):
            p = jnp.exp(sc[j, c] - tops[j])
            sc[j, c] = p
            return total + added(p)

        sums[j] = lax.fori_loop(1, chunks[j], weigh, sums[j])

    inverses = [1.0 / sums[j] for j in requests]
    mixed = [
        dot(onto_values(extras[j] * inverses[j], rows), extra)
        + dot(onto_values(firsts[j] * inverses[j]), block(j, 0))
        for j in requests
    ]
    for j in requests:

        def gather(c, total, j=j):
            return total + dot(onto_values(sc[j, c] * inverses[j]), block(j, c))

        mixed[j] = lax.fori_loop(1, chunks[j], gather, mixed[j])

    for j in requests:
        kept = jnp.where(diagonal, mixed[j], 0.0)
        o = kept[:, :HD]
        for h in range(1, heads):
            o = o + kept[:, h * HD : (h + 1) * HD]
        os[:, 2 * j, :] = o[:group]
        os[:, 2 * j + 1, :] = o[group:]
    for h in range(heads):
        first, second = os[h], os[heads + h]
        for e in range(EXPERTS):
            value = jnp.where(masks[0][e], first, 0.0) + jnp.where(masks[1][e], second, 0.0)
            out[e * heads + h] = value.astype(BF16)


def columns_of(z, core, quarter):
    return pl.ds(pl.multiple_of((2 * z + core) * quarter, quarter), quarter)


def project_kernel(near, returned, wo, answers, theirs):
    peers, halves, rows, quarter = theirs.shape
    core = lax.axis_index("rep") % 2
    values = returned[...].reshape(peers * rows, returned.shape[2])
    a = lax.dot_general(
        order_of(near), values, (((0,), (0,)), ((), ())), preferred_element_type=F32
    ).astype(BF16)
    answers[...] = a
    for z in range(halves):
        part = dot(a, wo[0, :, columns_of(z, 1 - core, quarter)])
        theirs[:, z] = part.astype(BF16).reshape(peers, rows, quarter)


def part_kernel(left, weight, out):
    peers, halves, rows, quarter = out.shape
    core = lax.axis_index("rep") % 2
    a = left[...]
    for z in range(halves):
        part = dot(a, weight[0, :, columns_of(z, core, quarter)])
        out[:, z] = part.reshape(peers, rows, quarter)


def place_kernel(*refs):
    pieces, out = refs[:-1], refs[-1]
    rep = lax.axis_index("rep")
    count, _, width = out.shape
    quarter = width // len(pieces)
    for m, piece in enumerate(pieces):
        place = pl.multiple_of((rep ^ m) * quarter, quarter)
        out[:, :, pl.ds(place, quarter)] = piece[...].reshape(count, 2, quarter)


def fetch_kernel(*refs):
    count = len(refs) // 2
    sems = refs[-1]
    copies = [pltpu.make_async_copy(refs[i], refs[count + i], sems.at[i]) for i in range(count)]
    for copy in copies:
        copy.start()
    for copy in copies:
        copy.wait()


def fetch(*arrays):
    return call(
        fetch_kernel,
        [pltpu.VMEM(a.shape, a.dtype) for a in arrays],
        [FAR] * len(arrays),
        [pltpu.SemaphoreType.DMA((len(arrays),))],
    )(*[in_hbm(a) for a in arrays])


def expert_kernel(near, far, gains, wg, wu, wd_far, units, theirs, wd, sem):
    load = pltpu.make_async_copy(wd_far, wd, sem)
    load.start()
    peers, halves, rows, quarter = near.shape
    core = lax.axis_index("rep") % 2
    total = peers * rows
    squares = jnp.zeros((total, 1), F32)
    for block in (near, far):
        for z in range(halves):
            v = block[:, z].reshape(total, quarter).astype(F32)
            squares = squares + jnp.sum(v * v, axis=1, keepdims=True)
    scaling = lax.rsqrt(squares / (2 * halves * quarter) + EPSILON)
    gate = jnp.zeros((total, wg.shape[1]), F32)
    up = jnp.zeros((total, wg.shape[1]), F32)
    for block, side in ((near, core), (far, 1 - core)):
        for z in range(halves):
            where = columns_of(z, side, quarter)
            v = block[:, z].reshape(total, quarter).astype(F32)
            v = (v * scaling * gains[1:2, where]).astype(BF16)
            gate = gate + dot_rows(v, wg[0, :, where])
            up = up + dot_rows(v, wu[0, :, where])
    a = (gate / (1.0 + jnp.exp(-gate)) * up).astype(BF16)
    units[...] = a
    load.wait()
    for z in range(halves):
        part = dot(a, wd[0, :, columns_of(z, 1 - core, quarter)])
        theirs[:, z] = part.astype(BF16).reshape(peers, rows, quarter)


def shards(
    tokens,
    norm_gains,
    w_kv,
    w_query,
    w_out,
    w_gate,
    w_up,
    w_down,
    kv_pages,
    page_table,
    cache_len,
    route_ids,
    route_gates,
    new_slot,
):
    req_count = lax.axis_size("req")
    rep_count = lax.axis_size("rep")
    mine, _, width = tokens.shape
    rows = 2 * mine
    total = rows * req_count
    half = width // 2
    quarter = width // rep_count
    wide = kv_pages.shape[-1]
    rep = lax.axis_index("rep")
    swap = [(p, p ^ 1) for p in range(rep_count)]
    wide_groups = [
        [r * rep_count + 2 * z + c for r in range(req_count) for z in range(rep_count // 2)]
        for c in range(2)
    ]
    peers = req_count * rep_count // 2
    split = (req_count, rep_count // 2, rows, quarter)

    def spread_req(value):
        return lax.all_to_all(value, "req", split_axis=0, concat_axis=0, tiled=True)

    def spread_wide(value):
        return lax.all_to_all(
            value,
            ("req", "rep"),
            split_axis=0,
            concat_axis=0,
            tiled=True,
            axis_index_groups=wide_groups,
        )

    def other_core(value):
        return lax.ppermute(value, "rep", swap)

    inputs = tokens.reshape(rows, width)
    ids = route_ids.transpose(0, 2, 1, 3).reshape(rows, 2, 2)
    gates = route_gates.astype(F32).transpose(0, 2, 1, 3).reshape(rows, 2, 2)
    experts_row = jnp.arange(EXPERTS, dtype=jnp.int32)
    shares = jnp.sum(jnp.where(ids[..., None] == experts_row, gates[..., None], 0.0), axis=2)

    routes = route_ids.transpose(1, 2, 3, 0)
    message = call(
        message_kernel,
        shape_of((req_count, rows, half + HD)),
        [FAR] * 4,
        [
            pltpu.SMEM(new_slot.shape, jnp.int32),
            pltpu.SMEM(routes.shape, jnp.int32),
            pltpu.VMEM(tokens.shape, BF16),
            pltpu.VMEM(norm_gains.shape, F32),
            pltpu.SemaphoreType.DMA((4,)),
        ],
    )(in_hbm(new_slot), in_hbm(routes), in_hbm(tokens), in_hbm(norm_gains))
    near = spread_req(message)
    length = page_table.shape[1] * kv_pages.shape[1]
    cache = call(
        page_kernel,
        pltpu.HBM((mine, length) + kv_pages.shape[2:], BF16),
        [FAR] * 3,
        [
            pltpu.SMEM(page_table.shape, jnp.int32),
            pltpu.SMEM(cache_len.shape, jnp.int32),
            pltpu.VMEM((mine, length) + kv_pages.shape[2:], BF16),
            pltpu.SemaphoreType.DMA((mine, length // SPAN)),
            pltpu.SemaphoreType.DMA((mine, length // SPAN)),
            pltpu.SemaphoreType.DMA((2,)),
        ],
        outs=FAR,
    )(in_hbm(page_table), in_hbm(cache_len), in_hbm(kv_pages))
    near, cache = lax.optimization_barrier((near, cache))
    far = other_core(near)
    ordered = call(query_kernel, shape_of((req_count, rows, HD)), [VM] * 3)(near, far, w_query)
    arrived = spread_req(ordered)
    sel, fresh = call(
        own_kernel, [shape_of((rows, HD), F32), shape_of((2 * rows, wide))], [VM] * 3
    )(near, far, w_kv)
    back = call(
        attention_kernel,
        shape_of((req_count, rows, HD)),
        [SM, VM, VM, VM, FAR],
        [
            pltpu.VMEM(cache.shape, BF16),
            pltpu.VMEM((2 * wide // HD, rows, HD), F32),
            pltpu.VMEM((2 * wide // HD, rows, HD), F32),
            pltpu.VMEM((mine, length // SPAN, 4 * wide // HD, 2 * SPAN), F32),
            pltpu.VMEM((HD, wide), BF16),
            pltpu.SemaphoreType.DMA((mine, length // SPAN)),
        ],
        16,
    )(cache_len, sel, arrived, fresh, in_hbm(cache))
    returned = spread_req(back)
    answers, theirs = call(
        project_kernel, [shape_of((total, w_out.shape[1])), shape_of(split)], [VM] * 3
    )(near, returned, w_out)

    def reduce_wide(left, theirs, weight, share):
        part = call(part_kernel, shape_of(split, F32), [VM] * 2)(left, weight)
        summed = (part + other_core(theirs).astype(F32)).astype(BF16)
        got = spread_wide(summed.reshape(peers, rows, quarter))
        got = got.reshape(EXPERTS, peers // EXPERTS, rows, quarter).astype(F32)
        return jnp.sum(jnp.sum(got, axis=1) * share.T[:, :, None], axis=0)

    kept = lax.dynamic_slice_in_dim(inputs, rep * quarter, quarter, 1).astype(F32)
    hidden = kept + reduce_wide(answers, theirs, w_out, shares[:, 0])
    copies = jnp.broadcast_to(hidden.astype(BF16)[None], (peers, rows, quarter))
    copies, *weights = lax.optimization_barrier(
        (copies, w_gate.transpose(0, 2, 1), w_up.transpose(0, 2, 1))
    )
    block = spread_wide(copies)
    block, *weights = lax.optimization_barrier((block, *fetch(*weights)))
    units, theirs, down = call(
        expert_kernel,
        [
            shape_of((total, w_down.shape[1])),
            shape_of(split),
            pltpu.VMEM(w_down.shape, BF16),
        ],
        [VM] * 5 + [FAR],
        [pltpu.SemaphoreType.DMA],
    )(
        block.reshape(split),
        other_core(block).reshape(split),
        norm_gains,
        *[in_vmem(w) for w in weights],
        in_hbm(w_down),
    )
    feed = reduce_wide(units, theirs, in_vmem(down), shares[:, 1])
    piece = (hidden + feed).astype(BF16)
    pieces = [piece] + [
        lax.ppermute(piece, "rep", [(p, p ^ m) for p in range(rep_count)])
        for m in range(1, rep_count)
    ]
    return call(place_kernel, shape_of((mine, 2, width)), [VM] * rep_count)(*pieces)


def solution(mesh):
    in_specs = (
        P("req", None, None),
        P(),
        P(None, None, "rep"),
        P("req", None, "rep"),
        P("req", "rep", None),
        P("req", None, "rep"),
        P("req", None, "rep"),
        P("req", "rep", None),
        P("req", None, None, "rep"),
        P("req", None),
        P("req"),
        P("req", None, None, None),
        P("req", None, None, None),
        P("req"),
    )
    out_specs = P("req", None, None)
    return jax.shard_map(shards, mesh=mesh, in_specs=in_specs, out_specs=out_specs, check_vma=False)
```

profile of v0, /device:TPU:1, one launch (start us, length us, event | category | flops | bytes accessed | tf_op | source)
XLA Modules:
  0.0 134.8 jit_solution(1354498869375156240)
XLA Ops:
  0.0 1.8 %shard_map.136 = bf16[32,8,1152]{2,1,0:T(8,128)(2,1)} custom-call(s32[4]{0:T(128)} %slots_far.1, s32[2,2,2,4]{3,2,1,0:T(2,128)} %bitcast.32, bf16[4,2,2048]{2,1,0:T(2,128)(2,1)} %tokens_far.1, f32[2,2048]{1,0:T(2,128)} %gains.1), custom_call_target="tpu_custom_call" | custom-call | tf_op jit(solution)/shard_map/pallas_call | solution.py:431
  1.8 11.2 %all-to-all-start = ((bf16[32,8,1152]{2,1,0:T(8,128)(2,1)}), bf16[32,8,1152]{2,1,0:T(8,128)(2,1)S(1)}, u32[]{:S(2)}, u32[]{:S(2)}) async-start(bf16[32,8,1152]{2,1,0:T(8,128)(2,1)} %shard_map.136), calls=%async_computation | async-start | bytes 1179648 | tf_op jit(solution)/shard_map/all_to_all | solution.py:409
  13.0 0.0 copy-start.2
  13.0 3.8 %shard_map.137.cache_far = bf16[4,1024,2,512]{3,2,1,0:T(2,128)(2,1)} custom-call(s32[4,64]{1,0:T(4,128)} %table_far.1, s32[4]{0:T(128)} %lens.1, bf16[256,16,2,512]{3,2,1,0:T(2,128)(2,1)} %pool.1), custom_call_target="tpu_custom_call" | custom-call | tf_op jit(solution)/shard_map/pallas_call | solution.py:445
  16.9 9.1 %all-to-all-done.near = bf16[32,8,1152]{2,1,0:T(8,128)(2,1)S(1)} async-done(((bf16[32,8,1152]{2,1,0:T(8,128)(2,1)}), bf16[32,8,1152]{2,1,0:T(8,128)(2,1)S(1)}, u32[]{:S(2)}, u32[]{:S(2)}) %all-to-all-start) | async-done | bytes 589856 | tf_op jit(solution)/shard_map/all_to_all | solution.py:409
  26.0 2.2 %collective-permute-start = (bf16[32,8,1152]{2,1,0:T(8,128)(2,1)S(1)}, bf16[32,8,1152]{2,1,0:T(8,128)(2,1)S(1)}, u32[]{:S(2)}, u32[]{:S(2)}) collective-permute-start(bf16[32,8,1152]{2,1,0:T(8,128)(2,1)S(1)} %all-to-all-done.near), channel_id=1, source_target_pairs={{0,1},{1,0},{2,3},{3,2},{4,5},{5,4},{6,7},{7,6},{8,9},{9,8},{10,11... | collective-permute-start | bytes 1769480 | tf_op jit(solution)/shard_map/ppermute | solution.py:422
  28.2 1.6 %collective-permute-done.far = bf16[32,8,1152]{2,1,0:T(8,128)(2,1)S(1)} collective-permute-done((bf16[32,8,1152]{2,1,0:T(8,128)(2,1)S(1)}, bf16[32,8,1152]{2,1,0:T(8,128)(2,1)S(1)}, u32[]{:S(2)}, u32[]{:S(2)}) %collective-permute-start) | collective-permute-done | bytes 589856 | tf_op jit(solution)/shard_map/ppermute | solution.py:422
  29.8 0.0 copy-done.2
  29.8 1.3 shard_map.139
  31.1 3.8 %all-to-all-start.1 = ((bf16[32,8,128]{2,1,0:T(8,128)(2,1)}), bf16[32,8,128]{2,1,0:T(8,128)(2,1)S(1)}, u32[]{:S(2)}, u32[]{:S(2)}) async-start(bf16[32,8,128]{2,1,0:T(8,128)(2,1)} %shard_map.139), calls=%async_computation.1 | async-start | bytes 131072 | tf_op jit(solution)/shard_map/all_to_all | solution.py:409
  35.0 0.0 copy-start
  35.0 2.2 %copy-done = bf16[2048,2,512]{2,1,0:T(2,128)(2,1)S(1)} copy-done((bf16[2048,2,512]{2,1,0:T(2,128)(2,1)S(1)}, bf16[2048,2,512]{2,1,0:T(2,128)(2,1)}, u32[]{:S(2)}) %copy-start) | copy-done | bytes 4194328
  37.1 0.0 copy-start.4
  37.1 1.0 shard_map.138
  38.2 5.4 %all-to-all-done.1.arrived = bf16[32,8,128]{2,1,0:T(8,128)(2,1)S(1)} async-done(((bf16[32,8,128]{2,1,0:T(8,128)(2,1)}), bf16[32,8,128]{2,1,0:T(8,128)(2,1)S(1)}, u32[]{:S(2)}, u32[]{:S(2)}) %all-to-all-start.1) | async-done | bytes 65568 | tf_op jit(solution)/shard_map/all_to_all | solution.py:409
  43.6 0.0 copy-done.4
  43.6 5.1 %shard_map.140 = bf16[32,8,128]{2,1,0:T(8,128)(2,1)S(1)} custom-call(s32[4]{0:T(128)S(1)} %copy-done.4, f32[8,128]{1,0:T(8,128)S(1)} %get-tuple-element.23.sel, bf16[32,8,128]{2,1,0:T(8,128)(2,1)S(1)} %all-to-all-done.1.arrived, bf16[16,512]{1,0:T(8,128)(2,1)S(1)} %get-tuple-element.24.fresh, bf16[4,1024,2,512]{3,2,1,0:T(2,128)(2,1)} %shard_map.137.cache_far), custom_call_target="tpu_custom_call" | custom-call | tf_op jit(solution)/shard_map/pallas_call | solution.py:466
  48.7 14.0 %all_to_all.30.returned = bf16[32,8,128]{2,1,0:T(8,128)(2,1)S(1)} all-to-all(bf16[32,8,128]{2,1,0:T(8,128)(2,1)S(1)} %shard_map.140), channel_id=1, replica_groups=mesh['req'=32,'rep'=4] {'req'}, dimensions={0} | all-to-all | bytes 131072 | tf_op jit(solution)/shard_map/all_to_all | solution.py:409
  62.7 0.0 copy-done.1
  62.7 0.5 shard_map.141
  63.3 2.8 %collective-permute-start.1 = (bf16[32,2,8,512]{3,2,1,0:T(8,128)(2,1)S(1)}, bf16[32,2,8,512]{3,2,1,0:T(8,128)(2,1)S(1)}, u32[]{:S(2)}, u32[]{:S(2)}) collective-permute-start(bf16[32,2,8,512]{3,2,1,0:T(8,128)(2,1)S(1)} %get-tuple-element.27), channel_id=1, source_target_pairs={{0,1},{1,0},{2,3},{3,2},{4,5},{5,4},{6,7},{7,6},{8,9},{9,8},{10,11... | collective-permute-start | bytes 1572872 | tf_op jit(solution)/shard_map/ppermute | solution.py:422
  66.1 0.0 copy-done.5
  66.1 0.3 shard_map.142
  66.4 0.0 copy-start.7
  66.4 0.0 copy-start.6
  66.4 1.2 collective-permute-done.1
  67.6 1.0 add_convert_fusion.1
  68.6 4.6 %all-to-all-start.3 = ((bf16[64,8,512]{2,1,0:T(8,128)(2,1)}), bf16[64,8,512]{2,1,0:T(8,128)(2,1)S(1)}, u32[]{:S(2)}, u32[]{:S(2)}) async-start(bf16[64,8,512]{2,1,0:T(8,128)(2,1)} %bitcast.1), calls=%async_computation.3 | async-start | bytes 1048576 | tf_op jit(solution)/shard_map/all_to_all | solution.py:412
  73.2 0.0 copy-done.7
  73.2 0.1 copy.28
  73.3 0.1 reshape.32
  73.4 0.0 copy-done.6
  73.4 0.1 copy.27
  73.5 0.1 eq.15
  73.6 0.1 select_reduce_fusion
  73.7 0.1 copy.29
  73.8 11.4 %all-to-all-done.3 = bf16[64,8,512]{2,1,0:T(8,128)(2,1)S(1)} async-done(((bf16[64,8,512]{2,1,0:T(8,128)(2,1)}), bf16[64,8,512]{2,1,0:T(8,128)(2,1)S(1)}, u32[]{:S(2)}, u32[]{:S(2)}) %all-to-all-start.3) | async-done | bytes 524320 | tf_op jit(solution)/shard_map/all_to_all | solution.py:412
  85.2 0.1 convert_reduce_fusion.1
  85.2 0.1 multiply_reduce_fusion.1
  85.4 0.8 broadcast_in_dim.30
  86.2 4.9 %all-to-all-start.4 = ((bf16[64,8,512]{2,1,0:T(8,128)(2,1)}), bf16[64,8,512]{2,1,0:T(8,128)(2,1)S(1)}, u32[]{:S(2)}, u32[]{:S(2)}) async-start(bf16[64,8,512]{2,1,0:T(8,128)(2,1)} %broadcast_in_dim.30), calls=%async_computation.4 | async-start | bytes 1048576 | tf_op jit(solution)/shard_map/all_to_all | solution.py:412
  91.0 0.0 copy-start.3
  91.1 1.8 %shard_map.143 = (bf16[1,352,2048]{2,1,0:T(8,128)(2,1)S(1)}, bf16[1,352,2048]{2,1,0:T(8,128)(2,1)S(1)}) custom-call(bf16[1,352,2048]{2,1,0:T(8,128)(2,1)} %bitcast.30, bf16[1,352,2048]{2,1,0:T(8,128)(2,1)} %bitcast.31), custom_call_target="tpu_custom_call" | custom-call | tf_op jit(solution)/shard_map/pallas_call | solution.py:338
  92.9 9.0 %all-to-all-done.4 = bf16[64,8,512]{2,1,0:T(8,128)(2,1)S(1)} async-done(((bf16[64,8,512]{2,1,0:T(8,128)(2,1)}), bf16[64,8,512]{2,1,0:T(8,128)(2,1)S(1)}, u32[]{:S(2)}, u32[]{:S(2)}) %all-to-all-start.4) | async-done | bytes 524320 | tf_op jit(solution)/shard_map/all_to_all | solution.py:412
  101.9 3.2 %collective-permute-start.2 = (bf16[64,8,512]{2,1,0:T(8,128)(2,1)S(1)}, bf16[64,8,512]{2,1,0:T(8,128)(2,1)S(1)}, u32[]{:S(2)}, u32[]{:S(2)}) collective-permute-start(bf16[64,8,512]{2,1,0:T(8,128)(2,1)S(1)} %all-to-all-done.4), channel_id=1, source_target_pairs={{0,1},{1,0},{2,3},{3,2},{4,5},{5,4},{6,7},{7,6},{8,9},{9,8},{10,11... | collective-permute-start | bytes 1572872 | tf_op jit(solution)/shard_map/ppermute | solution.py:422
  105.1 1.5 %collective-permute-done.2 = bf16[64,8,512]{2,1,0:T(8,128)(2,1)S(1)} collective-permute-done((bf16[64,8,512]{2,1,0:T(8,128)(2,1)S(1)}, bf16[64,8,512]{2,1,0:T(8,128)(2,1)S(1)}, u32[]{:S(2)}, u32[]{:S(2)}) %collective-permute-start.2) | collective-permute-done | bytes 524320 | tf_op jit(solution)/shard_map/ppermute | solution.py:422
  106.6 0.0 copy-done.3
  106.6 2.1 %shard_map.144 = (bf16[256,352]{1,0:T(8,128)(2,1)S(1)}, bf16[32,2,8,512]{3,2,1,0:T(8,128)(2,1)S(1)}, bf16[1,352,2048]{2,1,0:T(8,128)(2,1)S(1)}) custom-call(bf16[32,2,8,512]{3,2,1,0:T(8,128)(2,1)S(1)} %bitcast.28, bf16[32,2,8,512]{3,2,1,0:T(8,128)(2,1)S(1)} %bitcast.29, f32[2,2048]{1,0:T(2,128)S(1)} %copy-done.3, ...), custom_call_target="tpu_custom_call" | custom-call | tf_op jit(solution)/shard_map/pallas_call | solution.py:500
  108.8 0.5 collective-permute-start.3
  109.2 0.4 shard_map.145
  109.7 1.1 collective-permute-done.3
  110.8 1.0 add_convert_fusion
  111.7 4.6 %all-to-all-start.5 = ((bf16[64,8,512]{2,1,0:T(8,128)(2,1)}), bf16[64,8,512]{2,1,0:T(8,128)(2,1)S(1)}, u32[]{:S(2)}, u32[]{:S(2)}) async-start(bf16[64,8,512]{2,1,0:T(8,128)(2,1)} %bitcast.11), calls=%async_computation.5 | async-start | bytes 1048576 | tf_op jit(solution)/shard_map/all_to_all | solution.py:412
  116.4 0.1 copy.30
  116.4 11.9 %all-to-all-done.5 = bf16[64,8,512]{2,1,0:T(8,128)(2,1)S(1)} async-done(((bf16[64,8,512]{2,1,0:T(8,128)(2,1)}), bf16[64,8,512]{2,1,0:T(8,128)(2,1)S(1)}, u32[]{:S(2)}, u32[]{:S(2)}) %all-to-all-start.5) | async-done | bytes 524320 | tf_op jit(solution)/shard_map/all_to_all | solution.py:412
  128.3 0.1 convert_reduce_fusion
  128.4 0.1 multiply_reduce_fusion
  128.5 2.2 %collective-permute-start.4 = (bf16[8,512]{1,0:T(8,128)(2,1)S(1)}, bf16[8,512]{1,0:T(8,128)(2,1)S(1)}, u32[]{:S(2)}, u32[]{:S(2)}) collective-permute-start(bf16[8,512]{1,0:T(8,128)(2,1)S(1)} %add_convert_fusion.2.refs_0_), channel_id=1, source_target_pairs={{0,1},{1,0},{2,3},{3,2},{4,5},{5,4},{6,7},{7,6},{8,9},{9,8},{10,11... | collective-permute-start | bytes 24584 | tf_op jit(solution)/shard_map/ppermute | solution.py:519
  130.7 0.4 collective-permute-start.5
  131.1 1.3 collective-permute-start.6
  132.4 0.0 collective-permute-done.4.refs_1_
  132.4 0.8 collective-permute-done.5.refs_2_
  133.2 1.0 collective-permute-done.6.refs_3_
  134.1 0.6 shard_map.146
  (7 shorter events, 0.1 us)
Async XLA Ops:
  1.8 24.2 %all-to-all-start = ((bf16[32,8,1152]{2,1,0:T(8,128)(2,1)}), bf16[32,8,1152]{2,1,0:T(8,128)(2,1)S(1)}, u32[]{:S(2)}, u32[]{:S(2)}) async-start(bf16[32,8,1152]{2,1,0:T(8,128)(2,1)} %shard_map.136), calls=%async_computation | async-start | bytes 1179648 | tf_op jit(solution)/shard_map/all_to_all | solution.py:409
  13.0 16.8 %copy-start.2 = (bf16[1,2048,128]{2,1,0:T(8,128)(2,1)S(1)}, bf16[1,2048,128]{2,1,0:T(8,128)(2,1)}, u32[]{:S(2)}) copy-start(bf16[1,2048,128]{2,1,0:T(8,128)(2,1)} %wq.1) | copy-start | bytes 1572868
  26.0 3.8 %collective-permute-start = (bf16[32,8,1152]{2,1,0:T(8,128)(2,1)S(1)}, bf16[32,8,1152]{2,1,0:T(8,128)(2,1)S(1)}, u32[]{:S(2)}, u32[]{:S(2)}) collective-permute-start(bf16[32,8,1152]{2,1,0:T(8,128)(2,1)S(1)} %all-to-all-done.near), channel_id=1, source_target_pairs={{0,1},{1,0},{2,3},{3,2},{4,5},{5,4},{6,7},{7,6},{8,9},{9,8},{10,11... | collective-permute-start | bytes 1769480 | tf_op jit(solution)/shard_map/ppermute | solution.py:422
  31.1 12.5 %all-to-all-start.1 = ((bf16[32,8,128]{2,1,0:T(8,128)(2,1)}), bf16[32,8,128]{2,1,0:T(8,128)(2,1)S(1)}, u32[]{:S(2)}, u32[]{:S(2)}) async-start(bf16[32,8,128]{2,1,0:T(8,128)(2,1)} %shard_map.139), calls=%async_computation.1 | async-start | bytes 131072 | tf_op jit(solution)/shard_map/all_to_all | solution.py:409
  35.0 2.2 %copy-start = (bf16[2048,2,512]{2,1,0:T(2,128)(2,1)S(1)}, bf16[2048,2,512]{2,1,0:T(2,128)(2,1)}, u32[]{:S(2)}) copy-start(bf16[2048,2,512]{2,1,0:T(2,128)(2,1)} %wkv.1) | copy-start | bytes 12582916
  37.1 6.4 %copy-start.4 = (s32[4]{0:T(128)S(1)}, s32[4]{0:T(128)}, u32[]{:S(2)}) copy-start(s32[4]{0:T(128)} %lens.1) | copy-start | bytes 52
  43.6 19.1 %copy-start.1 = (bf16[1,128,2048]{2,1,0:T(8,128)(2,1)S(1)}, bf16[1,128,2048]{2,1,0:T(8,128)(2,1)}, u32[]{:S(2)}) copy-start(bf16[1,128,2048]{2,1,0:T(8,128)(2,1)} %weight.1) | copy-start | bytes 1572868
  43.6 22.5 %copy-start.5 = (bf16[4,2,2048]{2,1,0:T(2,128)(2,1)S(1)}, bf16[4,2,2048]{2,1,0:T(2,128)(2,1)}, u32[]{:S(2)}) copy-start(bf16[4,2,2048]{2,1,0:T(2,128)(2,1)} %tokens_far.1) | copy-start | bytes 98308
  63.3 4.3 %collective-permute-start.1 = (bf16[32,2,8,512]{3,2,1,0:T(8,128)(2,1)S(1)}, bf16[32,2,8,512]{3,2,1,0:T(8,128)(2,1)S(1)}, u32[]{:S(2)}, u32[]{:S(2)}) collective-permute-start(bf16[32,2,8,512]{3,2,1,0:T(8,128)(2,1)S(1)} %get-tuple-element.27), channel_id=1, source_target_pairs={{0,1},{1,0},{2,3},{3,2},{4,5},{5,4},{6,7},{7,6},{8,9},{9,8},{10,11... | collective-permute-start | bytes 1572872 | tf_op jit(solution)/shard_map/ppermute | solution.py:422
  66.4 6.8 %copy-start.7 = (bf16[4,2,2,2]{0,3,2,1:T(2,128)(2,1)S(1)}, bf16[4,2,2,2]{0,3,2,1:T(2,128)(2,1)}, u32[]{:S(2)}) copy-start(bf16[4,2,2,2]{0,3,2,1:T(2,128)(2,1)} %param.26) | copy-start | bytes 196
  66.4 7.0 %copy-start.6 = (s32[4,2,2,2]{0,3,2,1:T(2,128)S(1)}, s32[4,2,2,2]{0,3,2,1:T(2,128)}, u32[]{:S(2)}) copy-start(s32[4,2,2,2]{0,3,2,1:T(2,128)} %param.25) | copy-start | bytes 388
  68.6 16.6 %all-to-all-start.3 = ((bf16[64,8,512]{2,1,0:T(8,128)(2,1)}), bf16[64,8,512]{2,1,0:T(8,128)(2,1)S(1)}, u32[]{:S(2)}, u32[]{:S(2)}) async-start(bf16[64,8,512]{2,1,0:T(8,128)(2,1)} %bitcast.1), calls=%async_computation.3 | async-start | bytes 1048576 | tf_op jit(solution)/shard_map/all_to_all | solution.py:412
  86.2 15.7 %all-to-all-start.4 = ((bf16[64,8,512]{2,1,0:T(8,128)(2,1)}), bf16[64,8,512]{2,1,0:T(8,128)(2,1)S(1)}, u32[]{:S(2)}, u32[]{:S(2)}) async-start(bf16[64,8,512]{2,1,0:T(8,128)(2,1)} %broadcast_in_dim.30), calls=%async_computation.4 | async-start | bytes 1048576 | tf_op jit(solution)/shard_map/all_to_all | solution.py:412
  91.0 15.6 %copy-start.3 = (f32[2,2048]{1,0:T(2,128)S(1)}, f32[2,2048]{1,0:T(2,128)}, u32[]{:S(2)}) copy-start(f32[2,2048]{1,0:T(2,128)} %gains.1) | copy-start | bytes 49156
  101.9 4.8 %collective-permute-start.2 = (bf16[64,8,512]{2,1,0:T(8,128)(2,1)S(1)}, bf16[64,8,512]{2,1,0:T(8,128)(2,1)S(1)}, u32[]{:S(2)}, u32[]{:S(2)}) collective-permute-start(bf16[64,8,512]{2,1,0:T(8,128)(2,1)S(1)} %all-to-all-done.4), channel_id=1, source_target_pairs={{0,1},{1,0},{2,3},{3,2},{4,5},{5,4},{6,7},{7,6},{8,9},{9,8},{10,11... | collective-permute-start | bytes 1572872 | tf_op jit(solution)/shard_map/ppermute | solution.py:422
  108.8 2.0 %collective-permute-start.3 = (bf16[32,2,8,512]{3,2,1,0:T(8,128)(2,1)S(1)}, bf16[32,2,8,512]{3,2,1,0:T(8,128)(2,1)S(1)}, u32[]{:S(2)}, u32[]{:S(2)}) collective-permute-start(bf16[32,2,8,512]{3,2,1,0:T(8,128)(2,1)S(1)} %get-tuple-element.38), channel_id=1, source_target_pairs={{0,1},{1,0},{2,3},{3,2},{4,5},{5,4},{6,7},{7,6},{8,9},{9,8},{10,11... | collective-permute-start | bytes 1572872 | tf_op jit(solution)/shard_map/ppermute | solution.py:422
  111.7 16.6 %all-to-all-start.5 = ((bf16[64,8,512]{2,1,0:T(8,128)(2,1)}), bf16[64,8,512]{2,1,0:T(8,128)(2,1)S(1)}, u32[]{:S(2)}, u32[]{:S(2)}) async-start(bf16[64,8,512]{2,1,0:T(8,128)(2,1)} %bitcast.11), calls=%async_computation.5 | async-start | bytes 1048576 | tf_op jit(solution)/shard_map/all_to_all | solution.py:412
  128.5 3.9 %collective-permute-start.4 = (bf16[8,512]{1,0:T(8,128)(2,1)S(1)}, bf16[8,512]{1,0:T(8,128)(2,1)S(1)}, u32[]{:S(2)}, u32[]{:S(2)}) collective-permute-start(bf16[8,512]{1,0:T(8,128)(2,1)S(1)} %add_convert_fusion.2.refs_0_), channel_id=1, source_target_pairs={{0,1},{1,0},{2,3},{3,2},{4,5},{5,4},{6,7},{7,6},{8,9},{9,8},{10,11... | collective-permute-start | bytes 24584 | tf_op jit(solution)/shard_map/ppermute | solution.py:519
  130.7 2.5 %collective-permute-start.5 = (bf16[8,512]{1,0:T(8,128)(2,1)S(1)}, bf16[8,512]{1,0:T(8,128)(2,1)S(1)}, u32[]{:S(2)}, u32[]{:S(2)}) collective-permute-start(bf16[8,512]{1,0:T(8,128)(2,1)S(1)} %add_convert_fusion.2.refs_0_), channel_id=1, source_target_pairs={{0,2},{1,3},{2,0},{3,1},{4,6},{5,7},{6,4},{7,5},{8,10},{9,11},{10,... | collective-permute-start | bytes 24584 | tf_op jit(solution)/shard_map/ppermute | solution.py:519
  131.1 3.1 %collective-permute-start.6 = (bf16[8,512]{1,0:T(8,128)(2,1)S(1)}, bf16[8,512]{1,0:T(8,128)(2,1)S(1)}, u32[]{:S(2)}, u32[]{:S(2)}) collective-permute-start(bf16[8,512]{1,0:T(8,128)(2,1)S(1)} %add_convert_fusion.2.refs_0_), channel_id=1, source_target_pairs={{0,3},{1,2},{2,1},{3,0},{4,7},{5,6},{6,5},{7,4},{8,11},{9,10},{10,... | collective-permute-start | bytes 24584 | tf_op jit(solution)/shard_map/ppermute | solution.py:519
where the time goes:
time: 135 us
  waiting for transfers between devices  54.1 us (40%)
  starting transfers between devices  41.7 us (31%)
  Pallas kernels  18.8 us (14%)
  blocking collectives  14 us (10%)
  local copies, waits for them, and re-layouts  3.6 us (3%)
  other arithmetic  2.34 us (2%)
    all_to_all x3, waiting for transfers between devices, spread_wide(): lax.all_to_all(value, ('req', 'rep'), split_axis=0, concat_axis=0, tiled=...  32.3 us
    all_to_all x2, starting transfers between devices, spread_req(): return lax.all_to_all(value, 'req', split_axis=0, concat_axis=0, tiled=True)  15 us
    all_to_all x2, waiting for transfers between devices, spread_req(): return lax.all_to_all(value, 'req', split_axis=0, concat_axis=0, tiled=True)  14.6 us
    all_to_all x3, starting transfers between devices, spread_wide(): lax.all_to_all(value, ('req', 'rep'), split_axis=0, concat_axis=0, tiled=...  14.1 us
    all_to_all x1, blocking collectives, spread_req(): return lax.all_to_all(value, 'req', split_axis=0, concat_axis=0, tiled=True)  14 us
    ppermute x4, starting transfers between devices, other_core(): return lax.ppermute(value, 'rep', swap)  8.65 us
    ppermute x4, waiting for transfers between devices, other_core(): return lax.ppermute(value, 'rep', swap)  5.46 us
    pallas_call x1, Pallas kernels, shards(): call(attention_kernel, shape_of((req_count, rows, HD)), [SM, VM, VM, VM,...  5.09 us
  transfers between devices with their start and end apart: 12, of which 11 were waited for; matrix products, arithmetic and copies ran while one was open for 0% of the time, Pallas kernels for 5%

commit v1 on v0

--- a/solution.py
+++ b/solution.py
@@ -84,22 +84,32 @@
         out[r] = message
 
 
-def order_of(near):
-    peers, rows, wide = near.shape
-    source = near[:, :, wide - HD :].reshape(peers * rows, HD)[:, :1]
-    column = lax.broadcasted_iota(jnp.int32, (peers * rows, peers * rows), 1)
+def order_of(notes):
+    source = notes[:, :1]
+    column = lax.broadcasted_iota(jnp.int32, (notes.shape[0], notes.shape[0]), 1)
     return (source.astype(jnp.int32) == column).astype(BF16)
 
 
-def query_kernel(near, far, wq, out):
+def near_query_kernel(near, wq_far, wq, out, sem):
+    load = pltpu.make_async_copy(wq_far, wq, sem)
+    load.start()
     peers, rows, wide = near.shape
     half = wide - HD
     core = lax.axis_index("rep") % 2
     a = near[:, :, :half].reshape(peers * rows, half)
+    load.wait()
+    out[...] = dot(a, wq[0, pl.ds(pl.multiple_of(core * half, half), half)])
+
+
+def query_kernel(near, far, wq, begun, out, notes):
+    peers, rows, wide = near.shape
+    half = wide - HD
+    core = lax.axis_index("rep") % 2
     b = far[:, :, :half].reshape(peers * rows, half)
-    q = dot(a, wq[0, pl.ds(pl.multiple_of(core * half, half), half)])
-    q = q + dot(b, wq[0, pl.ds(pl.multiple_of((1 - core) * half, half), half)])
-    out[...] = dot(order_of(near), q.astype(BF16)).astype(BF16).reshape(out.shape)
+    q = begun[...] + dot(b, wq[0, pl.ds(pl.multiple_of((1 - core) * half, half), half)])
+    marks = near[:, :, half:].reshape(peers * rows, HD)
+    notes[...] = marks
+    out[...] = dot(order_of(marks), q.astype(BF16)).astype(BF16).reshape(out.shape)
 
 
 def own_kernel(near, far, wkv, sel, fresh):
@@ -130,61 +140,67 @@
     fresh[...] = total.astype(BF16)
 
 
-def page_kernel(table_far, lens_far, pool, out, table, lens, staged, sems, back, small):
+def page_kernel(table_far, lens_far, pool, start, out, table, lens, staged, sems, back, small):
     first = pltpu.make_async_copy(table_far, table, small.at[0])
     second = pltpu.make_async_copy(lens_far, lens, small.at[1])
     first.start()
     second.start()
     first.wait()
     second.wait()
-    count, length = out.shape[:2]
+    count = out.shape[0]
     page = pool.shape[1]
-    chunks = length // SPAN
+    chunks = 1 + out.shape[1] // SPAN
 
     def each(act):
         for j in range(count):
             for c in range(chunks):
                 pl.when(c * SPAN < lens[j])(functools.partial(act, j, c))
 
-    def start(j, c):
+    def block_of(j, c):
+        return start.at[j] if c == 0 else staged.at[j, pl.ds((c - 1) * SPAN, SPAN)]
+
+    def read(j, c):
+        block = block_of(j, c)
         for p in range(SPAN // page):
             pltpu.make_async_copy(
                 pool.at[table[j, c * (SPAN // page) + p]],
-                staged.at[j, pl.ds(c * SPAN + p * page, page)],
+                block.at[pl.ds(p * page, page)],
                 sems.at[j, c],
             ).start()
 
     def write(j, c):
-        span = pl.ds(c * SPAN, SPAN)
-        return pltpu.make_async_copy(staged.at[j, span], out.at[j, span], back.at[j, c])
+        place = out.at[j, pl.ds((c - 1) * SPAN, SPAN)]
+        return pltpu.make_async_copy(block_of(j, c), place, back.at[j, c])
 
     def forward(j, c):
-        block = staged.at[j, pl.ds(c * SPAN, SPAN)]
+        block = block_of(j, c)
         pltpu.make_async_copy(block, block, sems.at[j, c]).wait()
-        write(j, c).start()
+        if c:
+            write(j, c).start()
 
     def finish(j, c):
-        write(j, c).wait()
-
-    each(start)
+        if c:
+            write(j, c).wait()
+
+    each(read)
     each(forward)
     each(finish)
 
 
-def attention_kernel(lens, sel, arrived, fresh, cache_far, out, cache, qs, os, sc, ef, sems):
+def attention_kernel(lens, sel, arrived, fresh, start, far, out, cache, qs, os, sc, ef, sems):
     def copy_of(j, c):
-        span = pl.ds(c * SPAN, SPAN)
-        return pltpu.make_async_copy(cache_far.at[j, span], cache.at[j, span], sems.at[j, c])
-
-    for c in range(cache.shape[1] // SPAN):
-        for j in range(cache.shape[0]):
+        span = pl.ds((c - 1) * SPAN, SPAN)
+        return pltpu.make_async_copy(far.at[j, span], cache.at[j, span], sems.at[j, c])
+
+    count, _, _, wide = cache.shape
+    for c in range(1, 1 + cache.shape[1] // SPAN):
+        for j in range(count):
 
             @pl.when(c * SPAN < lens[j])
             def _(j=j, c=c):
                 copy_of(j, c).start()
 
     peers, rows, _ = arrived.shape
-    count, _, _, wide = cache.shape
     heads = wide // HD
     group = 2 * heads
     inv_scale = 1.0 / math.sqrt(HD)
@@ -210,12 +226,14 @@
     e_row = lax.broadcasted_iota(jnp.int32, (2 * group, HD), 0)
     requests = range(count)
 
+    def first(j):
+        return start[j].reshape(2 * SPAN, wide)
+
     def block(j, c):
-        return cache[j, pl.ds(c * SPAN, SPAN)].reshape(2 * SPAN, wide)
-
-    def masked_scores(q, j, c):
-        copy_of(j, c).wait()
-        s = dot_rows(q, block(j, c)) * inv_scale
+        return cache[j, pl.ds((c - 1) * SPAN, SPAN)].reshape(2 * SPAN, wide)
+
+    def masked_scores(q, rows_of, j, c):
+        s = dot_rows(q, rows_of) * inv_scale
         return jnp.where(keys & (column < 2 * (lens[j] - c * SPAN)), s, MASKED)
 
     def highest(s):
@@ -234,7 +252,7 @@
         q = jnp.where(diagonal, jnp.concatenate([q] * heads, axis=1), 0.0).astype(BF16)
         live = (e_col == 2 * j) | ((e_col == 2 * j + 1) & (e_row >= group))
         e = jnp.where(live, dot_rows(q, extra) * inv_scale, MASKED)
-        s = masked_scores(q, j, 0)
+        s = masked_scores(q, first(j), j, 0)
         queries.append(q)
         extras.append(e)
         firsts.append(s)
@@ -243,8 +261,9 @@
     for j in requests:
 
         def score(c, top, j=j):
-            s = masked_scores(queries[j], j, c)
-            sc[j, c] = s
+            copy_of(j, c).wait()
+            s = masked_scores(queries[j], block(j, c), j, c)
+            sc[j, c - 1] = s
             return jnp.maximum(top, highest(s))
 
         tops[j] = lax.fori_loop(1, chunks[j], score, tops[j])
@@ -252,39 +271,30 @@
     extras = [jnp.exp(extras[j] - tops[j]) for j in requests]
     firsts = [jnp.exp(firsts[j] - tops[j]) for j in requests]
     sums = [added(extras[j]) + added(firsts[j]) for j in requests]
-    for j in requests:
-
-        def weigh(c, total, j=j):
-            p = jnp.exp(sc[j, c] - tops[j])
-            sc[j, c] = p
-            return total + added(p)
-
-        sums[j] = lax.fori_loop(1, chunks[j], weigh, sums[j])
-
-    inverses = [1.0 / sums[j] for j in requests]
     mixed = [
-        dot(onto_values(extras[j] * inverses[j], rows), extra)
-        + dot(onto_values(firsts[j] * inverses[j]), block(j, 0))
+        dot(onto_values(extras[j], rows), extra) + dot(onto_values(firsts[j]), first(j))
         for j in requests
     ]
     for j in requests:
 
-        def gather(c, total, j=j):
-            return total + dot(onto_values(sc[j, c] * inverses[j]), block(j, c))
-
-        mixed[j] = lax.fori_loop(1, chunks[j], gather, mixed[j])
+        def gather(c, state, j=j):
+            p = jnp.exp(sc[j, c - 1] - tops[j])
+            return state[0] + added(p), state[1] + dot(onto_values(p), block(j, c))
+
+        sums[j], mixed[j] = lax.fori_loop(1, chunks[j], gather, (sums[j], mixed[j]))
 
     for j in requests:
         kept = jnp.where(diagonal, mixed[j], 0.0)
         o = kept[:, :HD]
         for h in range(1, heads):
             o = o + kept[:, h * HD : (h + 1) * HD]
+        o = o / sums[j]
         os[:, 2 * j, :] = o[:group]
         os[:, 2 * j + 1, :] = o[group:]
     for h in range(heads):
-        first, second = os[h], os[heads + h]
+        one, two = os[h], os[heads + h]
         for e in range(EXPERTS):
-            value = jnp.where(masks[0][e], first, 0.0) + jnp.where(masks[1][e], second, 0.0)
+            value = jnp.where(masks[0][e], one, 0.0) + jnp.where(masks[1][e], two, 0.0)
             out[e * heads + h] = value.astype(BF16)
 
 
@@ -292,12 +302,12 @@
     return pl.ds(pl.multiple_of((2 * z + core) * quarter, quarter), quarter)
 
 
-def project_kernel(near, returned, wo, answers, theirs):
+def project_kernel(notes, returned, wo, answers, theirs):
     peers, halves, rows, quarter = theirs.shape
     core = lax.axis_index("rep") % 2
     values = returned[...].reshape(peers * rows, returned.shape[2])
     a = lax.dot_general(
-        order_of(near), values, (((0,), (0,)), ((), ())), preferred_element_type=F32
+        order_of(notes[...]), values, (((0,), (0,)), ((), ())), preferred_element_type=F32
     ).astype(BF16)
     answers[...] = a
     for z in range(halves):
@@ -324,49 +334,47 @@
         out[:, :, pl.ds(place, quarter)] = piece[...].reshape(count, 2, quarter)
 
 
-def fetch_kernel(*refs):
-    count = len(refs) // 2
-    sems = refs[-1]
-    copies = [pltpu.make_async_copy(refs[i], refs[count + i], sems.at[i]) for i in range(count)]
+def raw_products(block, side, gains, wg, wu):
+    peers, halves, rows, quarter = block.shape
+    total = peers * rows
+    squares = jnp.zeros((total, 1), F32)
+    gate = jnp.zeros((total, wg.shape[1]), F32)
+    up = jnp.zeros((total, wg.shape[1]), F32)
+    for z in range(halves):
+        where = columns_of(z, side, quarter)
+        v = block[:, z].reshape(total, quarter).astype(F32)
+        squares = squares + jnp.sum(v * v, axis=1, keepdims=True)
+        v = (v * gains[1:2, where]).astype(BF16)
+        gate = gate + dot_rows(v, wg[0, :, where])
+        up = up + dot_rows(v, wu[0, :, where])
+    return squares, gate, up
+
+
+def near_kernel(near, gains, wg_far, wu_far, wd_far, wg, wu, wd, squares, gate, up, sems):
+    pairs = ((wg_far, wg), (wu_far, wu), (wd_far, wd))
+    copies = [pltpu.make_async_copy(a, b, sems.at[i]) for i, (a, b) in enumerate(pairs)]
     for copy in copies:
         copy.start()
-    for copy in copies:
-        copy.wait()
-
-
-def fetch(*arrays):
-    return call(
-        fetch_kernel,
-        [pltpu.VMEM(a.shape, a.dtype) for a in arrays],
-        [FAR] * len(arrays),
-        [pltpu.SemaphoreType.DMA((len(arrays),))],
-    )(*[in_hbm(a) for a in arrays])
-
-
-def expert_kernel(near, far, gains, wg, wu, wd_far, units, theirs, wd, sem):
-    load = pltpu.make_async_copy(wd_far, wd, sem)
-    load.start()
-    peers, halves, rows, quarter = near.shape
     core = lax.axis_index("rep") % 2
-    total = peers * rows
-    squares = jnp.zeros((total, 1), F32)
-    for block in (near, far):
-        for z in range(halves):
-            v = block[:, z].reshape(total, quarter).astype(F32)
-            squares = squares + jnp.sum(v * v, axis=1, keepdims=True)
+    copies[0].wait()
+    copies[1].wait()
+    a, b, c = raw_products(near, core, gains, wg, wu)
+    squares[...] = jnp.broadcast_to(a, squares.shape)
+    gate[...] = b
+    up[...] = c
+    copies[2].wait()
+
+
+def expert_kernel(far, gains, wg, wu, wd, near_squares, near_gate, near_up, units, theirs):
+    peers, halves, rows, quarter = far.shape
+    core = lax.axis_index("rep") % 2
+    squares, gate, up = raw_products(far, 1 - core, gains, wg, wu)
+    squares = squares + near_squares[:, :1]
     scaling = lax.rsqrt(squares / (2 * halves * quarter) + EPSILON)
-    gate = jnp.zeros((total, wg.shape[1]), F32)
-    up = jnp.zeros((total, wg.shape[1]), F32)
-    for block, side in ((near, core), (far, 1 - core)):
-        for z in range(halves):
-            where = columns_of(z, side, quarter)
-            v = block[:, z].reshape(total, quarter).astype(F32)
-            v = (v * scaling * gains[1:2, where]).astype(BF16)
-            gate = gate + dot_rows(v, wg[0, :, where])
-            up = up + dot_rows(v, wu[0, :, where])
+    gate = (gate + near_gate[...]) * scaling
+    up = (up + near_up[...]) * scaling
     a = (gate / (1.0 + jnp.exp(-gate)) * up).astype(BF16)
     units[...] = a
-    load.wait()
     for z in range(halves):
         part = dot(a, wd[0, :, columns_of(z, 1 - core, quarter)])
         theirs[:, z] = part.astype(BF16).reshape(peers, rows, quarter)
@@ -426,6 +434,9 @@
     gates = route_gates.astype(F32).transpose(0, 2, 1, 3).reshape(rows, 2, 2)
     experts_row = jnp.arange(EXPERTS, dtype=jnp.int32)
     shares = jnp.sum(jnp.where(ids[..., None] == experts_row, gates[..., None], 0.0), axis=2)
+    shares = shares.transpose(1, 2, 0)[..., None]
+    shares = [shares[0], shares[1]]
+    kept = lax.dynamic_slice_in_dim(inputs, rep * quarter, quarter, 1).astype(F32)
 
     routes = route_ids.transpose(1, 2, 3, 0)
     message = call(
@@ -442,23 +453,34 @@
     )(in_hbm(new_slot), in_hbm(routes), in_hbm(tokens), in_hbm(norm_gains))
     near = spread_req(message)
     length = page_table.shape[1] * kv_pages.shape[1]
-    cache = call(
+    tail = (mine, length - SPAN) + kv_pages.shape[2:]
+    start, cache = call(
         page_kernel,
-        pltpu.HBM((mine, length) + kv_pages.shape[2:], BF16),
+        [pltpu.VMEM((mine, SPAN) + kv_pages.shape[2:], BF16), pltpu.HBM(tail, BF16)],
         [FAR] * 3,
         [
             pltpu.SMEM(page_table.shape, jnp.int32),
             pltpu.SMEM(cache_len.shape, jnp.int32),
-            pltpu.VMEM((mine, length) + kv_pages.shape[2:], BF16),
+            pltpu.VMEM(tail, BF16),
             pltpu.SemaphoreType.DMA((mine, length // SPAN)),
             pltpu.SemaphoreType.DMA((mine, length // SPAN)),
             pltpu.SemaphoreType.DMA((2,)),
         ],
-        outs=FAR,
+        outs=[VM, FAR],
     )(in_hbm(page_table), in_hbm(cache_len), in_hbm(kv_pages))
-    near, cache = lax.optimization_barrier((near, cache))
+    near, start, cache, shares, kept = lax.optimization_barrier(
+        (near, start, cache, shares, kept)
+    )
     far = other_core(near)
-    ordered = call(query_kernel, shape_of((req_count, rows, HD)), [VM] * 3)(near, far, w_query)
+    wq, begun = call(
+        near_query_kernel,
+        [pltpu.VMEM(w_query.shape, BF16), shape_of((total, HD), F32)],
+        [VM, FAR],
+        [pltpu.SemaphoreType.DMA],
+    )(near, in_hbm(w_query))
+    ordered, notes = call(
+        query_kernel, [shape_of((req_count, rows, HD)), shape_of((total, HD))], [VM] * 4
+    )(near, far, in_vmem(wq), begun)
     arrived = spread_req(ordered)
     sel, fresh = call(
         own_kernel, [shape_of((rows, HD), F32), shape_of((2 * rows, wide))], [VM] * 3
@@ -466,54 +488,49 @@
     back = call(
         attention_kernel,
         shape_of((req_count, rows, HD)),
-        [SM, VM, VM, VM, FAR],
+        [SM, VM, VM, VM, VM, FAR],
         [
             pltpu.VMEM(cache.shape, BF16),
             pltpu.VMEM((2 * wide // HD, rows, HD), F32),
             pltpu.VMEM((2 * wide // HD, rows, HD), F32),
-            pltpu.VMEM((mine, length // SPAN, 4 * wide // HD, 2 * SPAN), F32),
+            pltpu.VMEM((mine, length // SPAN - 1, 4 * wide // HD, 2 * SPAN), F32),
             pltpu.VMEM((HD, wide), BF16),
             pltpu.SemaphoreType.DMA((mine, length // SPAN)),
         ],
         16,
-    )(cache_len, sel, arrived, fresh, in_hbm(cache))
+    )(cache_len, sel, arrived, fresh, in_vmem(start), in_hbm(cache))
     returned = spread_req(back)
     answers, theirs = call(
         project_kernel, [shape_of((total, w_out.shape[1])), shape_of(split)], [VM] * 3
-    )(near, returned, w_out)
+    )(notes, returned, w_out)
 
     def reduce_wide(left, theirs, weight, share):
         part = call(part_kernel, shape_of(split, F32), [VM] * 2)(left, weight)
         summed = (part + other_core(theirs).astype(F32)).astype(BF16)
         got = spread_wide(summed.reshape(peers, rows, quarter))
         got = got.reshape(EXPERTS, peers // EXPERTS, rows, quarter).astype(F32)
-        return jnp.sum(jnp.sum(got, axis=1) * share.T[:, :, None], axis=0)
-
-    kept = lax.dynamic_slice_in_dim(inputs, rep * quarter, quarter, 1).astype(F32)
-    hidden = kept + reduce_wide(answers, theirs, w_out, shares[:, 0])
+        return jnp.sum(jnp.sum(got, axis=1) * share, axis=0)
+
+    hidden = kept + reduce_wide(answers, theirs, w_out, shares[0])
     copies = jnp.broadcast_to(hidden.astype(BF16)[None], (peers, rows, quarter))
-    copies, *weights = lax.optimization_barrier(
-        (copies, w_gate.transpose(0, 2, 1), w_up.transpose(0, 2, 1))
+    block = spread_wide(copies)
+    far = other_core(block).reshape(split)
+    block, *weights = lax.optimization_barrier(
+        (block, w_gate.transpose(0, 2, 1), w_up.transpose(0, 2, 1), w_down)
     )
-    block = spread_wide(copies)
-    block, *weights = lax.optimization_barrier((block, *fetch(*weights)))
-    units, theirs, down = call(
-        expert_kernel,
-        [
-            shape_of((total, w_down.shape[1])),
-            shape_of(split),
-            pltpu.VMEM(w_down.shape, BF16),
-        ],
-        [VM] * 5 + [FAR],
-        [pltpu.SemaphoreType.DMA],
-    )(
-        block.reshape(split),
-        other_core(block).reshape(split),
-        norm_gains,
-        *[in_vmem(w) for w in weights],
-        in_hbm(w_down),
-    )
-    feed = reduce_wide(units, theirs, in_vmem(down), shares[:, 1])
+    units_dev = w_down.shape[1]
+    wg, wu, wd, squares, gate, up = call(
+        near_kernel,
+        [pltpu.VMEM(w.shape, BF16) for w in weights]
+        + [shape_of((total, HD), F32)]
+        + [shape_of((total, units_dev), F32)] * 2,
+        [VM, VM, FAR, FAR, FAR],
+        [pltpu.SemaphoreType.DMA((3,))],
+    )(block.reshape(split), norm_gains, *[in_hbm(w) for w in weights])
+    units, theirs = call(
+        expert_kernel, [shape_of((total, units_dev)), shape_of(split)], [VM] * 8
+    )(far, norm_gains, in_vmem(wg), in_vmem(wu), in_vmem(wd), squares, gate, up)
+    feed = reduce_wide(units, theirs, in_vmem(wd), shares[1])
     piece = (hidden + feed).astype(BF16)
     pieces = [piece] + [
         lax.ppermute(piece, "rep", [(p, p ^ m) for p in range(rep_count)])

time: 135 us -> 131 us (0.970)
  blocking collectives: 14 us -> 62.4 us
  waiting for transfers between devices: 54.1 us -> 19.3 us
  starting transfers between devices: 41.7 us -> 27.1 us
  other arithmetic: 2.34 us -> 0.75 us
    all_to_all x0 -> x3, blocking collectives: none -> 48.4 us  [spread_wide(): lax.all_to_all(value, ('req', 'rep'), split_axis=0, concat_axis=0, tiled=...]
    all_to_all x3 -> x0, waiting for transfers between devices: 32.3 us -> none  [spread_wide(): lax.all_to_all(value, ('req', 'rep'), split_axis=0, concat_axis=0, tiled=...]
    all_to_all x3 -> x0, starting transfers between devices: 14.1 us -> none  [spread_wide(): lax.all_to_all(value, ('req', 'rep'), split_axis=0, concat_axis=0, tiled=...]
    ppermute x4, waiting for transfers between devices: 5.46 us -> 2.98 us  [other_core(): return lax.ppermute(value, 'rep', swap)]
    convert_element_type x2, other arithmetic: 1.94 us -> 0.35 us  [reduce_wide(): summed = (part + other_core(theirs).astype(F32)).astype(BF16)]
    pallas_call x4 -> x5, Pallas kernels: 9.02 us -> 9.27 us  [the longest x1 3.14 us: shards(): call(page_kernel, [pltpu.VMEM((mine, SPAN) + kv_pages.shape[2:], BF16), p...]
  transfers between devices with their start and end apart: 12 -> 9, of which waited for: 11 -> 7; matrix products, arithmetic and copies ran while one was open for 0% -> 1% of each run, Pallas kernels for 5% -> 7%
where the time goes in v1:
time: 131 us; the launch traced here: 130 us
  blocking collectives  62.4 us (48%)
  starting transfers between devices  27.1 us (21%)
  waiting for transfers between devices  19.3 us (15%)
  Pallas kernels  17.9 us (14%)
  local copies, waits for them, and re-layouts  2.8 us (2%)
    all_to_all x3, blocking collectives, spread_wide(): lax.all_to_all(value, ('req', 'rep'), split_axis=0, concat_axis=0, tiled=...  48.4 us
    all_to_all x2, starting transfers between devices, spread_req(): return lax.all_to_all(value, 'req', split_axis=0, concat_axis=0, tiled=True)  15 us
    all_to_all x2, waiting for transfers between devices, spread_req(): return lax.all_to_all(value, 'req', split_axis=0, concat_axis=0, tiled=True)  14.6 us
    all_to_all x1, blocking collectives, spread_req(): return lax.all_to_all(value, 'req', split_axis=0, concat_axis=0, tiled=True)  14 us
    ppermute x4, starting transfers between devices, other_core(): return lax.ppermute(value, 'rep', swap)  8.26 us
    pallas_call x1, Pallas kernels, shards(): call(attention_kernel, shape_of((req_count, rows, HD)), [SM, VM, VM, VM,...  3.89 us
    ppermute x3, starting transfers between devices, shards(): lax.ppermute(piece, 'rep', [(p, p ^ m) for p in range(rep_count)])  3.79 us
    pallas_call x1, Pallas kernels, shards(): call(page_kernel, [pltpu.VMEM((mine, SPAN) + kv_pages.shape[2:], BF16), p...  3.14 us
  transfers between devices with their start and end apart: 9, of which 7 were waited for; matrix products, arithmetic and copies ran while one was open for 1% of the time, Pallas kernels for 7%

profile of v1, /device:TPU:1, one launch (start us, length us, event | category | flops | bytes accessed | tf_op | source)
XLA Modules:
  0.0 130.4 jit_solution(10153765942498150371)
XLA Ops:
  0.0 0.0 copy-start.4
  0.0 0.0 copy-start.5
  0.0 0.0 copy-start.6
  0.0 1.9 %shard_map.136 = bf16[32,8,1152]{2,1,0:T(8,128)(2,1)} custom-call(s32[4]{0:T(128)} %slots_far.1, s32[2,2,2,4]{3,2,1,0:T(2,128)} %bitcast.32, bf16[4,2,2048]{2,1,0:T(2,128)(2,1)} %tokens_far.1, f32[2,2048]{1,0:T(2,128)} %gains.3), custom_call_target="tpu_custom_call" | custom-call | tf_op jit(solution)/shard_map/pallas_call | solution.py:442
  1.9 11.2 %all-to-all-start = ((bf16[32,8,1152]{2,1,0:T(8,128)(2,1)}), bf16[32,8,1152]{2,1,0:T(8,128)(2,1)S(1)}, u32[]{:S(2)}, u32[]{:S(2)}) async-start(bf16[32,8,1152]{2,1,0:T(8,128)(2,1)} %shard_map.136), calls=%async_computation | async-start | bytes 1179648 | tf_op jit(solution)/shard_map/all_to_all | solution.py:417
  13.1 0.0 copy-done.4
  13.1 0.0 copy-done.6
  13.2 0.1 copy.24
  13.3 0.1 reshape.33
  13.4 0.0 copy-done.5
  13.4 0.1 copy.23
  13.5 0.1 eq.15
  13.6 0.1 select_reduce_fusion
  13.6 0.1 copy.25
  13.7 0.1 copy.26
  13.8 3.1 %shard_map.137 = (bf16[4,256,2,512]{3,2,1,0:T(2,128)(2,1)S(1)}, bf16[4,768,2,512]{3,2,1,0:T(2,128)(2,1)}) custom-call(s32[4,64]{1,0:T(4,128)} %table_far.1, s32[4]{0:T(128)} %lens.1, bf16[256,16,2,512]{3,2,1,0:T(2,128)(2,1)} %pool.1), custom_call_target="tpu_custom_call" | custom-call | tf_op jit(solution)/shard_map/pallas_call | solution.py:457
  17.0 9.1 %all-to-all-done.near = bf16[32,8,1152]{2,1,0:T(8,128)(2,1)S(1)} async-done(((bf16[32,8,1152]{2,1,0:T(8,128)(2,1)}), bf16[32,8,1152]{2,1,0:T(8,128)(2,1)S(1)}, u32[]{:S(2)}, u32[]{:S(2)}) %all-to-all-start) | async-done | bytes 589856 | tf_op jit(solution)/shard_map/all_to_all | solution.py:417
  26.1 2.2 %collective-permute-start = (bf16[32,8,1152]{2,1,0:T(8,128)(2,1)S(1)}, bf16[32,8,1152]{2,1,0:T(8,128)(2,1)S(1)}, u32[]{:S(2)}, u32[]{:S(2)}) collective-permute-start(bf16[32,8,1152]{2,1,0:T(8,128)(2,1)S(1)} %all-to-all-done.near), channel_id=1, source_target_pairs={{0,1},{1,0},{2,3},{3,2},{4,5},{5,4},{6,7},{7,6},{8,9},{9,8},{10,11... | collective-permute-start | bytes 1769480 | tf_op jit(solution)/shard_map/ppermute | solution.py:430
  28.3 1.3 %shard_map.138 = (bf16[1,2048,128]{2,1,0:T(8,128)(2,1)S(1)}, f32[256,128]{1,0:T(8,128)S(1)}) custom-call(bf16[32,8,1152]{2,1,0:T(8,128)(2,1)S(1)} %all-to-all-done.near, bf16[1,2048,128]{2,1,0:T(8,128)(2,1)} %wq_far.1), custom_call_target="tpu_custom_call" | custom-call | tf_op jit(solution)/shard_map/pallas_call | solution.py:475
  29.6 0.3 collective-permute-done.far
  29.9 1.1 shard_map.139
  31.1 3.8 %all-to-all-start.1 = ((bf16[32,8,128]{2,1,0:T(8,128)(2,1)}), bf16[32,8,128]{2,1,0:T(8,128)(2,1)S(1)}, u32[]{:S(2)}, u32[]{:S(2)}) async-start(bf16[32,8,128]{2,1,0:T(8,128)(2,1)} %get-tuple-element.41), calls=%async_computation.1 | async-start | bytes 131072 | tf_op jit(solution)/shard_map/all_to_all | solution.py:417
  34.9 0.0 copy-start
  34.9 2.2 %copy-done = bf16[2048,2,512]{2,1,0:T(2,128)(2,1)S(1)} copy-done((bf16[2048,2,512]{2,1,0:T(2,128)(2,1)S(1)}, bf16[2048,2,512]{2,1,0:T(2,128)(2,1)}, u32[]{:S(2)}) %copy-start) | copy-done | bytes 4194328
  37.1 0.0 copy-start.3
  37.1 1.0 shard_map.140
  38.1 5.4 %all-to-all-done.1.arrived = bf16[32,8,128]{2,1,0:T(8,128)(2,1)S(1)} async-done(((bf16[32,8,128]{2,1,0:T(8,128)(2,1)}), bf16[32,8,128]{2,1,0:T(8,128)(2,1)S(1)}, u32[]{:S(2)}, u32[]{:S(2)}) %all-to-all-start.1) | async-done | bytes 65568 | tf_op jit(solution)/shard_map/all_to_all | solution.py:417
  43.5 0.0 copy-done.3
  43.5 0.0 copy-start.1
  43.5 3.9 %shard_map.141 = bf16[32,8,128]{2,1,0:T(8,128)(2,1)S(1)} custom-call(s32[4]{0:T(128)S(1)} %copy-done.3, f32[8,128]{1,0:T(8,128)S(1)} %get-tuple-element.40.sel, bf16[32,8,128]{2,1,0:T(8,128)(2,1)S(1)} %all-to-all-done.1.arrived, bf16[16,512]{1,0:T(8,128)(2,1)S(1)} %get-tuple-element.42.fresh, bf16[4,256,2,512]{3,2,1,0:T(2,128)(2,1)S(1)} %get-tuple-element.43.start, ...), custom_call_target="tpu_custom_call" | custom-call | tf_op jit(solution)/shard_map/pallas_call | solution.py:488
  47.4 14.0 %all_to_all.30.returned = bf16[32,8,128]{2,1,0:T(8,128)(2,1)S(1)} all-to-all(bf16[32,8,128]{2,1,0:T(8,128)(2,1)S(1)} %shard_map.141), channel_id=1, replica_groups=mesh['req'=32,'rep'=4] {'req'}, dimensions={0} | all-to-all | bytes 131072 | tf_op jit(solution)/shard_map/all_to_all | solution.py:417
  61.4 0.0 copy-done.1
  61.4 0.5 shard_map.142
  62.0 2.7 %collective-permute-start.1 = (bf16[32,2,8,512]{3,2,1,0:T(8,128)(2,1)S(1)}, bf16[32,2,8,512]{3,2,1,0:T(8,128)(2,1)S(1)}, u32[]{:S(2)}, u32[]{:S(2)}) collective-permute-start(bf16[32,2,8,512]{3,2,1,0:T(8,128)(2,1)S(1)} %get-tuple-element.46), channel_id=1, source_target_pairs={{0,1},{1,0},{2,3},{3,2},{4,5},{5,4},{6,7},{7,6},{8,9},{9,8},{10,11... | collective-permute-start | bytes 1572872 | tf_op jit(solution)/shard_map/ppermute | solution.py:430
  64.7 0.3 shard_map.143
  65.0 1.3 collective-permute-done.1
  66.2 0.2 add_convert_fusion.1
  66.4 16.4 %all_to_all.31 = bf16[64,8,512]{2,1,0:T(8,128)(2,1)S(1)} all-to-all(bf16[64,8,512]{2,1,0:T(8,128)(2,1)S(1)} %bitcast.27), channel_id=1, replica_groups={{0,2,4,6,8,10,12,14,16,18,20,22,24,26,28,30,32,34,36,38,40,42,44,46,48,..., dimensions={0} | all-to-all | bytes 1048576 | tf_op jit(solution)/shard_map/all_to_all | solution.py:420
  82.8 0.0 copy-start.2
  82.8 0.1 convert_reduce_fusion.1
  82.9 0.1 multiply_reduce_fusion.1
  83.0 15.5 %all_to_all.32 = bf16[64,8,512]{2,1,0:T(8,128)(2,1)S(1)} all-to-all(bf16[64,8,512]{2,1,0:T(8,128)(2,1)S(1)} %broadcast_in_dim.29), channel_id=1, replica_groups={{0,2,4,6,8,10,12,14,16,18,20,22,24,26,28,30,32,34,36,38,40,42,44,46,48,..., dimensions={0} | all-to-all | bytes 1048576 | tf_op jit(solution)/shard_map/all_to_all | solution.py:420
  98.5 3.2 %collective-permute-start.2 = (bf16[64,8,512]{2,1,0:T(8,128)(2,1)S(1)}, bf16[64,8,512]{2,1,0:T(8,128)(2,1)S(1)}, u32[]{:S(2)}, u32[]{:S(2)}) collective-permute-start(bf16[64,8,512]{2,1,0:T(8,128)(2,1)S(1)} %all_to_all.32), channel_id=1, source_target_pairs={{0,1},{1,0},{2,3},{3,2},{4,5},{5,4},{6,7},{7,6},{8,9},{9,8},{10,11... | collective-permute-start | bytes 1572872 | tf_op jit(solution)/shard_map/ppermute | solution.py:430
  101.8 0.0 copy-done.2
  101.8 2.5 %shard_map.144 = (bf16[1,352,2048]{2,1,0:T(8,128)(2,1)S(1)}, bf16[1,352,2048]{2,1,0:T(8,128)(2,1)S(1)}, bf16[1,352,2048]{2,1,0:T(8,128)(2,1)S(1)}, f32[256,128]{...) custom-call(bf16[32,2,8,512]{3,2,1,0:T(8,128)(2,1)S(1)} %bitcast.25, f32[2,2048]{1,0:T(2,128)S(1)} %copy-done.2, ...), custom_call_target="tpu_custom_call" | custom-call | tf_op jit(solution)/shard_map/pallas_call | solution.py:522
  104.3 0.0 collective-permute-done.2
  104.3 1.1 shard_map.145
  105.4 0.1 collective-permute-start.3
  105.5 0.4 shard_map.146
  106.0 1.4 %collective-permute-done.3 = bf16[32,2,8,512]{3,2,1,0:T(8,128)(2,1)S(1)} collective-permute-done((bf16[32,2,8,512]{3,2,1,0:T(8,128)(2,1)S(1)}, bf16[32,2,8,512]{3,2,1,0:T(8,128)(2,1)S(1)}, u32[]{:S(2)}, u32[]{:S(2)}) %collective-permute-start.3) | collective-permute-done | bytes 524320 | tf_op jit(solution)/shard_map/ppermute | solution.py:430
  107.4 0.2 add_convert_fusion
  107.6 16.5 %all_to_all.33 = bf16[64,8,512]{2,1,0:T(8,128)(2,1)S(1)} all-to-all(bf16[64,8,512]{2,1,0:T(8,128)(2,1)S(1)} %bitcast.28), channel_id=1, replica_groups={{0,2,4,6,8,10,12,14,16,18,20,22,24,26,28,30,32,34,36,38,40,42,44,46,48,..., dimensions={0} | all-to-all | bytes 1048576 | tf_op jit(solution)/shard_map/all_to_all | solution.py:420
  124.1 0.1 convert_reduce_fusion
  124.2 0.1 multiply_reduce_fusion
  124.3 2.1 %collective-permute-start.4 = (bf16[8,512]{1,0:T(8,128)(2,1)S(1)}, bf16[8,512]{1,0:T(8,128)(2,1)S(1)}, u32[]{:S(2)}, u32[]{:S(2)}) collective-permute-start(bf16[8,512]{1,0:T(8,128)(2,1)S(1)} %add_convert_fusion.2.refs_0_), channel_id=1, source_target_pairs={{0,1},{1,0},{2,3},{3,2},{4,5},{5,4},{6,7},{7,6},{8,9},{9,8},{10,11... | collective-permute-start | bytes 24584 | tf_op jit(solution)/shard_map/ppermute | solution.py:536
  126.3 0.4 collective-permute-start.5
  126.7 1.3 %collective-permute-start.6 = (bf16[8,512]{1,0:T(8,128)(2,1)S(1)}, bf16[8,512]{1,0:T(8,128)(2,1)S(1)}, u32[]{:S(2)}, u32[]{:S(2)}) collective-permute-start(bf16[8,512]{1,0:T(8,128)(2,1)S(1)} %add_convert_fusion.2.refs_0_), channel_id=1, source_target_pairs={{0,3},{1,2},{2,1},{3,0},{4,7},{5,6},{6,5},{7,4},{8,11},{9,10},{10,... | collective-permute-start | bytes 24584 | tf_op jit(solution)/shard_map/ppermute | solution.py:536
  128.1 0.0 collective-permute-done.4.refs_1_
  128.1 0.8 collective-permute-done.5.refs_2_
  128.9 1.0 collective-permute-done.6.refs_3_
  129.8 0.6 shard_map.147
  (7 shorter events, 0.1 us)
Async XLA Ops:
  0.0 13.1 %copy-start.4 = (bf16[4,2,2048]{2,1,0:T(2,128)(2,1)S(1)}, bf16[4,2,2048]{2,1,0:T(2,128)(2,1)}, u32[]{:S(2)}) copy-start(bf16[4,2,2048]{2,1,0:T(2,128)(2,1)} %tokens_far.1) | copy-start | bytes 98308
  0.0 13.4 %copy-start.5 = (s32[4,2,2,2]{0,3,2,1:T(2,128)S(1)}, s32[4,2,2,2]{0,3,2,1:T(2,128)}, u32[]{:S(2)}) copy-start(s32[4,2,2,2]{0,3,2,1:T(2,128)} %param.25) | copy-start | bytes 388
  0.0 13.1 %copy-start.6 = (bf16[4,2,2,2]{0,3,2,1:T(2,128)(2,1)S(1)}, bf16[4,2,2,2]{0,3,2,1:T(2,128)(2,1)}, u32[]{:S(2)}) copy-start(bf16[4,2,2,2]{0,3,2,1:T(2,128)(2,1)} %param.26) | copy-start | bytes 196
  1.9 24.2 %all-to-all-start = ((bf16[32,8,1152]{2,1,0:T(8,128)(2,1)}), bf16[32,8,1152]{2,1,0:T(8,128)(2,1)S(1)}, u32[]{:S(2)}, u32[]{:S(2)}) async-start(bf16[32,8,1152]{2,1,0:T(8,128)(2,1)} %shard_map.136), calls=%async_computation | async-start | bytes 1179648 | tf_op jit(solution)/shard_map/all_to_all | solution.py:417
  26.1 3.8 %collective-permute-start = (bf16[32,8,1152]{2,1,0:T(8,128)(2,1)S(1)}, bf16[32,8,1152]{2,1,0:T(8,128)(2,1)S(1)}, u32[]{:S(2)}, u32[]{:S(2)}) collective-permute-start(bf16[32,8,1152]{2,1,0:T(8,128)(2,1)S(1)} %all-to-all-done.near), channel_id=1, source_target_pairs={{0,1},{1,0},{2,3},{3,2},{4,5},{5,4},{6,7},{7,6},{8,9},{9,8},{10,11... | collective-permute-start | bytes 1769480 | tf_op jit(solution)/shard_map/ppermute | solution.py:430
  31.1 12.5 %all-to-all-start.1 = ((bf16[32,8,128]{2,1,0:T(8,128)(2,1)}), bf16[32,8,128]{2,1,0:T(8,128)(2,1)S(1)}, u32[]{:S(2)}, u32[]{:S(2)}) async-start(bf16[32,8,128]{2,1,0:T(8,128)(2,1)} %get-tuple-element.41), calls=%async_computation.1 | async-start | bytes 131072 | tf_op jit(solution)/shard_map/all_to_all | solution.py:417
  34.9 2.2 %copy-start = (bf16[2048,2,512]{2,1,0:T(2,128)(2,1)S(1)}, bf16[2048,2,512]{2,1,0:T(2,128)(2,1)}, u32[]{:S(2)}) copy-start(bf16[2048,2,512]{2,1,0:T(2,128)(2,1)} %wkv.1) | copy-start | bytes 12582916
  37.1 6.4 %copy-start.3 = (s32[4]{0:T(128)S(1)}, s32[4]{0:T(128)}, u32[]{:S(2)}) copy-start(s32[4]{0:T(128)} %lens.1) | copy-start | bytes 52
  43.5 17.9 %copy-start.1 = (bf16[1,128,2048]{2,1,0:T(8,128)(2,1)S(1)}, bf16[1,128,2048]{2,1,0:T(8,128)(2,1)}, u32[]{:S(2)}) copy-start(bf16[1,128,2048]{2,1,0:T(8,128)(2,1)} %weight.1) | copy-start | bytes 1572868
  62.0 4.3 %collective-permute-start.1 = (bf16[32,2,8,512]{3,2,1,0:T(8,128)(2,1)S(1)}, bf16[32,2,8,512]{3,2,1,0:T(8,128)(2,1)S(1)}, u32[]{:S(2)}, u32[]{:S(2)}) collective-permute-start(bf16[32,2,8,512]{3,2,1,0:T(8,128)(2,1)S(1)} %get-tuple-element.46), channel_id=1, source_target_pairs={{0,1},{1,0},{2,3},{3,2},{4,5},{5,4},{6,7},{7,6},{8,9},{9,8},{10,11... | collective-permute-start | bytes 1572872 | tf_op jit(solution)/shard_map/ppermute | solution.py:430
  82.8 18.9 %copy-start.2 = (f32[2,2048]{1,0:T(2,128)S(1)}, f32[2,2048]{1,0:T(2,128)}, u32[]{:S(2)}) copy-start(f32[2,2048]{1,0:T(2,128)} %gains.3) | copy-start | bytes 49156
  98.5 5.8 %collective-permute-start.2 = (bf16[64,8,512]{2,1,0:T(8,128)(2,1)S(1)}, bf16[64,8,512]{2,1,0:T(8,128)(2,1)S(1)}, u32[]{:S(2)}, u32[]{:S(2)}) collective-permute-start(bf16[64,8,512]{2,1,0:T(8,128)(2,1)S(1)} %all_to_all.32), channel_id=1, source_target_pairs={{0,1},{1,0},{2,3},{3,2},{4,5},{5,4},{6,7},{7,6},{8,9},{9,8},{10,11... | collective-permute-start | bytes 1572872 | tf_op jit(solution)/shard_map/ppermute | solution.py:430
  105.4 2.0 %collective-permute-start.3 = (bf16[32,2,8,512]{3,2,1,0:T(8,128)(2,1)S(1)}, bf16[32,2,8,512]{3,2,1,0:T(8,128)(2,1)S(1)}, u32[]{:S(2)}, u32[]{:S(2)}) collective-permute-start(bf16[32,2,8,512]{3,2,1,0:T(8,128)(2,1)S(1)} %get-tuple-element.59), channel_id=1, source_target_pairs={{0,1},{1,0},{2,3},{3,2},{4,5},{5,4},{6,7},{7,6},{8,9},{9,8},{10,11... | collective-permute-start | bytes 1572872 | tf_op jit(solution)/shard_map/ppermute | solution.py:430
  124.3 3.8 %collective-permute-start.4 = (bf16[8,512]{1,0:T(8,128)(2,1)S(1)}, bf16[8,512]{1,0:T(8,128)(2,1)S(1)}, u32[]{:S(2)}, u32[]{:S(2)}) collective-permute-start(bf16[8,512]{1,0:T(8,128)(2,1)S(1)} %add_convert_fusion.2.refs_0_), channel_id=1, source_target_pairs={{0,1},{1,0},{2,3},{3,2},{4,5},{5,4},{6,7},{7,6},{8,9},{9,8},{10,11... | collective-permute-start | bytes 24584 | tf_op jit(solution)/shard_map/ppermute | solution.py:536
  126.3 2.5 %collective-permute-start.5 = (bf16[8,512]{1,0:T(8,128)(2,1)S(1)}, bf16[8,512]{1,0:T(8,128)(2,1)S(1)}, u32[]{:S(2)}, u32[]{:S(2)}) collective-permute-start(bf16[8,512]{1,0:T(8,128)(2,1)S(1)} %add_convert_fusion.2.refs_0_), channel_id=1, source_target_pairs={{0,2},{1,3},{2,0},{3,1},{4,6},{5,7},{6,4},{7,5},{8,10},{9,11},{10,... | collective-permute-start | bytes 24584 | tf_op jit(solution)/shard_map/ppermute | solution.py:536
  126.7 3.1 %collective-permute-start.6 = (bf16[8,512]{1,0:T(8,128)(2,1)S(1)}, bf16[8,512]{1,0:T(8,128)(2,1)S(1)}, u32[]{:S(2)}, u32[]{:S(2)}) collective-permute-start(bf16[8,512]{1,0:T(8,128)(2,1)S(1)} %add_convert_fusion.2.refs_0_), channel_id=1, source_target_pairs={{0,3},{1,2},{2,1},{3,0},{4,7},{5,6},{6,5},{7,4},{8,11},{9,10},{10,... | collective-permute-start | bytes 24584 | tf_op jit(solution)/shard_map/ppermute | solution.py:536

commit v2 on v1

--- a/solution.py
+++ b/solution.py
@@ -152,9 +152,12 @@
     chunks = 1 + out.shape[1] // SPAN
 
     def each(act):
-        for j in range(count):
-            for c in range(chunks):
-                pl.when(c * SPAN < lens[j])(functools.partial(act, j, c))
+        for c in range(chunks):
+            for j in range(count):
+                if c < 2:
+                    act(j, c)
+                else:
+                    pl.when(lens[j] > 2 * SPAN)(functools.partial(act, j, c))
 
     def block_of(j, c):
         return start.at[j] if c == 0 else staged.at[j, pl.ds((c - 1) * SPAN, SPAN)]
@@ -187,18 +190,42 @@
     each(finish)
 
 
+def pages_call(table, lens, pool):
+    mine, pages = table.shape
+    length = pages * pool.shape[1]
+    tail = (mine, length - SPAN) + pool.shape[2:]
+    return call(
+        page_kernel,
+        [pltpu.VMEM((mine, SPAN) + pool.shape[2:], BF16), pltpu.HBM(tail, BF16)],
+        [FAR] * 3,
+        [
+            pltpu.SMEM(table.shape, jnp.int32),
+            pltpu.SMEM(lens.shape, jnp.int32),
+            pltpu.VMEM(tail, BF16),
+            pltpu.SemaphoreType.DMA((mine, length // SPAN)),
+            pltpu.SemaphoreType.DMA((mine, length // SPAN)),
+            pltpu.SemaphoreType.DMA((2,)),
+        ],
+        outs=[VM, FAR],
+    )(in_hbm(table), in_hbm(lens), in_hbm(pool))
+
+
 def attention_kernel(lens, sel, arrived, fresh, start, far, out, cache, qs, os, sc, ef, sems):
-    def copy_of(j, c):
-        span = pl.ds((c - 1) * SPAN, SPAN)
-        return pltpu.make_async_copy(far.at[j, span], cache.at[j, span], sems.at[j, c])
-
-    count, _, _, wide = cache.shape
-    for c in range(1, 1 + cache.shape[1] // SPAN):
-        for j in range(count):
-
-            @pl.when(c * SPAN < lens[j])
-            def _(j=j, c=c):
-                copy_of(j, c).start()
+    count, tail, _, wide = cache.shape
+    requests = range(count)
+    spans = (pl.ds(0, SPAN), pl.ds(SPAN, tail - SPAN))
+
+    def copy_of(j, part):
+        span = spans[part]
+        return pltpu.make_async_copy(far.at[j, span], cache.at[j, span], sems.at[j, part])
+
+    for j in requests:
+        copy_of(j, 0).start()
+    for j in requests:
+
+        @pl.when(lens[j] > 2 * SPAN)
+        def _(j=j):
+            copy_of(j, 1).start()
 
     peers, rows, _ = arrived.shape
     heads = wide // HD
@@ -219,22 +246,22 @@
     big = (2 * group, wide)
     block_row = lax.broadcasted_iota(jnp.int32, big, 0) % heads
     diagonal = block_row == lax.broadcasted_iota(jnp.int32, big, 1) // HD
-    scores_shape = (2 * group, 2 * SPAN)
-    column = lax.broadcasted_iota(jnp.int32, scores_shape, 1)
-    keys = column % 2 == 0
     e_col = lax.broadcasted_iota(jnp.int32, (2 * group, HD), 1)
     e_row = lax.broadcasted_iota(jnp.int32, (2 * group, HD), 0)
-    requests = range(count)
-
-    def first(j):
-        return start[j].reshape(2 * SPAN, wide)
-
-    def block(j, c):
-        return cache[j, pl.ds((c - 1) * SPAN, SPAN)].reshape(2 * SPAN, wide)
-
-    def masked_scores(q, rows_of, j, c):
-        s = dot_rows(q, rows_of) * inv_scale
-        return jnp.where(keys & (column < 2 * (lens[j] - c * SPAN)), s, MASKED)
+
+    def rows_of(j, part):
+        if part == 0:
+            return start[j].reshape(2 * SPAN, wide)
+        if part == 1:
+            return cache[j, :SPAN].reshape(2 * SPAN, wide)
+        return cache[j, SPAN:].reshape(2 * (tail - SPAN), wide)
+
+    def masked_scores(q, j, part):
+        s = dot_rows(q, rows_of(j, part)) * inv_scale
+        column = lax.broadcasted_iota(jnp.int32, s.shape, 1)
+        return jnp.where(
+            (column % 2 == 0) & (column < 2 * (lens[j] - part * SPAN)), s, MASKED
+        )
 
     def highest(s):
         return jnp.max(s, axis=1, keepdims=True)
@@ -245,43 +272,49 @@
     def onto_values(p, distance=1):
         return pltpu.roll(p, distance, 1).astype(BF16)
 
-    chunks = [(lens[j] + SPAN - 1) // SPAN for j in requests]
-    queries, extras, firsts, tops = [], [], [], []
+    longer = [jnp.where(lens[j] > 2 * SPAN, 1, 0) for j in requests]
+    queries, extras, firsts, seconds, tops = [], [], [], [], []
     for j in requests:
         q = jnp.concatenate([qs[:, 2 * j, :], qs[:, 2 * j + 1, :]], axis=0)
         q = jnp.where(diagonal, jnp.concatenate([q] * heads, axis=1), 0.0).astype(BF16)
         live = (e_col == 2 * j) | ((e_col == 2 * j + 1) & (e_row >= group))
-        e = jnp.where(live, dot_rows(q, extra) * inv_scale, MASKED)
-        s = masked_scores(q, first(j), j, 0)
         queries.append(q)
-        extras.append(e)
-        firsts.append(s)
-        tops.append(jnp.maximum(highest(e), highest(s)))
-
-    for j in requests:
-
-        def score(c, top, j=j):
-            copy_of(j, c).wait()
-            s = masked_scores(queries[j], block(j, c), j, c)
-            sc[j, c - 1] = s
+        extras.append(jnp.where(live, dot_rows(q, extra) * inv_scale, MASKED))
+        firsts.append(masked_scores(q, j, 0))
+    for j in requests:
+        copy_of(j, 0).wait()
+    for j in requests:
+        seconds.append(masked_scores(queries[j], j, 1))
+        top = jnp.maximum(highest(extras[j]), highest(firsts[j]))
+        tops.append(jnp.maximum(top, highest(seconds[j])))
+
+    for j in requests:
+
+        def score(_, top, j=j):
+            copy_of(j, 1).wait()
+            s = masked_scores(queries[j], j, 2)
+            sc[j] = s
             return jnp.maximum(top, highest(s))
 
-        tops[j] = lax.fori_loop(1, chunks[j], score, tops[j])
+        tops[j] = lax.fori_loop(0, longer[j], score, tops[j])
 
     extras = [jnp.exp(extras[j] - tops[j]) for j in requests]
     firsts = [jnp.exp(firsts[j] - tops[j]) for j in requests]
-    sums = [added(extras[j]) + added(firsts[j]) for j in requests]
+    seconds = [jnp.exp(seconds[j] - tops[j]) for j in requests]
+    sums = [added(extras[j]) + added(firsts[j]) + added(seconds[j]) for j in requests]
     mixed = [
-        dot(onto_values(extras[j], rows), extra) + dot(onto_values(firsts[j]), first(j))
+        dot(onto_values(extras[j], rows), extra)
+        + dot(onto_values(firsts[j]), rows_of(j, 0))
+        + dot(onto_values(seconds[j]), rows_of(j, 1))
         for j in requests
     ]
     for j in requests:
 
-        def gather(c, state, j=j):
-            p = jnp.exp(sc[j, c - 1] - tops[j])
-            return state[0] + added(p), state[1] + dot(onto_values(p), block(j, c))
-
-        sums[j], mixed[j] = lax.fori_loop(1, chunks[j], gather, (sums[j], mixed[j]))
+        def gather(_, state, j=j):
+            p = jnp.exp(sc[j] - tops[j])
+            return state[0] + added(p), state[1] + dot(onto_values(p), rows_of(j, 2))
+
+        sums[j], mixed[j] = lax.fori_loop(0, longer[j], gather, (sums[j], mixed[j]))
 
     for j in requests:
         kept = jnp.where(diagonal, mixed[j], 0.0)
@@ -296,6 +329,26 @@
         for e in range(EXPERTS):
             value = jnp.where(masks[0][e], one, 0.0) + jnp.where(masks[1][e], two, 0.0)
             out[e * heads + h] = value.astype(BF16)
+
+
+def attention_call(lens, sel, arrived, fresh, start, cache):
+    rows, wide = arrived.shape[1], cache.shape[-1]
+    mine, tail = cache.shape[:2]
+    pairs = 2 * wide // HD
+    return call(
+        attention_kernel,
+        shape_of(arrived.shape),
+        [SM, VM, VM, VM, VM, FAR],
+        [
+            pltpu.VMEM(cache.shape, BF16),
+            pltpu.VMEM((pairs, rows, HD), F32),
+            pltpu.VMEM((pairs, rows, HD), F32),
+            pltpu.VMEM((mine, 2 * pairs, 2 * (tail - SPAN)), F32),
+            pltpu.VMEM((HD, wide), BF16),
+            pltpu.SemaphoreType.DMA((mine, 2)),
+        ],
+        16,
+    )(lens, sel, arrived, fresh, in_vmem(start), in_hbm(cache))
 
 
 def columns_of(z, core, quarter):
@@ -350,19 +403,12 @@
     return squares, gate, up
 
 
-def near_kernel(near, gains, wg_far, wu_far, wd_far, wg, wu, wd, squares, gate, up, sems):
-    pairs = ((wg_far, wg), (wu_far, wu), (wd_far, wd))
-    copies = [pltpu.make_async_copy(a, b, sems.at[i]) for i, (a, b) in enumerate(pairs)]
-    for copy in copies:
-        copy.start()
+def near_kernel(near, gains, wg, wu, squares, gate, up):
     core = lax.axis_index("rep") % 2
-    copies[0].wait()
-    copies[1].wait()
     a, b, c = raw_products(near, core, gains, wg, wu)
     squares[...] = jnp.broadcast_to(a, squares.shape)
     gate[...] = b
     up[...] = c
-    copies[2].wait()
 
 
 def expert_kernel(far, gains, wg, wu, wd, near_squares, near_gate, near_up, units, theirs):
@@ -452,22 +498,7 @@
         ],
     )(in_hbm(new_slot), in_hbm(routes), in_hbm(tokens), in_hbm(norm_gains))
     near = spread_req(message)
-    length = page_table.shape[1] * kv_pages.shape[1]
-    tail = (mine, length - SPAN) + kv_pages.shape[2:]
-    start, cache = call(
-        page_kernel,
-        [pltpu.VMEM((mine, SPAN) + kv_pages.shape[2:], BF16), pltpu.HBM(tail, BF16)],
-        [FAR] * 3,
-        [
-            pltpu.SMEM(page_table.shape, jnp.int32),
-            pltpu.SMEM(cache_len.shape, jnp.int32),
-            pltpu.VMEM(tail, BF16),
-            pltpu.SemaphoreType.DMA((mine, length // SPAN)),
-            pltpu.SemaphoreType.DMA((mine, length // SPAN)),
-            pltpu.SemaphoreType.DMA((2,)),
-        ],
-        outs=[VM, FAR],
-    )(in_hbm(page_table), in_hbm(cache_len), in_hbm(kv_pages))
+    start, cache = pages_call(page_table, cache_len, kv_pages)
     near, start, cache, shares, kept = lax.optimization_barrier(
         (near, start, cache, shares, kept)
     )
@@ -485,20 +516,7 @@
     sel, fresh = call(
         own_kernel, [shape_of((rows, HD), F32), shape_of((2 * rows, wide))], [VM] * 3
     )(near, far, w_kv)
-    back = call(
-        attention_kernel,
-        shape_of((req_count, rows, HD)),
-        [SM, VM, VM, VM, VM, FAR],
-        [
-            pltpu.VMEM(cache.shape, BF16),
-            pltpu.VMEM((2 * wide // HD, rows, HD), F32),
-            pltpu.VMEM((2 * wide // HD, rows, HD), F32),
-            pltpu.VMEM((mine, length // SPAN - 1, 4 * wide // HD, 2 * SPAN), F32),
-            pltpu.VMEM((HD, wide), BF16),
-            pltpu.SemaphoreType.DMA((mine, length // SPAN)),
-        ],
-        16,
-    )(cache_len, sel, arrived, fresh, in_vmem(start), in_hbm(cache))
+    back = attention_call(cache_len, sel, arrived, fresh, start, cache)
     returned = spread_req(back)
     answers, theirs = call(
         project_kernel, [shape_of((total, w_out.shape[1])), shape_of(split)], [VM] * 3
@@ -515,22 +533,17 @@
     copies = jnp.broadcast_to(hidden.astype(BF16)[None], (peers, rows, quarter))
     block = spread_wide(copies)
     far = other_core(block).reshape(split)
-    block, *weights = lax.optimization_barrier(
-        (block, w_gate.transpose(0, 2, 1), w_up.transpose(0, 2, 1), w_down)
-    )
+    wg, wu = w_gate.transpose(0, 2, 1), w_up.transpose(0, 2, 1)
     units_dev = w_down.shape[1]
-    wg, wu, wd, squares, gate, up = call(
+    squares, gate, up = call(
         near_kernel,
-        [pltpu.VMEM(w.shape, BF16) for w in weights]
-        + [shape_of((total, HD), F32)]
-        + [shape_of((total, units_dev), F32)] * 2,
-        [VM, VM, FAR, FAR, FAR],
-        [pltpu.SemaphoreType.DMA((3,))],
-    )(block.reshape(split), norm_gains, *[in_hbm(w) for w in weights])
+        [shape_of((total, HD), F32)] + [shape_of((total, units_dev), F32)] * 2,
+        [VM] * 4,
+    )(block.reshape(split), norm_gains, wg, wu)
     units, theirs = call(
         expert_kernel, [shape_of((total, units_dev)), shape_of(split)], [VM] * 8
-    )(far, norm_gains, in_vmem(wg), in_vmem(wu), in_vmem(wd), squares, gate, up)
-    feed = reduce_wide(units, theirs, in_vmem(wd), shares[1])
+    )(far, norm_gains, wg, wu, w_down, squares, gate, up)
+    feed = reduce_wide(units, theirs, w_down, shares[1])
     piece = (hidden + feed).astype(BF16)
     pieces = [piece] + [
         lax.ppermute(piece, "rep", [(p, p ^ m) for p in range(rep_count)])

time: 131 us -> 130 us (level)
  waiting for transfers between devices: 19.3 us -> 16.8 us
  local copies, waits for them, and re-layouts: 2.8 us -> 4.25 us
    all_to_all x2, waiting for transfers between devices: 14.6 us -> 11.6 us  [spread_req(): return lax.all_to_all(value, 'req', split_axis=0, concat_axis=0, tiled=True)]
  transfers between devices with their start and end apart: 9 -> 9, of which waited for: 7 -> 8; matrix products, arithmetic and copies ran while one was open for 1% -> 2% of each run, Pallas kernels for 7% -> 6%
where the time goes in v2:
time: 130 us; the launch traced here: 129 us
  blocking collectives  61.7 us (47%)
  starting transfers between devices  27.6 us (21%)
  waiting for transfers between devices  16.8 us (13%)
  Pallas kernels  16.7 us (13%)
  local copies, waits for them, and re-layouts  4.25 us (3%)
  other arithmetic  1.43 us (1%)
    all_to_all x3, blocking collectives, spread_wide(): lax.all_to_all(value, ('req', 'rep'), split_axis=0, concat_axis=0, tiled=...  48.7 us
    all_to_all x2, starting transfers between devices, spread_req(): return lax.all_to_all(value, 'req', split_axis=0, concat_axis=0, tiled=True)  15 us
    all_to_all x1, blocking collectives, spread_req(): return lax.all_to_all(value, 'req', split_axis=0, concat_axis=0, tiled=True)  13 us
    all_to_all x2, waiting for transfers between devices, spread_req(): return lax.all_to_all(value, 'req', split_axis=0, concat_axis=0, tiled=True)  11.6 us
    ppermute x4, starting transfers between devices, other_core(): return lax.ppermute(value, 'rep', swap)  8.66 us
    pallas_call x1, Pallas kernels, pages_call(): call(page_kernel, [pltpu.VMEM((mine, SPAN) + pool.shape[2:], BF16), pltpu...  4 us
    ppermute x3, starting transfers between devices, shards(): lax.ppermute(piece, 'rep', [(p, p ^ m) for p in range(rep_count)])  3.88 us
    pallas_call x1, Pallas kernels, attention_call(): call(attention_kernel, shape_of(arrived.shape), [SM, VM, VM, VM, VM, FAR]...  3.8 us
  transfers between devices with their start and end apart: 9, of which 8 were waited for; matrix products, arithmetic and copies ran while one was open for 2% of the time, Pallas kernels for 6%

profile of v2, /device:TPU:1, one launch (start us, length us, event | category | flops | bytes accessed | tf_op | source)
XLA Modules:
  0.0 128.7 jit_solution(6705852196000481202)
XLA Ops:
  0.0 1.8 %shard_map.136 = bf16[32,8,1152]{2,1,0:T(8,128)(2,1)} custom-call(s32[4]{0:T(128)} %slots_far.1, s32[2,2,2,4]{3,2,1,0:T(2,128)} %bitcast.34, bf16[4,2,2048]{2,1,0:T(2,128)(2,1)} %tokens_far.1, f32[2,2048]{1,0:T(2,128)} %gains.3), custom_call_target="tpu_custom_call" | custom-call | tf_op jit(solution)/shard_map/pallas_call | solution.py:488
  1.8 11.2 %all-to-all-start = ((bf16[32,8,1152]{2,1,0:T(8,128)(2,1)}), bf16[32,8,1152]{2,1,0:T(8,128)(2,1)S(1)}, u32[]{:S(2)}, u32[]{:S(2)}) async-start(bf16[32,8,1152]{2,1,0:T(8,128)(2,1)} %shard_map.136), calls=%async_computation | async-start | bytes 1179648 | tf_op jit(solution)/shard_map/all_to_all | solution.py:463
  13.0 0.8 reshape.28
  13.8 0.7 convert_bitcast_fusion
  14.5 0.1 copy.24
  14.6 0.1 reshape.33
  14.7 0.8 copy.23
  15.5 0.1 eq.15
  15.5 0.1 select_reduce_fusion
  15.6 0.1 copy.25
  15.7 0.1 copy.26
  15.8 4.0 %shard_map.137 = (bf16[4,256,2,512]{3,2,1,0:T(2,128)(2,1)S(1)}, bf16[4,768,2,512]{3,2,1,0:T(2,128)(2,1)}) custom-call(s32[4,64]{1,0:T(4,128)} %table_far.1, s32[4]{0:T(128)} %lens.1, bf16[256,16,2,512]{3,2,1,0:T(2,128)(2,1)} %pool.1), custom_call_target="tpu_custom_call" | custom-call | tf_op jit(solution)/shard_map/pallas_call | solution.py:197
  19.8 6.2 %all-to-all-done.near = bf16[32,8,1152]{2,1,0:T(8,128)(2,1)S(1)} async-done(((bf16[32,8,1152]{2,1,0:T(8,128)(2,1)}), bf16[32,8,1152]{2,1,0:T(8,128)(2,1)S(1)}, u32[]{:S(2)}, u32[]{:S(2)}) %all-to-all-start) | async-done | bytes 589856 | tf_op jit(solution)/shard_map/all_to_all | solution.py:463
  26.0 2.2 %collective-permute-start = (bf16[32,8,1152]{2,1,0:T(8,128)(2,1)S(1)}, bf16[32,8,1152]{2,1,0:T(8,128)(2,1)S(1)}, u32[]{:S(2)}, u32[]{:S(2)}) collective-permute-start(bf16[32,8,1152]{2,1,0:T(8,128)(2,1)S(1)} %all-to-all-done.near), channel_id=1, source_target_pairs={{0,1},{1,0},{2,3},{3,2},{4,5},{5,4},{6,7},{7,6},{8,9},{9,8},{10,11... | collective-permute-start | bytes 1769480 | tf_op jit(solution)/shard_map/ppermute | solution.py:476
  28.2 1.3 %shard_map.138 = (bf16[1,2048,128]{2,1,0:T(8,128)(2,1)S(1)}, f32[256,128]{1,0:T(8,128)S(1)}) custom-call(bf16[32,8,1152]{2,1,0:T(8,128)(2,1)S(1)} %all-to-all-done.near, bf16[1,2048,128]{2,1,0:T(8,128)(2,1)} %wq_far.1), custom_call_target="tpu_custom_call" | custom-call | tf_op jit(solution)/shard_map/pallas_call | solution.py:506
  29.5 0.3 collective-permute-done.far
  29.8 1.1 shard_map.139
  30.9 3.8 %all-to-all-start.1 = ((bf16[32,8,128]{2,1,0:T(8,128)(2,1)}), bf16[32,8,128]{2,1,0:T(8,128)(2,1)S(1)}, u32[]{:S(2)}, u32[]{:S(2)}) async-start(bf16[32,8,128]{2,1,0:T(8,128)(2,1)} %get-tuple-element.34), calls=%async_computation.1 | async-start | bytes 131072 | tf_op jit(solution)/shard_map/all_to_all | solution.py:463
  34.8 0.0 copy-start.3
  34.8 2.2 %copy-done.3 = bf16[2048,2,512]{2,1,0:T(2,128)(2,1)S(1)} copy-done((bf16[2048,2,512]{2,1,0:T(2,128)(2,1)S(1)}, bf16[2048,2,512]{2,1,0:T(2,128)(2,1)}, u32[]{:S(2)}) %copy-start.3) | copy-done | bytes 4194328
  37.0 0.0 copy-start.6
  37.0 1.0 shard_map.140
  38.0 5.4 %all-to-all-done.1.arrived = bf16[32,8,128]{2,1,0:T(8,128)(2,1)S(1)} async-done(((bf16[32,8,128]{2,1,0:T(8,128)(2,1)}), bf16[32,8,128]{2,1,0:T(8,128)(2,1)S(1)}, u32[]{:S(2)}, u32[]{:S(2)}) %all-to-all-start.1) | async-done | bytes 65568 | tf_op jit(solution)/shard_map/all_to_all | solution.py:463
  43.4 0.0 copy-done.6
  43.4 0.0 copy-start.4
  43.4 3.8 %shard_map.141 = bf16[32,8,128]{2,1,0:T(8,128)(2,1)S(1)} custom-call(s32[4]{0:T(128)S(1)} %copy-done.6, f32[8,128]{1,0:T(8,128)S(1)} %get-tuple-element.33.sel, bf16[32,8,128]{2,1,0:T(8,128)(2,1)S(1)} %all-to-all-done.1.arrived, bf16[16,512]{1,0:T(8,128)(2,1)S(1)} %get-tuple-element.35.fresh, bf16[4,256,2,512]{3,2,1,0:T(2,128)(2,1)S(1)} %get-tuple-element.36.start, ...), custom_call_target="tpu_custom_call" | custom-call | tf_op jit(solution)/shard_map/pallas_call | solution.py:338
  47.2 13.0 %all_to_all.30.returned = bf16[32,8,128]{2,1,0:T(8,128)(2,1)S(1)} all-to-all(bf16[32,8,128]{2,1,0:T(8,128)(2,1)S(1)} %shard_map.141), channel_id=1, replica_groups=mesh['req'=32,'rep'=4] {'req'}, dimensions={0} | all-to-all | bytes 131072 | tf_op jit(solution)/shard_map/all_to_all | solution.py:463
  60.3 0.0 copy-done.4
  60.3 0.5 shard_map.142
  60.8 2.7 %collective-permute-start.1 = (bf16[32,2,8,512]{3,2,1,0:T(8,128)(2,1)S(1)}, bf16[32,2,8,512]{3,2,1,0:T(8,128)(2,1)S(1)}, u32[]{:S(2)}, u32[]{:S(2)}) collective-permute-start(bf16[32,2,8,512]{3,2,1,0:T(8,128)(2,1)S(1)} %get-tuple-element.39), channel_id=1, source_target_pairs={{0,1},{1,0},{2,3},{3,2},{4,5},{5,4},{6,7},{7,6},{8,9},{9,8},{10,11... | collective-permute-start | bytes 1572872 | tf_op jit(solution)/shard_map/ppermute | solution.py:476
  63.6 0.3 shard_map.143
  63.8 1.3 collective-permute-done.1
  65.1 0.2 add_convert_fusion.1
  65.3 0.0 copy-start
  65.3 0.0 copy-start.1
  65.3 0.0 copy-start.5
  65.3 16.6 %all_to_all.31 = bf16[64,8,512]{2,1,0:T(8,128)(2,1)S(1)} all-to-all(bf16[64,8,512]{2,1,0:T(8,128)(2,1)S(1)} %bitcast.31), channel_id=1, replica_groups={{0,2,4,6,8,10,12,14,16,18,20,22,24,26,28,30,32,34,36,38,40,42,44,46,48,..., dimensions={0} | all-to-all | bytes 1048576 | tf_op jit(solution)/shard_map/all_to_all | solution.py:466
  82.0 0.1 convert_reduce_fusion.1
  82.0 0.1 multiply_reduce_fusion.1
  82.2 0.0 copy-start.2
  82.2 15.6 %all_to_all.32 = bf16[64,8,512]{2,1,0:T(8,128)(2,1)S(1)} all-to-all(bf16[64,8,512]{2,1,0:T(8,128)(2,1)S(1)} %broadcast_in_dim.29), channel_id=1, replica_groups={{0,2,4,6,8,10,12,14,16,18,20,22,24,26,28,30,32,34,36,38,40,42,44,46,48,..., dimensions={0} | all-to-all | bytes 1048576 | tf_op jit(solution)/shard_map/all_to_all | solution.py:466
  97.8 3.2 %collective-permute-start.2 = (bf16[64,8,512]{2,1,0:T(8,128)(2,1)S(1)}, bf16[64,8,512]{2,1,0:T(8,128)(2,1)S(1)}, u32[]{:S(2)}, u32[]{:S(2)}) collective-permute-start(bf16[64,8,512]{2,1,0:T(8,128)(2,1)S(1)} %all_to_all.32), channel_id=1, source_target_pairs={{0,1},{1,0},{2,3},{3,2},{4,5},{5,4},{6,7},{7,6},{8,9},{9,8},{10,11... | collective-permute-start | bytes 1572872 | tf_op jit(solution)/shard_map/ppermute | solution.py:476
  101.0 0.0 copy-done
  101.0 0.0 copy-done.1
  101.0 0.0 copy-done.5
  101.0 0.7 shard_map.144
  101.8 0.8 collective-permute-done.2
  102.6 0.0 copy-done.2
  102.6 1.1 shard_map.145
  103.7 0.5 collective-permute-start.3
  104.2 0.4 shard_map.146
  104.6 1.1 collective-permute-done.3
  105.7 0.2 add_convert_fusion
  105.9 16.4 %all_to_all.33 = bf16[64,8,512]{2,1,0:T(8,128)(2,1)S(1)} all-to-all(bf16[64,8,512]{2,1,0:T(8,128)(2,1)S(1)} %bitcast.32), channel_id=1, replica_groups={{0,2,4,6,8,10,12,14,16,18,20,22,24,26,28,30,32,34,36,38,40,42,44,46,48,..., dimensions={0} | all-to-all | bytes 1048576 | tf_op jit(solution)/shard_map/all_to_all | solution.py:466
  122.3 0.1 convert_reduce_fusion
  122.4 0.1 multiply_reduce_fusion
  122.5 2.2 %collective-permute-start.4 = (bf16[8,512]{1,0:T(8,128)(2,1)S(1)}, bf16[8,512]{1,0:T(8,128)(2,1)S(1)}, u32[]{:S(2)}, u32[]{:S(2)}) collective-permute-start(bf16[8,512]{1,0:T(8,128)(2,1)S(1)} %add_convert_fusion.2.refs_0_), channel_id=1, source_target_pairs={{0,1},{1,0},{2,3},{3,2},{4,5},{5,4},{6,7},{7,6},{8,9},{9,8},{10,11... | collective-permute-start | bytes 24584 | tf_op jit(solution)/shard_map/ppermute | solution.py:549
  124.6 0.4 collective-permute-start.5
  125.0 1.3 %collective-permute-start.6 = (bf16[8,512]{1,0:T(8,128)(2,1)S(1)}, bf16[8,512]{1,0:T(8,128)(2,1)S(1)}, u32[]{:S(2)}, u32[]{:S(2)}) collective-permute-start(bf16[8,512]{1,0:T(8,128)(2,1)S(1)} %add_convert_fusion.2.refs_0_), channel_id=1, source_target_pairs={{0,3},{1,2},{2,1},{3,0},{4,7},{5,6},{6,5},{7,4},{8,11},{9,10},{10,... | collective-permute-start | bytes 24584 | tf_op jit(solution)/shard_map/ppermute | solution.py:549
  126.3 0.0 collective-permute-done.4.refs_1_
  126.3 0.8 collective-permute-done.5.refs_2_
  127.1 1.0 collective-permute-done.6.refs_3_
  128.1 0.6 shard_map.147
  (5 shorter events, 0.1 us)
Async XLA Ops:
  1.8 24.2 %all-to-all-start = ((bf16[32,8,1152]{2,1,0:T(8,128)(2,1)}), bf16[32,8,1152]{2,1,0:T(8,128)(2,1)S(1)}, u32[]{:S(2)}, u32[]{:S(2)}) async-start(bf16[32,8,1152]{2,1,0:T(8,128)(2,1)} %shard_map.136), calls=%async_computation | async-start | bytes 1179648 | tf_op jit(solution)/shard_map/all_to_all | solution.py:463
  26.0 3.8 %collective-permute-start = (bf16[32,8,1152]{2,1,0:T(8,128)(2,1)S(1)}, bf16[32,8,1152]{2,1,0:T(8,128)(2,1)S(1)}, u32[]{:S(2)}, u32[]{:S(2)}) collective-permute-start(bf16[32,8,1152]{2,1,0:T(8,128)(2,1)S(1)} %all-to-all-done.near), channel_id=1, source_target_pairs={{0,1},{1,0},{2,3},{3,2},{4,5},{5,4},{6,7},{7,6},{8,9},{9,8},{10,11... | collective-permute-start | bytes 1769480 | tf_op jit(solution)/shard_map/ppermute | solution.py:476
  30.9 12.5 %all-to-all-start.1 = ((bf16[32,8,128]{2,1,0:T(8,128)(2,1)}), bf16[32,8,128]{2,1,0:T(8,128)(2,1)S(1)}, u32[]{:S(2)}, u32[]{:S(2)}) async-start(bf16[32,8,128]{2,1,0:T(8,128)(2,1)} %get-tuple-element.34), calls=%async_computation.1 | async-start | bytes 131072 | tf_op jit(solution)/shard_map/all_to_all | solution.py:463
  34.8 2.2 %copy-start.3 = (bf16[2048,2,512]{2,1,0:T(2,128)(2,1)S(1)}, bf16[2048,2,512]{2,1,0:T(2,128)(2,1)}, u32[]{:S(2)}) copy-start(bf16[2048,2,512]{2,1,0:T(2,128)(2,1)} %wkv.1) | copy-start | bytes 12582916
  37.0 6.4 %copy-start.6 = (s32[4]{0:T(128)S(1)}, s32[4]{0:T(128)}, u32[]{:S(2)}) copy-start(s32[4]{0:T(128)} %lens.1) | copy-start | bytes 52
  43.4 16.9 %copy-start.4 = (bf16[1,128,2048]{2,1,0:T(8,128)(2,1)S(1)}, bf16[1,128,2048]{2,1,0:T(8,128)(2,1)}, u32[]{:S(2)}) copy-start(bf16[1,128,2048]{2,1,0:T(8,128)(2,1)} %weight.2) | copy-start | bytes 1572868
  60.8 4.3 %collective-permute-start.1 = (bf16[32,2,8,512]{3,2,1,0:T(8,128)(2,1)S(1)}, bf16[32,2,8,512]{3,2,1,0:T(8,128)(2,1)S(1)}, u32[]{:S(2)}, u32[]{:S(2)}) collective-permute-start(bf16[32,2,8,512]{3,2,1,0:T(8,128)(2,1)S(1)} %get-tuple-element.39), channel_id=1, source_target_pairs={{0,1},{1,0},{2,3},{3,2},{4,5},{5,4},{6,7},{7,6},{8,9},{9,8},{10,11... | collective-permute-start | bytes 1572872 | tf_op jit(solution)/shard_map/ppermute | solution.py:476
  65.3 35.8 %copy-start = (bf16[1,2048,352]{1,2,0:T(8,128)(2,1)S(1)}, bf16[1,2048,352]{1,2,0:T(8,128)(2,1)}, u32[]{:S(2)}) copy-start(bf16[1,2048,352]{1,2,0:T(8,128)(2,1)} %param.19) | copy-start | bytes 4325380
  65.3 35.8 %copy-start.1 = (bf16[1,2048,352]{1,2,0:T(8,128)(2,1)S(1)}, bf16[1,2048,352]{1,2,0:T(8,128)(2,1)}, u32[]{:S(2)}) copy-start(bf16[1,2048,352]{1,2,0:T(8,128)(2,1)} %param.20) | copy-start | bytes 4325380
  65.3 35.7 %copy-start.5 = (f32[2,2048]{1,0:T(2,128)S(1)}, f32[2,2048]{1,0:T(2,128)}, u32[]{:S(2)}) copy-start(f32[2,2048]{1,0:T(2,128)} %gains.3) | copy-start | bytes 49156
  82.2 20.4 %copy-start.2 = (bf16[1,352,2048]{2,1,0:T(8,128)(2,1)S(1)}, bf16[1,352,2048]{2,1,0:T(8,128)(2,1)}, u32[]{:S(2)}) copy-start(bf16[1,352,2048]{2,1,0:T(8,128)(2,1)} %weight.3) | copy-start | bytes 4325380
  97.8 4.8 %collective-permute-start.2 = (bf16[64,8,512]{2,1,0:T(8,128)(2,1)S(1)}, bf16[64,8,512]{2,1,0:T(8,128)(2,1)S(1)}, u32[]{:S(2)}, u32[]{:S(2)}) collective-permute-start(bf16[64,8,512]{2,1,0:T(8,128)(2,1)S(1)} %all_to_all.32), channel_id=1, source_target_pairs={{0,1},{1,0},{2,3},{3,2},{4,5},{5,4},{6,7},{7,6},{8,9},{9,8},{10,11... | collective-permute-start | bytes 1572872 | tf_op jit(solution)/shard_map/ppermute | solution.py:476
  103.7 2.0 %collective-permute-start.3 = (bf16[32,2,8,512]{3,2,1,0:T(8,128)(2,1)S(1)}, bf16[32,2,8,512]{3,2,1,0:T(8,128)(2,1)S(1)}, u32[]{:S(2)}, u32[]{:S(2)}) collective-permute-start(bf16[32,2,8,512]{3,2,1,0:T(8,128)(2,1)S(1)} %get-tuple-element.45), channel_id=1, source_target_pairs={{0,1},{1,0},{2,3},{3,2},{4,5},{5,4},{6,7},{7,6},{8,9},{9,8},{10,11... | collective-permute-start | bytes 1572872 | tf_op jit(solution)/shard_map/ppermute | solution.py:476
  122.5 3.9 %collective-permute-start.4 = (bf16[8,512]{1,0:T(8,128)(2,1)S(1)}, bf16[8,512]{1,0:T(8,128)(2,1)S(1)}, u32[]{:S(2)}, u32[]{:S(2)}) collective-permute-start(bf16[8,512]{1,0:T(8,128)(2,1)S(1)} %add_convert_fusion.2.refs_0_), channel_id=1, source_target_pairs={{0,1},{1,0},{2,3},{3,2},{4,5},{5,4},{6,7},{7,6},{8,9},{9,8},{10,11... | collective-permute-start | bytes 24584 | tf_op jit(solution)/shard_map/ppermute | solution.py:549
  124.6 2.5 %collective-permute-start.5 = (bf16[8,512]{1,0:T(8,128)(2,1)S(1)}, bf16[8,512]{1,0:T(8,128)(2,1)S(1)}, u32[]{:S(2)}, u32[]{:S(2)}) collective-permute-start(bf16[8,512]{1,0:T(8,128)(2,1)S(1)} %add_convert_fusion.2.refs_0_), channel_id=1, source_target_pairs={{0,2},{1,3},{2,0},{3,1},{4,6},{5,7},{6,4},{7,5},{8,10},{9,11},{10,... | collective-permute-start | bytes 24584 | tf_op jit(solution)/shard_map/ppermute | solution.py:549
  125.0 3.1 %collective-permute-start.6 = (bf16[8,512]{1,0:T(8,128)(2,1)S(1)}, bf16[8,512]{1,0:T(8,128)(2,1)S(1)}, u32[]{:S(2)}, u32[]{:S(2)}) collective-permute-start(bf16[8,512]{1,0:T(8,128)(2,1)S(1)} %add_convert_fusion.2.refs_0_), channel_id=1, source_target_pairs={{0,3},{1,2},{2,1},{3,0},{4,7},{5,6},{6,5},{7,4},{8,11},{9,10},{10,... | collective-permute-start | bytes 24584 | tf_op jit(solution)/shard_map/ppermute | solution.py:549

commit v3 on v2

--- a/solution.py
+++ b/solution.py
@@ -112,7 +112,15 @@
     out[...] = dot(order_of(marks), q.astype(BF16)).astype(BF16).reshape(out.shape)
 
 
-def own_kernel(near, far, wkv, sel, fresh):
+def own_kernel(near, far, wkv, weight, sel, fresh, picked, sems):
+    halves, _, quarter = picked.shape
+    side = 1 - lax.axis_index("rep") % 2
+    copies = [
+        pltpu.make_async_copy(weight.at[0, :, columns_of(z, side, quarter)], picked.at[z], sems.at[z])
+        for z in range(halves)
+    ]
+    for copy in copies:
+        copy.start()
     peers, rows, wide = near.shape
     half = wide - HD
     rank, core = lax.axis_index("req"), lax.axis_index("rep") % 2
@@ -138,6 +146,8 @@
         w = wkv[c * HD : (c + 1) * HD].reshape(2 * HD, fresh.shape[1])
         total = total + dot(v.astype(BF16), w)
     fresh[...] = total.astype(BF16)
+    for copy in copies:
+        copy.wait()
 
 
 def page_kernel(table_far, lens_far, pool, start, out, table, lens, staged, sems, back, small):
@@ -355,26 +365,39 @@
     return pl.ds(pl.multiple_of((2 * z + core) * quarter, quarter), quarter)
 
 
-def project_kernel(notes, returned, wo, answers, theirs):
-    peers, halves, rows, quarter = theirs.shape
-    core = lax.axis_index("rep") % 2
-    values = returned[...].reshape(peers * rows, returned.shape[2])
-    a = lax.dot_general(
+def answers_of(notes, returned):
+    peers, rows, wide = returned.shape
+    values = returned[...].reshape(peers * rows, wide)
+    return lax.dot_general(
         order_of(notes[...]), values, (((0,), (0,)), ((), ())), preferred_element_type=F32
     ).astype(BF16)
-    answers[...] = a
-    for z in range(halves):
-        part = dot(a, wo[0, :, columns_of(z, 1 - core, quarter)])
-        theirs[:, z] = part.astype(BF16).reshape(peers, rows, quarter)
-
-
-def part_kernel(left, weight, out):
+
+
+def own_part(a, weight, out):
     peers, halves, rows, quarter = out.shape
     core = lax.axis_index("rep") % 2
-    a = left[...]
     for z in range(halves):
         part = dot(a, weight[0, :, columns_of(z, core, quarter)])
         out[:, z] = part.reshape(peers, rows, quarter)
+
+
+def other_part(a, weight, part, out):
+    peers, halves, rows, quarter = out.shape
+    for z in range(halves):
+        more = dot(a, weight[z]).reshape(peers, rows, quarter)
+        out[:, z] = (part[:, z] + more).astype(BF16)
+
+
+def project_kernel(notes, returned, weight, out):
+    own_part(answers_of(notes, returned), weight, out)
+
+
+def finish_project_kernel(notes, returned, weight, part, out):
+    other_part(answers_of(notes, returned), weight, part, out)
+
+
+def part_kernel(units, weight, out):
+    own_part(units[...], weight, out)
 
 
 def place_kernel(*refs):
@@ -513,23 +536,32 @@
         query_kernel, [shape_of((req_count, rows, HD)), shape_of((total, HD))], [VM] * 4
     )(near, far, in_vmem(wq), begun)
     arrived = spread_req(ordered)
-    sel, fresh = call(
-        own_kernel, [shape_of((rows, HD), F32), shape_of((2 * rows, wide))], [VM] * 3
-    )(near, far, w_kv)
+    sel, fresh, picked = call(
+        own_kernel,
+        [
+            shape_of((rows, HD), F32),
+            shape_of((2 * rows, wide)),
+            shape_of((rep_count // 2, w_out.shape[1], quarter)),
+        ],
+        [VM, VM, VM, FAR],
+        [pltpu.SemaphoreType.DMA((rep_count // 2,))],
+    )(near, far, w_kv, in_hbm(w_out))
+    arrived, picked = lax.optimization_barrier((arrived, picked))
+    out_x = other_core(picked)
     back = attention_call(cache_len, sel, arrived, fresh, start, cache)
     returned = spread_req(back)
-    answers, theirs = call(
-        project_kernel, [shape_of((total, w_out.shape[1])), shape_of(split)], [VM] * 3
-    )(notes, returned, w_out)
-
-    def reduce_wide(left, theirs, weight, share):
-        part = call(part_kernel, shape_of(split, F32), [VM] * 2)(left, weight)
-        summed = (part + other_core(theirs).astype(F32)).astype(BF16)
+    returned_x = other_core(returned)
+    part = call(project_kernel, shape_of(split, F32), [VM] * 3)(notes, returned, w_out)
+    summed = call(finish_project_kernel, shape_of(split), [VM] * 4)(
+        notes, returned_x, out_x, part
+    )
+
+    def reduce_wide(summed, share):
         got = spread_wide(summed.reshape(peers, rows, quarter))
         got = got.reshape(EXPERTS, peers // EXPERTS, rows, quarter).astype(F32)
         return jnp.sum(jnp.sum(got, axis=1) * share, axis=0)
 
-    hidden = kept + reduce_wide(answers, theirs, w_out, shares[0])
+    hidden = kept + reduce_wide(summed, shares[0])
     copies = jnp.broadcast_to(hidden.astype(BF16)[None], (peers, rows, quarter))
     block = spread_wide(copies)
     far = other_core(block).reshape(split)
@@ -543,7 +575,9 @@
     units, theirs = call(
         expert_kernel, [shape_of((total, units_dev)), shape_of(split)], [VM] * 8
     )(far, norm_gains, wg, wu, w_down, squares, gate, up)
-    feed = reduce_wide(units, theirs, w_down, shares[1])
+    theirs = other_core(theirs)
+    part = call(part_kernel, shape_of(split, F32), [VM] * 2)(units, w_down)
+    feed = reduce_wide((part + theirs.astype(F32)).astype(BF16), shares[1])
     piece = (hidden + feed).astype(BF16)
     pieces = [piece] + [
         lax.ppermute(piece, "rep", [(p, p ^ m) for p in range(rep_count)])

time: 130 us -> 129 us (level)
  waiting for transfers between devices: 16.8 us -> 14.4 us
    all_to_all x2, waiting for transfers between devices: 11.6 us -> 10.1 us  [spread_req(): return lax.all_to_all(value, 'req', split_axis=0, concat_axis=0, tiled=True)]
    ppermute x4 -> x5, waiting for transfers between devices: 3.43 us -> 2.55 us  [other_core(): return lax.ppermute(value, 'rep', swap)]
    unnamed x14 -> x16, local copies, waits for them, and re-layouts: 2.22 us -> 2.91 us
    ppermute x4 -> x5, starting transfers between devices: 8.66 us -> 8.88 us  [other_core(): return lax.ppermute(value, 'rep', swap)]
  transfers between devices with their start and end apart: 9 -> 10, of which waited for: 8 -> 8; matrix products, arithmetic and copies ran while one was open for 2% -> 2% of each run, Pallas kernels for 6% -> 10%
where the time goes in v3:
time: 129 us
  blocking collectives  62.4 us (48%)
  starting transfers between devices  27.8 us (22%)
  Pallas kernels  17.8 us (14%)
  waiting for transfers between devices  14.4 us (11%)
  local copies, waits for them, and re-layouts  4.94 us (4%)
    all_to_all x3, blocking collectives, spread_wide(): lax.all_to_all(value, ('req', 'rep'), split_axis=0, concat_axis=0, tiled=...  48.7 us
    all_to_all x2, starting transfers between devices, spread_req(): return lax.all_to_all(value, 'req', split_axis=0, concat_axis=0, tiled=True)  15 us
    all_to_all x1, blocking collectives, spread_req(): return lax.all_to_all(value, 'req', split_axis=0, concat_axis=0, tiled=True)  13.7 us
    all_to_all x2, waiting for transfers between devices, spread_req(): return lax.all_to_all(value, 'req', split_axis=0, concat_axis=0, tiled=True)  10.1 us
    ppermute x5, starting transfers between devices, other_core(): return lax.ppermute(value, 'rep', swap)  8.88 us
    pallas_call x1, Pallas kernels, pages_call(): call(page_kernel, [pltpu.VMEM((mine, SPAN) + pool.shape[2:], BF16), pltpu...  3.98 us
    ppermute x3, starting transfers between devices, shards(): lax.ppermute(piece, 'rep', [(p, p ^ m) for p in range(rep_count)])  3.88 us
    pallas_call x1, Pallas kernels, attention_call(): call(attention_kernel, shape_of(arrived.shape), [SM, VM, VM, VM, VM, FAR]...  3.8 us
  transfers between devices with their start and end apart: 10, of which 8 were waited for; matrix products, arithmetic and copies ran while one was open for 2% of the time, Pallas kernels for 10%

profile of v3, /device:TPU:1, one launch (start us, length us, event | category | flops | bytes accessed | tf_op | source)
XLA Modules:
  0.0 128.8 jit_solution(4490140481089007959)
XLA Ops:
  0.0 1.8 %shard_map.136 = bf16[32,8,1152]{2,1,0:T(8,128)(2,1)} custom-call(s32[4]{0:T(128)} %slots_far.1, s32[2,2,2,4]{3,2,1,0:T(2,128)} %bitcast.34, bf16[4,2,2048]{2,1,0:T(2,128)(2,1)} %tokens_far.1, f32[2,2048]{1,0:T(2,128)} %gains.3), custom_call_target="tpu_custom_call" | custom-call | tf_op jit(solution)/shard_map/pallas_call | solution.py:511
  1.8 11.2 %all-to-all-start = ((bf16[32,8,1152]{2,1,0:T(8,128)(2,1)}), bf16[32,8,1152]{2,1,0:T(8,128)(2,1)S(1)}, u32[]{:S(2)}, u32[]{:S(2)}) async-start(bf16[32,8,1152]{2,1,0:T(8,128)(2,1)} %shard_map.136), calls=%async_computation | async-start | bytes 1179648 | tf_op jit(solution)/shard_map/all_to_all | solution.py:486
  13.0 0.8 reshape.28
  13.8 0.7 convert_bitcast_fusion
  14.5 0.1 copy.24
  14.6 0.1 reshape.33
  14.7 0.8 copy.23
  15.4 0.1 eq.15
  15.5 0.1 select_reduce_fusion
  15.6 0.1 copy.25
  15.7 0.1 copy.26
  15.8 4.0 %shard_map.137 = (bf16[4,256,2,512]{3,2,1,0:T(2,128)(2,1)S(1)}, bf16[4,768,2,512]{3,2,1,0:T(2,128)(2,1)}) custom-call(s32[4,64]{1,0:T(4,128)} %table_far.1, s32[4]{0:T(128)} %lens.1, bf16[256,16,2,512]{3,2,1,0:T(2,128)(2,1)} %pool.1), custom_call_target="tpu_custom_call" | custom-call | tf_op jit(solution)/shard_map/pallas_call | solution.py:207
  19.8 6.2 %all-to-all-done.near = bf16[32,8,1152]{2,1,0:T(8,128)(2,1)S(1)} async-done(((bf16[32,8,1152]{2,1,0:T(8,128)(2,1)}), bf16[32,8,1152]{2,1,0:T(8,128)(2,1)S(1)}, u32[]{:S(2)}, u32[]{:S(2)}) %all-to-all-start) | async-done | bytes 589856 | tf_op jit(solution)/shard_map/all_to_all | solution.py:486
  26.0 2.2 %collective-permute-start = (bf16[32,8,1152]{2,1,0:T(8,128)(2,1)S(1)}, bf16[32,8,1152]{2,1,0:T(8,128)(2,1)S(1)}, u32[]{:S(2)}, u32[]{:S(2)}) collective-permute-start(bf16[32,8,1152]{2,1,0:T(8,128)(2,1)S(1)} %all-to-all-done.near), channel_id=1, source_target_pairs={{0,1},{1,0},{2,3},{3,2},{4,5},{5,4},{6,7},{7,6},{8,9},{9,8},{10,11... | collective-permute-start | bytes 1769480 | tf_op jit(solution)/shard_map/ppermute | solution.py:499
  28.2 1.3 %shard_map.138 = (bf16[1,2048,128]{2,1,0:T(8,128)(2,1)S(1)}, f32[256,128]{1,0:T(8,128)S(1)}) custom-call(bf16[32,8,1152]{2,1,0:T(8,128)(2,1)S(1)} %all-to-all-done.near, bf16[1,2048,128]{2,1,0:T(8,128)(2,1)} %wq_far.1), custom_call_target="tpu_custom_call" | custom-call | tf_op jit(solution)/shard_map/pallas_call | solution.py:529
  29.5 0.3 collective-permute-done.far
  29.8 1.1 shard_map.139
  30.9 3.8 %all-to-all-start.1 = ((bf16[32,8,128]{2,1,0:T(8,128)(2,1)}), bf16[32,8,128]{2,1,0:T(8,128)(2,1)S(1)}, u32[]{:S(2)}, u32[]{:S(2)}) async-start(bf16[32,8,128]{2,1,0:T(8,128)(2,1)} %get-tuple-element.35), calls=%async_computation.1 | async-start | bytes 131072 | tf_op jit(solution)/shard_map/all_to_all | solution.py:486
  34.7 0.0 copy-start.3
  34.8 2.2 %copy-done.3 = bf16[2048,2,512]{2,1,0:T(2,128)(2,1)S(1)} copy-done((bf16[2048,2,512]{2,1,0:T(2,128)(2,1)S(1)}, bf16[2048,2,512]{2,1,0:T(2,128)(2,1)}, u32[]{:S(2)}) %copy-start.3) | copy-done | bytes 4194328
  36.9 1.9 %shard_map.140 = (f32[8,128]{1,0:T(8,128)S(1)}, bf16[16,512]{1,0:T(8,128)(2,1)S(1)}, bf16[2,128,512]{2,1,0:T(8,128)(2,1)S(1)}) custom-call(bf16[32,8,1152]{2,1,0:T(8,128)(2,1)S(1)} %all-to-all-done.near, bf16[32,8,1152]{2,1,0:T(8,128)(2,1)S(1)} %collective-permute-done.far, bf16[2048,2,512]{2,1,0:T(2,128)(2,1)S(1)} %copy-done.3, bf16[1,128,2048]{2,1,0:T(8,128)(2,1)} %weight.4), custom_call_target="tpu_custom_call" | custom-call | tf_op jit(solution)/shard_map/pallas_call | solution.py:539
  38.8 0.0 copy-start.7
  38.8 0.7 copy-done.7
  39.5 3.9 %all-to-all-done.1.arrived = bf16[32,8,128]{2,1,0:T(8,128)(2,1)S(1)} async-done(((bf16[32,8,128]{2,1,0:T(8,128)(2,1)}), bf16[32,8,128]{2,1,0:T(8,128)(2,1)S(1)}, u32[]{:S(2)}, u32[]{:S(2)}) %all-to-all-start.1) | async-done | bytes 65568 | tf_op jit(solution)/shard_map/all_to_all | solution.py:486
  43.4 1.5 %collective-permute-start.2 = (bf16[2,128,512]{2,1,0:T(8,128)(2,1)}, bf16[2,128,512]{2,1,0:T(8,128)(2,1)S(1)}, u32[]{:S(2)}, u32[]{:S(2)}) collective-permute-start(bf16[2,128,512]{2,1,0:T(8,128)(2,1)} %copy-done.7), channel_id=1, source_target_pairs={{0,1},{1,0},{2,3},{3,2},{4,5},{5,4},{6,7},{7,6},{8,9},{9,8},{10,11... | collective-permute-start | bytes 786440 | tf_op jit(solution)/shard_map/ppermute | solution.py:499
  44.9 0.0 copy-done.6
  44.9 3.8 %shard_map.141 = bf16[32,8,128]{2,1,0:T(8,128)(2,1)S(1)} custom-call(s32[4]{0:T(128)S(1)} %copy-done.6, f32[8,128]{1,0:T(8,128)S(1)} %get-tuple-element.34.sel, bf16[32,8,128]{2,1,0:T(8,128)(2,1)S(1)} %all-to-all-done.1.arrived, bf16[16,512]{1,0:T(8,128)(2,1)S(1)} %get-tuple-element.38.fresh, bf16[4,256,2,512]{3,2,1,0:T(2,128)(2,1)S(1)} %get-tuple-element.39.start, ...), custom_call_target="tpu_custom_call" | custom-call | tf_op jit(solution)/shard_map/pallas_call | solution.py:348
  48.7 13.7 %all_to_all.30.returned = bf16[32,8,128]{2,1,0:T(8,128)(2,1)S(1)} all-to-all(bf16[32,8,128]{2,1,0:T(8,128)(2,1)S(1)} %shard_map.141), channel_id=1, replica_groups=mesh['req'=32,'rep'=4] {'req'}, dimensions={0} | all-to-all | bytes 131072 | tf_op jit(solution)/shard_map/all_to_all | solution.py:486
  62.4 1.4 %collective-permute-start.1 = (bf16[32,8,128]{2,1,0:T(8,128)(2,1)S(1)}, bf16[32,8,128]{2,1,0:T(8,128)(2,1)S(1)}, u32[]{:S(2)}, u32[]{:S(2)}) collective-permute-start(bf16[32,8,128]{2,1,0:T(8,128)(2,1)S(1)} %all_to_all.30.returned), channel_id=1, source_target_pairs={{0,1},{1,0},{2,3},{3,2},{4,5},{5,4},{6,7},{7,6},{8,9},{9,8},{10,11... | collective-permute-start | bytes 196616 | tf_op jit(solution)/shard_map/ppermute | solution.py:499
  63.9 0.0 copy-done.4
  63.9 0.5 shard_map.142.part
  64.4 0.4 collective-permute-done.1.returned
  64.8 0.0 collective-permute-done.2.weight
  64.8 0.5 shard_map.143
  65.3 0.0 copy-start
  65.3 0.0 copy-start.1
  65.3 0.0 copy-start.5
  65.4 16.6 %all_to_all.31 = bf16[64,8,512]{2,1,0:T(8,128)(2,1)S(1)} all-to-all(bf16[64,8,512]{2,1,0:T(8,128)(2,1)S(1)} %bitcast.30), channel_id=1, replica_groups={{0,2,4,6,8,10,12,14,16,18,20,22,24,26,28,30,32,34,36,38,40,42,44,46,48,..., dimensions={0} | all-to-all | bytes 1048576 | tf_op jit(solution)/shard_map/all_to_all | solution.py:489
  82.0 0.1 convert_reduce_fusion.1
  82.1 0.1 multiply_reduce_fusion.1
  82.2 0.0 copy-start.2
  82.2 15.6 %all_to_all.32 = bf16[64,8,512]{2,1,0:T(8,128)(2,1)S(1)} all-to-all(bf16[64,8,512]{2,1,0:T(8,128)(2,1)S(1)} %broadcast_in_dim.29), channel_id=1, replica_groups={{0,2,4,6,8,10,12,14,16,18,20,22,24,26,28,30,32,34,36,38,40,42,44,46,48,..., dimensions={0} | all-to-all | bytes 1048576 | tf_op jit(solution)/shard_map/all_to_all | solution.py:489
  97.9 3.2 %collective-permute-start.3 = (bf16[64,8,512]{2,1,0:T(8,128)(2,1)S(1)}, bf16[64,8,512]{2,1,0:T(8,128)(2,1)S(1)}, u32[]{:S(2)}, u32[]{:S(2)}) collective-permute-start(bf16[64,8,512]{2,1,0:T(8,128)(2,1)S(1)} %all_to_all.32), channel_id=1, source_target_pairs={{0,1},{1,0},{2,3},{3,2},{4,5},{5,4},{6,7},{7,6},{8,9},{9,8},{10,11... | collective-permute-start | bytes 1572872 | tf_op jit(solution)/shard_map/ppermute | solution.py:499
  101.1 0.0 copy-done
  101.1 0.0 copy-done.1
  101.1 0.0 copy-done.5
  101.1 0.7 shard_map.144
  101.8 0.8 collective-permute-done.3
  102.6 0.0 copy-done.2
  102.6 1.1 shard_map.145
  103.7 0.5 collective-permute-start.4
  104.2 0.4 shard_map.146
  104.7 1.1 collective-permute-done.4
  105.8 0.2 add_convert_fusion
  105.9 16.4 %all_to_all.33 = bf16[64,8,512]{2,1,0:T(8,128)(2,1)S(1)} all-to-all(bf16[64,8,512]{2,1,0:T(8,128)(2,1)S(1)} %bitcast.32), channel_id=1, replica_groups={{0,2,4,6,8,10,12,14,16,18,20,22,24,26,28,30,32,34,36,38,40,42,44,46,48,..., dimensions={0} | all-to-all | bytes 1048576 | tf_op jit(solution)/shard_map/all_to_all | solution.py:489
  122.3 0.1 convert_reduce_fusion
  122.4 0.1 multiply_reduce_fusion
  122.5 2.2 %collective-permute-start.5 = (bf16[8,512]{1,0:T(8,128)(2,1)S(1)}, bf16[8,512]{1,0:T(8,128)(2,1)S(1)}, u32[]{:S(2)}, u32[]{:S(2)}) collective-permute-start(bf16[8,512]{1,0:T(8,128)(2,1)S(1)} %add_convert_fusion.1.refs_0_), channel_id=1, source_target_pairs={{0,1},{1,0},{2,3},{3,2},{4,5},{5,4},{6,7},{7,6},{8,9},{9,8},{10,11... | collective-permute-start | bytes 24584 | tf_op jit(solution)/shard_map/ppermute | solution.py:583
  124.7 0.4 collective-permute-start.6
  125.1 1.3 %collective-permute-start.7 = (bf16[8,512]{1,0:T(8,128)(2,1)S(1)}, bf16[8,512]{1,0:T(8,128)(2,1)S(1)}, u32[]{:S(2)}, u32[]{:S(2)}) collective-permute-start(bf16[8,512]{1,0:T(8,128)(2,1)S(1)} %add_convert_fusion.1.refs_0_), channel_id=1, source_target_pairs={{0,3},{1,2},{2,1},{3,0},{4,7},{5,6},{6,5},{7,4},{8,11},{9,10},{10,... | collective-permute-start | bytes 24584 | tf_op jit(solution)/shard_map/ppermute | solution.py:583
  126.4 0.0 collective-permute-done.5.refs_1_
  126.4 0.8 collective-permute-done.6.refs_2_
  127.2 1.0 collective-permute-done.7.refs_3_
  128.1 0.6 shard_map.147
  (7 shorter events, 0.1 us)
Async XLA Ops:
  1.8 24.2 %all-to-all-start = ((bf16[32,8,1152]{2,1,0:T(8,128)(2,1)}), bf16[32,8,1152]{2,1,0:T(8,128)(2,1)S(1)}, u32[]{:S(2)}, u32[]{:S(2)}) async-start(bf16[32,8,1152]{2,1,0:T(8,128)(2,1)} %shard_map.136), calls=%async_computation | async-start | bytes 1179648 | tf_op jit(solution)/shard_map/all_to_all | solution.py:486
  26.0 3.8 %collective-permute-start = (bf16[32,8,1152]{2,1,0:T(8,128)(2,1)S(1)}, bf16[32,8,1152]{2,1,0:T(8,128)(2,1)S(1)}, u32[]{:S(2)}, u32[]{:S(2)}) collective-permute-start(bf16[32,8,1152]{2,1,0:T(8,128)(2,1)S(1)} %all-to-all-done.near), channel_id=1, source_target_pairs={{0,1},{1,0},{2,3},{3,2},{4,5},{5,4},{6,7},{7,6},{8,9},{9,8},{10,11... | collective-permute-start | bytes 1769480 | tf_op jit(solution)/shard_map/ppermute | solution.py:499
  30.9 12.4 %all-to-all-start.1 = ((bf16[32,8,128]{2,1,0:T(8,128)(2,1)}), bf16[32,8,128]{2,1,0:T(8,128)(2,1)S(1)}, u32[]{:S(2)}, u32[]{:S(2)}) async-start(bf16[32,8,128]{2,1,0:T(8,128)(2,1)} %get-tuple-element.35), calls=%async_computation.1 | async-start | bytes 131072 | tf_op jit(solution)/shard_map/all_to_all | solution.py:486
  34.7 2.2 %copy-start.3 = (bf16[2048,2,512]{2,1,0:T(2,128)(2,1)S(1)}, bf16[2048,2,512]{2,1,0:T(2,128)(2,1)}, u32[]{:S(2)}) copy-start(bf16[2048,2,512]{2,1,0:T(2,128)(2,1)} %wkv.1) | copy-start | bytes 12582916
  36.9 8.0 %copy-start.6 = (s32[4]{0:T(128)S(1)}, s32[4]{0:T(128)}, u32[]{:S(2)}) copy-start(s32[4]{0:T(128)} %lens.1) | copy-start | bytes 52
  38.8 0.7 copy-start.7
  43.4 21.4 %collective-permute-start.2 = (bf16[2,128,512]{2,1,0:T(8,128)(2,1)}, bf16[2,128,512]{2,1,0:T(8,128)(2,1)S(1)}, u32[]{:S(2)}, u32[]{:S(2)}) collective-permute-start(bf16[2,128,512]{2,1,0:T(8,128)(2,1)} %copy-done.7), channel_id=1, source_target_pairs={{0,1},{1,0},{2,3},{3,2},{4,5},{5,4},{6,7},{7,6},{8,9},{9,8},{10,11... | collective-permute-start | bytes 786440 | tf_op jit(solution)/shard_map/ppermute | solution.py:499
  44.9 19.0 %copy-start.4 = (bf16[1,128,2048]{2,1,0:T(8,128)(2,1)S(1)}, bf16[1,128,2048]{2,1,0:T(8,128)(2,1)}, u32[]{:S(2)}) copy-start(bf16[1,128,2048]{2,1,0:T(8,128)(2,1)} %weight.4) | copy-start | bytes 1572868
  62.4 2.3 %collective-permute-start.1 = (bf16[32,8,128]{2,1,0:T(8,128)(2,1)S(1)}, bf16[32,8,128]{2,1,0:T(8,128)(2,1)S(1)}, u32[]{:S(2)}, u32[]{:S(2)}) collective-permute-start(bf16[32,8,128]{2,1,0:T(8,128)(2,1)S(1)} %all_to_all.30.returned), channel_id=1, source_target_pairs={{0,1},{1,0},{2,3},{3,2},{4,5},{5,4},{6,7},{7,6},{8,9},{9,8},{10,11... | collective-permute-start | bytes 196616 | tf_op jit(solution)/shard_map/ppermute | solution.py:499
  65.3 35.8 %copy-start = (bf16[1,2048,352]{1,2,0:T(8,128)(2,1)S(1)}, bf16[1,2048,352]{1,2,0:T(8,128)(2,1)}, u32[]{:S(2)}) copy-start(bf16[1,2048,352]{1,2,0:T(8,128)(2,1)} %param.19) | copy-start | bytes 4325380
  65.3 35.8 %copy-start.1 = (bf16[1,2048,352]{1,2,0:T(8,128)(2,1)S(1)}, bf16[1,2048,352]{1,2,0:T(8,128)(2,1)}, u32[]{:S(2)}) copy-start(bf16[1,2048,352]{1,2,0:T(8,128)(2,1)} %param.20) | copy-start | bytes 4325380
  65.3 35.8 %copy-start.5 = (f32[2,2048]{1,0:T(2,128)S(1)}, f32[2,2048]{1,0:T(2,128)}, u32[]{:S(2)}) copy-start(f32[2,2048]{1,0:T(2,128)} %gains.3) | copy-start | bytes 49156
  82.2 20.4 %copy-start.2 = (bf16[1,352,2048]{2,1,0:T(8,128)(2,1)S(1)}, bf16[1,352,2048]{2,1,0:T(8,128)(2,1)}, u32[]{:S(2)}) copy-start(bf16[1,352,2048]{2,1,0:T(8,128)(2,1)} %weight.5) | copy-start | bytes 4325380
  97.9 4.8 %collective-permute-start.3 = (bf16[64,8,512]{2,1,0:T(8,128)(2,1)S(1)}, bf16[64,8,512]{2,1,0:T(8,128)(2,1)S(1)}, u32[]{:S(2)}, u32[]{:S(2)}) collective-permute-start(bf16[64,8,512]{2,1,0:T(8,128)(2,1)S(1)} %all_to_all.32), channel_id=1, source_target_pairs={{0,1},{1,0},{2,3},{3,2},{4,5},{5,4},{6,7},{7,6},{8,9},{9,8},{10,11... | collective-permute-start | bytes 1572872 | tf_op jit(solution)/shard_map/ppermute | solution.py:499
  103.7 2.0 %collective-permute-start.4 = (bf16[32,2,8,512]{3,2,1,0:T(8,128)(2,1)S(1)}, bf16[32,2,8,512]{3,2,1,0:T(8,128)(2,1)S(1)}, u32[]{:S(2)}, u32[]{:S(2)}) collective-permute-start(bf16[32,2,8,512]{3,2,1,0:T(8,128)(2,1)S(1)} %get-tuple-element.47), channel_id=1, source_target_pairs={{0,1},{1,0},{2,3},{3,2},{4,5},{5,4},{6,7},{7,6},{8,9},{9,8},{10,11... | collective-permute-start | bytes 1572872 | tf_op jit(solution)/shard_map/ppermute | solution.py:499
  122.5 3.9 %collective-permute-start.5 = (bf16[8,512]{1,0:T(8,128)(2,1)S(1)}, bf16[8,512]{1,0:T(8,128)(2,1)S(1)}, u32[]{:S(2)}, u32[]{:S(2)}) collective-permute-start(bf16[8,512]{1,0:T(8,128)(2,1)S(1)} %add_convert_fusion.1.refs_0_), channel_id=1, source_target_pairs={{0,1},{1,0},{2,3},{3,2},{4,5},{5,4},{6,7},{7,6},{8,9},{9,8},{10,11... | collective-permute-start | bytes 24584 | tf_op jit(solution)/shard_map/ppermute | solution.py:583
  124.7 2.5 %collective-permute-start.6 = (bf16[8,512]{1,0:T(8,128)(2,1)S(1)}, bf16[8,512]{1,0:T(8,128)(2,1)S(1)}, u32[]{:S(2)}, u32[]{:S(2)}) collective-permute-start(bf16[8,512]{1,0:T(8,128)(2,1)S(1)} %add_convert_fusion.1.refs_0_), channel_id=1, source_target_pairs={{0,2},{1,3},{2,0},{3,1},{4,6},{5,7},{6,4},{7,5},{8,10},{9,11},{10,... | collective-permute-start | bytes 24584 | tf_op jit(solution)/shard_map/ppermute | solution.py:583
  125.1 3.1 %collective-permute-start.7 = (bf16[8,512]{1,0:T(8,128)(2,1)S(1)}, bf16[8,512]{1,0:T(8,128)(2,1)S(1)}, u32[]{:S(2)}, u32[]{:S(2)}) collective-permute-start(bf16[8,512]{1,0:T(8,128)(2,1)S(1)} %add_convert_fusion.1.refs_0_), channel_id=1, source_target_pairs={{0,3},{1,2},{2,1},{3,0},{4,7},{5,6},{6,5},{7,4},{8,11},{9,10},{10,... | collective-permute-start | bytes 24584 | tf_op jit(solution)/shard_map/ppermute | solution.py:583

commit v4 on v3

--- a/solution.py
+++ b/solution.py
@@ -546,11 +546,10 @@
         [VM, VM, VM, FAR],
         [pltpu.SemaphoreType.DMA((rep_count // 2,))],
     )(near, far, w_kv, in_hbm(w_out))
-    arrived, picked = lax.optimization_barrier((arrived, picked))
-    out_x = other_core(picked)
     back = attention_call(cache_len, sel, arrived, fresh, start, cache)
     returned = spread_req(back)
-    returned_x = other_core(returned)
+    returned, picked = lax.optimization_barrier((returned, picked))
+    returned_x, out_x = other_core(returned), other_core(picked)
     part = call(project_kernel, shape_of(split, F32), [VM] * 3)(notes, returned, w_out)
     summed = call(finish_project_kernel, shape_of(split), [VM] * 4)(
         notes, returned_x, out_x, part

time: 129 us -> 131 us (1.016)
  blocking collectives: 62.4 us -> 64.1 us
    all_to_all x1, blocking collectives: 13.7 us -> 15.4 us  [spread_req(): return lax.all_to_all(value, 'req', split_axis=0, concat_axis=0, tiled=True)]
    unnamed x16 -> x18, local copies, waits for them, and re-layouts: 2.91 us -> 2.91 us
  transfers between devices with their start and end apart: 10 -> 10, of which waited for: 8 -> 8; matrix products, arithmetic and copies ran while one was open for 2% -> 2% of each run, Pallas kernels for 10% -> 7%
where the time goes in v4:
time: 131 us; the launch traced here: 130 us
  blocking collectives  64.1 us (49%)
  starting transfers between devices  26.9 us (21%)
  Pallas kernels  17.8 us (14%)
  waiting for transfers between devices  14.7 us (11%)
  local copies, waits for them, and re-layouts  4.95 us (4%)
    all_to_all x3, blocking collectives, spread_wide(): lax.all_to_all(value, ('req', 'rep'), split_axis=0, concat_axis=0, tiled=...  48.7 us
    all_to_all x1, blocking collectives, spread_req(): return lax.all_to_all(value, 'req', split_axis=0, concat_axis=0, tiled=True)  15.4 us
    all_to_all x2, starting transfers between devices, spread_req(): return lax.all_to_all(value, 'req', split_axis=0, concat_axis=0, tiled=True)  15 us
    all_to_all x2, waiting for transfers between devices, spread_req(): return lax.all_to_all(value, 'req', split_axis=0, concat_axis=0, tiled=True)  10 us
    ppermute x5, starting transfers between devices, other_core(): return lax.ppermute(value, 'rep', swap)  8 us
    pallas_call x1, Pallas kernels, pages_call(): call(page_kernel, [pltpu.VMEM((mine, SPAN) + pool.shape[2:], BF16), pltpu...  4 us
    ppermute x3, starting transfers between devices, shards(): lax.ppermute(piece, 'rep', [(p, p ^ m) for p in range(rep_count)])  3.88 us
    pallas_call x1, Pallas kernels, attention_call(): call(attention_kernel, shape_of(arrived.shape), [SM, VM, VM, VM, VM, FAR]...  3.8 us
  transfers between devices with their start and end apart: 10, of which 8 were waited for; matrix products, arithmetic and copies ran while one was open for 2% of the time, Pallas kernels for 7%

profile of v4, /device:TPU:1, one launch (start us, length us, event | category | flops | bytes accessed | tf_op | source)
XLA Modules:
  0.0 129.9 jit_solution(18041135015439851805)
XLA Ops:
  0.0 1.8 %shard_map.136 = bf16[32,8,1152]{2,1,0:T(8,128)(2,1)} custom-call(s32[4]{0:T(128)} %slots_far.1, s32[2,2,2,4]{3,2,1,0:T(2,128)} %bitcast.34, bf16[4,2,2048]{2,1,0:T(2,128)(2,1)} %tokens_far.1, f32[2,2048]{1,0:T(2,128)} %gains.3), custom_call_target="tpu_custom_call" | custom-call | tf_op jit(solution)/shard_map/pallas_call | solution.py:511
  1.8 11.2 %all-to-all-start = ((bf16[32,8,1152]{2,1,0:T(8,128)(2,1)}), bf16[32,8,1152]{2,1,0:T(8,128)(2,1)S(1)}, u32[]{:S(2)}, u32[]{:S(2)}) async-start(bf16[32,8,1152]{2,1,0:T(8,128)(2,1)} %shard_map.136), calls=%async_computation | async-start | bytes 1179648 | tf_op jit(solution)/shard_map/all_to_all | solution.py:486
  13.0 0.8 reshape.28
  13.8 0.7 convert_bitcast_fusion
  14.4 0.1 copy.24
  14.6 0.1 reshape.33
  14.6 0.8 copy.23
  15.4 0.1 eq.15
  15.5 0.1 select_reduce_fusion
  15.6 0.1 copy.25
  15.7 0.1 copy.26
  15.8 4.0 %shard_map.137 = (bf16[4,256,2,512]{3,2,1,0:T(2,128)(2,1)S(1)}, bf16[4,768,2,512]{3,2,1,0:T(2,128)(2,1)}) custom-call(s32[4,64]{1,0:T(4,128)} %table_far.1, s32[4]{0:T(128)} %lens.1, bf16[256,16,2,512]{3,2,1,0:T(2,128)(2,1)} %pool.1), custom_call_target="tpu_custom_call" | custom-call | tf_op jit(solution)/shard_map/pallas_call | solution.py:207
  19.8 6.2 %all-to-all-done.near = bf16[32,8,1152]{2,1,0:T(8,128)(2,1)S(1)} async-done(((bf16[32,8,1152]{2,1,0:T(8,128)(2,1)}), bf16[32,8,1152]{2,1,0:T(8,128)(2,1)S(1)}, u32[]{:S(2)}, u32[]{:S(2)}) %all-to-all-start) | async-done | bytes 589856 | tf_op jit(solution)/shard_map/all_to_all | solution.py:486
  26.0 2.2 %collective-permute-start = (bf16[32,8,1152]{2,1,0:T(8,128)(2,1)S(1)}, bf16[32,8,1152]{2,1,0:T(8,128)(2,1)S(1)}, u32[]{:S(2)}, u32[]{:S(2)}) collective-permute-start(bf16[32,8,1152]{2,1,0:T(8,128)(2,1)S(1)} %all-to-all-done.near), channel_id=1, source_target_pairs={{0,1},{1,0},{2,3},{3,2},{4,5},{5,4},{6,7},{7,6},{8,9},{9,8},{10,11... | collective-permute-start | bytes 1769480 | tf_op jit(solution)/shard_map/ppermute | solution.py:499
  28.2 1.3 %shard_map.138 = (bf16[1,2048,128]{2,1,0:T(8,128)(2,1)S(1)}, f32[256,128]{1,0:T(8,128)S(1)}) custom-call(bf16[32,8,1152]{2,1,0:T(8,128)(2,1)S(1)} %all-to-all-done.near, bf16[1,2048,128]{2,1,0:T(8,128)(2,1)} %wq_far.1), custom_call_target="tpu_custom_call" | custom-call | tf_op jit(solution)/shard_map/pallas_call | solution.py:529
  29.5 0.3 collective-permute-done.far
  29.8 1.1 shard_map.139
  30.9 3.8 %all-to-all-start.1 = ((bf16[32,8,128]{2,1,0:T(8,128)(2,1)}), bf16[32,8,128]{2,1,0:T(8,128)(2,1)S(1)}, u32[]{:S(2)}, u32[]{:S(2)}) async-start(bf16[32,8,128]{2,1,0:T(8,128)(2,1)} %get-tuple-element.35), calls=%async_computation.1 | async-start | bytes 131072 | tf_op jit(solution)/shard_map/all_to_all | solution.py:486
  34.8 0.0 copy-start.3
  34.8 2.2 %copy-done.3 = bf16[2048,2,512]{2,1,0:T(2,128)(2,1)S(1)} copy-done((bf16[2048,2,512]{2,1,0:T(2,128)(2,1)S(1)}, bf16[2048,2,512]{2,1,0:T(2,128)(2,1)}, u32[]{:S(2)}) %copy-start.3) | copy-done | bytes 4194328
  37.0 1.9 %shard_map.140 = (f32[8,128]{1,0:T(8,128)S(1)}, bf16[16,512]{1,0:T(8,128)(2,1)S(1)}, bf16[2,128,512]{2,1,0:T(8,128)(2,1)S(1)}) custom-call(bf16[32,8,1152]{2,1,0:T(8,128)(2,1)S(1)} %all-to-all-done.near, bf16[32,8,1152]{2,1,0:T(8,128)(2,1)S(1)} %collective-permute-done.far, bf16[2048,2,512]{2,1,0:T(2,128)(2,1)S(1)} %copy-done.3, bf16[1,128,2048]{2,1,0:T(8,128)(2,1)} %weight.4), custom_call_target="tpu_custom_call" | custom-call | tf_op jit(solution)/shard_map/pallas_call | solution.py:539
  38.8 0.0 copy-start.7
  38.8 0.7 copy-done.7
  39.5 3.9 %all-to-all-done.1.arrived = bf16[32,8,128]{2,1,0:T(8,128)(2,1)S(1)} async-done(((bf16[32,8,128]{2,1,0:T(8,128)(2,1)}), bf16[32,8,128]{2,1,0:T(8,128)(2,1)S(1)}, u32[]{:S(2)}, u32[]{:S(2)}) %all-to-all-start.1) | async-done | bytes 65568 | tf_op jit(solution)/shard_map/all_to_all | solution.py:486
  43.4 0.0 copy-done.6
  43.4 3.8 %shard_map.141 = bf16[32,8,128]{2,1,0:T(8,128)(2,1)S(1)} custom-call(s32[4]{0:T(128)S(1)} %copy-done.6, f32[8,128]{1,0:T(8,128)S(1)} %get-tuple-element.34.sel, bf16[32,8,128]{2,1,0:T(8,128)(2,1)S(1)} %all-to-all-done.1.arrived, bf16[16,512]{1,0:T(8,128)(2,1)S(1)} %get-tuple-element.36.fresh, bf16[4,256,2,512]{3,2,1,0:T(2,128)(2,1)S(1)} %get-tuple-element.37.start, ...), custom_call_target="tpu_custom_call" | custom-call | tf_op jit(solution)/shard_map/pallas_call | solution.py:348
  47.2 15.4 %all_to_all.30.returned = bf16[32,8,128]{2,1,0:T(8,128)(2,1)S(1)} all-to-all(bf16[32,8,128]{2,1,0:T(8,128)(2,1)S(1)} %shard_map.141), channel_id=1, replica_groups=mesh['req'=32,'rep'=4] {'req'}, dimensions={0} | all-to-all | bytes 131072 | tf_op jit(solution)/shard_map/all_to_all | solution.py:486
  62.6 0.0 copy-done.8
  62.6 2.1 %collective-permute-start.2 = (bf16[2,128,512]{2,1,0:T(8,128)(2,1)S(1)}, bf16[2,128,512]{2,1,0:T(8,128)(2,1)S(1)}, u32[]{:S(2)}, u32[]{:S(2)}) collective-permute-start(bf16[2,128,512]{2,1,0:T(8,128)(2,1)S(1)} %copy-done.8), channel_id=1, source_target_pairs={{0,1},{1,0},{2,3},{3,2},{4,5},{5,4},{6,7},{7,6},{8,9},{9,8},{10,11... | collective-permute-start | bytes 786440 | tf_op jit(solution)/shard_map/ppermute | solution.py:499
  64.7 0.0 collective-permute-start.1
  64.7 0.0 copy-done.4
  64.7 0.5 shard_map.142.part
  65.2 0.7 collective-permute-done.1.returned
  65.9 0.0 collective-permute-done.2.weight
  65.9 0.5 shard_map.143
  66.5 0.0 copy-start
  66.5 0.0 copy-start.1
  66.5 0.0 copy-start.5
  66.5 16.6 %all_to_all.31 = bf16[64,8,512]{2,1,0:T(8,128)(2,1)S(1)} all-to-all(bf16[64,8,512]{2,1,0:T(8,128)(2,1)S(1)} %bitcast.30), channel_id=1, replica_groups={{0,2,4,6,8,10,12,14,16,18,20,22,24,26,28,30,32,34,36,38,40,42,44,46,48,..., dimensions={0} | all-to-all | bytes 1048576 | tf_op jit(solution)/shard_map/all_to_all | solution.py:489
  83.1 0.1 convert_reduce_fusion.1
  83.2 0.1 multiply_reduce_fusion.1
  83.4 0.0 copy-start.2
  83.4 15.6 %all_to_all.32 = bf16[64,8,512]{2,1,0:T(8,128)(2,1)S(1)} all-to-all(bf16[64,8,512]{2,1,0:T(8,128)(2,1)S(1)} %broadcast_in_dim.29), channel_id=1, replica_groups={{0,2,4,6,8,10,12,14,16,18,20,22,24,26,28,30,32,34,36,38,40,42,44,46,48,..., dimensions={0} | all-to-all | bytes 1048576 | tf_op jit(solution)/shard_map/all_to_all | solution.py:489
  99.0 3.2 %collective-permute-start.3 = (bf16[64,8,512]{2,1,0:T(8,128)(2,1)S(1)}, bf16[64,8,512]{2,1,0:T(8,128)(2,1)S(1)}, u32[]{:S(2)}, u32[]{:S(2)}) collective-permute-start(bf16[64,8,512]{2,1,0:T(8,128)(2,1)S(1)} %all_to_all.32), channel_id=1, source_target_pairs={{0,1},{1,0},{2,3},{3,2},{4,5},{5,4},{6,7},{7,6},{8,9},{9,8},{10,11... | collective-permute-start | bytes 1572872 | tf_op jit(solution)/shard_map/ppermute | solution.py:499
  102.2 0.0 copy-done
  102.2 0.0 copy-done.1
  102.2 0.7 shard_map.144
  103.0 0.8 collective-permute-done.3
  103.8 0.0 copy-done.2
  103.8 1.1 shard_map.145
  104.9 0.5 collective-permute-start.4
  105.4 0.4 shard_map.146
  105.8 1.1 collective-permute-done.4
  106.9 0.2 add_convert_fusion
  107.1 16.4 %all_to_all.33 = bf16[64,8,512]{2,1,0:T(8,128)(2,1)S(1)} all-to-all(bf16[64,8,512]{2,1,0:T(8,128)(2,1)S(1)} %bitcast.32), channel_id=1, replica_groups={{0,2,4,6,8,10,12,14,16,18,20,22,24,26,28,30,32,34,36,38,40,42,44,46,48,..., dimensions={0} | all-to-all | bytes 1048576 | tf_op jit(solution)/shard_map/all_to_all | solution.py:489
  123.5 0.1 convert_reduce_fusion
  123.5 0.1 multiply_reduce_fusion
  123.6 2.2 %collective-permute-start.5 = (bf16[8,512]{1,0:T(8,128)(2,1)S(1)}, bf16[8,512]{1,0:T(8,128)(2,1)S(1)}, u32[]{:S(2)}, u32[]{:S(2)}) collective-permute-start(bf16[8,512]{1,0:T(8,128)(2,1)S(1)} %add_convert_fusion.1.refs_0_), channel_id=1, source_target_pairs={{0,1},{1,0},{2,3},{3,2},{4,5},{5,4},{6,7},{7,6},{8,9},{9,8},{10,11... | collective-permute-start | bytes 24584 | tf_op jit(solution)/shard_map/ppermute | solution.py:582
  125.8 0.4 collective-permute-start.6
  126.2 1.3 %collective-permute-start.7 = (bf16[8,512]{1,0:T(8,128)(2,1)S(1)}, bf16[8,512]{1,0:T(8,128)(2,1)S(1)}, u32[]{:S(2)}, u32[]{:S(2)}) collective-permute-start(bf16[8,512]{1,0:T(8,128)(2,1)S(1)} %add_convert_fusion.1.refs_0_), channel_id=1, source_target_pairs={{0,3},{1,2},{2,1},{3,0},{4,7},{5,6},{6,5},{7,4},{8,11},{9,10},{10,... | collective-permute-start | bytes 24584 | tf_op jit(solution)/shard_map/ppermute | solution.py:582
  127.5 0.0 collective-permute-done.5.refs_1_
  127.5 0.8 collective-permute-done.6.refs_2_
  128.3 1.0 collective-permute-done.7.refs_3_
  129.3 0.6 shard_map.147
  (9 shorter events, 0.1 us)
Async XLA Ops:
  1.8 24.2 %all-to-all-start = ((bf16[32,8,1152]{2,1,0:T(8,128)(2,1)}), bf16[32,8,1152]{2,1,0:T(8,128)(2,1)S(1)}, u32[]{:S(2)}, u32[]{:S(2)}) async-start(bf16[32,8,1152]{2,1,0:T(8,128)(2,1)} %shard_map.136), calls=%async_computation | async-start | bytes 1179648 | tf_op jit(solution)/shard_map/all_to_all | solution.py:486
  26.0 3.8 %collective-permute-start = (bf16[32,8,1152]{2,1,0:T(8,128)(2,1)S(1)}, bf16[32,8,1152]{2,1,0:T(8,128)(2,1)S(1)}, u32[]{:S(2)}, u32[]{:S(2)}) collective-permute-start(bf16[32,8,1152]{2,1,0:T(8,128)(2,1)S(1)} %all-to-all-done.near), channel_id=1, source_target_pairs={{0,1},{1,0},{2,3},{3,2},{4,5},{5,4},{6,7},{7,6},{8,9},{9,8},{10,11... | collective-permute-start | bytes 1769480 | tf_op jit(solution)/shard_map/ppermute | solution.py:499
  30.9 12.5 %all-to-all-start.1 = ((bf16[32,8,128]{2,1,0:T(8,128)(2,1)}), bf16[32,8,128]{2,1,0:T(8,128)(2,1)S(1)}, u32[]{:S(2)}, u32[]{:S(2)}) async-start(bf16[32,8,128]{2,1,0:T(8,128)(2,1)} %get-tuple-element.35), calls=%async_computation.1 | async-start | bytes 131072 | tf_op jit(solution)/shard_map/all_to_all | solution.py:486
  34.8 2.2 %copy-start.3 = (bf16[2048,2,512]{2,1,0:T(2,128)(2,1)S(1)}, bf16[2048,2,512]{2,1,0:T(2,128)(2,1)}, u32[]{:S(2)}) copy-start(bf16[2048,2,512]{2,1,0:T(2,128)(2,1)} %wkv.1) | copy-start | bytes 12582916
  37.0 6.4 %copy-start.6 = (s32[4]{0:T(128)S(1)}, s32[4]{0:T(128)}, u32[]{:S(2)}) copy-start(s32[4]{0:T(128)} %lens.1) | copy-start | bytes 52
  38.8 0.7 copy-start.7
  43.4 19.2 %copy-start.8 = (bf16[2,128,512]{2,1,0:T(8,128)(2,1)S(1)}, bf16[2,128,512]{2,1,0:T(8,128)(2,1)}, u32[]{:S(2)}) copy-start(bf16[2,128,512]{2,1,0:T(8,128)(2,1)} %copy-done.7) | copy-start | bytes 786436
  43.4 21.3 %copy-start.4 = (bf16[1,128,2048]{2,1,0:T(8,128)(2,1)S(1)}, bf16[1,128,2048]{2,1,0:T(8,128)(2,1)}, u32[]{:S(2)}) copy-start(bf16[1,128,2048]{2,1,0:T(8,128)(2,1)} %weight.4) | copy-start | bytes 1572868
  62.6 3.3 %collective-permute-start.2 = (bf16[2,128,512]{2,1,0:T(8,128)(2,1)S(1)}, bf16[2,128,512]{2,1,0:T(8,128)(2,1)S(1)}, u32[]{:S(2)}, u32[]{:S(2)}) collective-permute-start(bf16[2,128,512]{2,1,0:T(8,128)(2,1)S(1)} %copy-done.8), channel_id=1, source_target_pairs={{0,1},{1,0},{2,3},{3,2},{4,5},{5,4},{6,7},{7,6},{8,9},{9,8},{10,11... | collective-permute-start | bytes 786440 | tf_op jit(solution)/shard_map/ppermute | solution.py:499
  64.7 1.3 collective-permute-start.1
  66.5 35.8 %copy-start = (bf16[1,2048,352]{1,2,0:T(8,128)(2,1)S(1)}, bf16[1,2048,352]{1,2,0:T(8,128)(2,1)}, u32[]{:S(2)}) copy-start(bf16[1,2048,352]{1,2,0:T(8,128)(2,1)} %param.19) | copy-start | bytes 4325380
  66.5 35.8 %copy-start.1 = (bf16[1,2048,352]{1,2,0:T(8,128)(2,1)S(1)}, bf16[1,2048,352]{1,2,0:T(8,128)(2,1)}, u32[]{:S(2)}) copy-start(bf16[1,2048,352]{1,2,0:T(8,128)(2,1)} %param.20) | copy-start | bytes 4325380
  66.5 35.7 %copy-start.5 = (f32[2,2048]{1,0:T(2,128)S(1)}, f32[2,2048]{1,0:T(2,128)}, u32[]{:S(2)}) copy-start(f32[2,2048]{1,0:T(2,128)} %gains.3) | copy-start | bytes 49156
  83.4 20.4 %copy-start.2 = (bf16[1,352,2048]{2,1,0:T(8,128)(2,1)S(1)}, bf16[1,352,2048]{2,1,0:T(8,128)(2,1)}, u32[]{:S(2)}) copy-start(bf16[1,352,2048]{2,1,0:T(8,128)(2,1)} %weight.5) | copy-start | bytes 4325380
  99.0 4.8 %collective-permute-start.3 = (bf16[64,8,512]{2,1,0:T(8,128)(2,1)S(1)}, bf16[64,8,512]{2,1,0:T(8,128)(2,1)S(1)}, u32[]{:S(2)}, u32[]{:S(2)}) collective-permute-start(bf16[64,8,512]{2,1,0:T(8,128)(2,1)S(1)} %all_to_all.32), channel_id=1, source_target_pairs={{0,1},{1,0},{2,3},{3,2},{4,5},{5,4},{6,7},{7,6},{8,9},{9,8},{10,11... | collective-permute-start | bytes 1572872 | tf_op jit(solution)/shard_map/ppermute | solution.py:499
  104.9 2.0 %collective-permute-start.4 = (bf16[32,2,8,512]{3,2,1,0:T(8,128)(2,1)S(1)}, bf16[32,2,8,512]{3,2,1,0:T(8,128)(2,1)S(1)}, u32[]{:S(2)}, u32[]{:S(2)}) collective-permute-start(bf16[32,2,8,512]{3,2,1,0:T(8,128)(2,1)S(1)} %get-tuple-element.47), channel_id=1, source_target_pairs={{0,1},{1,0},{2,3},{3,2},{4,5},{5,4},{6,7},{7,6},{8,9},{9,8},{10,11... | collective-permute-start | bytes 1572872 | tf_op jit(solution)/shard_map/ppermute | solution.py:499
  123.6 3.9 %collective-permute-start.5 = (bf16[8,512]{1,0:T(8,128)(2,1)S(1)}, bf16[8,512]{1,0:T(8,128)(2,1)S(1)}, u32[]{:S(2)}, u32[]{:S(2)}) collective-permute-start(bf16[8,512]{1,0:T(8,128)(2,1)S(1)} %add_convert_fusion.1.refs_0_), channel_id=1, source_target_pairs={{0,1},{1,0},{2,3},{3,2},{4,5},{5,4},{6,7},{7,6},{8,9},{9,8},{10,11... | collective-permute-start | bytes 24584 | tf_op jit(solution)/shard_map/ppermute | solution.py:582
  125.8 2.5 %collective-permute-start.6 = (bf16[8,512]{1,0:T(8,128)(2,1)S(1)}, bf16[8,512]{1,0:T(8,128)(2,1)S(1)}, u32[]{:S(2)}, u32[]{:S(2)}) collective-permute-start(bf16[8,512]{1,0:T(8,128)(2,1)S(1)} %add_convert_fusion.1.refs_0_), channel_id=1, source_target_pairs={{0,2},{1,3},{2,0},{3,1},{4,6},{5,7},{6,4},{7,5},{8,10},{9,11},{10,... | collective-permute-start | bytes 24584 | tf_op jit(solution)/shard_map/ppermute | solution.py:582
  126.2 3.1 %collective-permute-start.7 = (bf16[8,512]{1,0:T(8,128)(2,1)S(1)}, bf16[8,512]{1,0:T(8,128)(2,1)S(1)}, u32[]{:S(2)}, u32[]{:S(2)}) collective-permute-start(bf16[8,512]{1,0:T(8,128)(2,1)S(1)} %add_convert_fusion.1.refs_0_), channel_id=1, source_target_pairs={{0,3},{1,2},{2,1},{3,0},{4,7},{5,6},{6,5},{7,4},{8,11},{9,10},{10,... | collective-permute-start | bytes 24584 | tf_op jit(solution)/shard_map/ppermute | solution.py:582

commit v5 on v4

--- a/solution.py
+++ b/solution.py
@@ -10,7 +10,8 @@
 
 HD = 128
 EXPERTS = 8
-SPAN = 256
+HEAD = 192
+MIDDLE = 192
 EPSILON = 1e-06
 MASKED = -1e30
 F32 = jnp.float32
@@ -112,7 +113,13 @@
     out[...] = dot(order_of(marks), q.astype(BF16)).astype(BF16).reshape(out.shape)
 
 
-def own_kernel(near, far, wkv, weight, sel, fresh, picked, sems):
+def middle_kernel(cache, out, sem):
+    fetch = pltpu.make_async_copy(cache.at[:, pl.ds(0, MIDDLE)], out, sem)
+    fetch.start()
+    fetch.wait()
+
+
+def own_kernel(near, far, wkv, weight, sel, fresh, picked_far, picked, sems, one):
     halves, _, quarter = picked.shape
     side = 1 - lax.axis_index("rep") % 2
     copies = [
@@ -145,9 +152,12 @@
         v = jnp.concatenate([jnp.where(even, v, 0.0), jnp.where(even, 0.0, v)], axis=0)
         w = wkv[c * HD : (c + 1) * HD].reshape(2 * HD, fresh.shape[1])
         total = total + dot(v.astype(BF16), w)
-    fresh[...] = total.astype(BF16)
     for copy in copies:
         copy.wait()
+    send = pltpu.make_async_copy(picked, picked_far, one)
+    send.start()
+    fresh[...] = total.astype(BF16)
+    send.wait()
 
 
 def page_kernel(table_far, lens_far, pool, start, out, table, lens, staged, sems, back, small):
@@ -159,41 +169,43 @@
     second.wait()
     count = out.shape[0]
     page = pool.shape[1]
-    chunks = 1 + out.shape[1] // SPAN
+    tail = out.shape[1]
+    sizes = (HEAD, MIDDLE, tail - MIDDLE)
+    starts = (0, HEAD, HEAD + MIDDLE)
+    places = (None, pl.ds(0, MIDDLE), pl.ds(MIDDLE, tail - MIDDLE))
 
     def each(act):
-        for c in range(chunks):
+        for part in range(3):
             for j in range(count):
-                if c < 2:
-                    act(j, c)
+                if part < 2:
+                    act(j, part)
                 else:
-                    pl.when(lens[j] > 2 * SPAN)(functools.partial(act, j, c))
-
-    def block_of(j, c):
-        return start.at[j] if c == 0 else staged.at[j, pl.ds((c - 1) * SPAN, SPAN)]
-
-    def read(j, c):
-        block = block_of(j, c)
-        for p in range(SPAN // page):
+                    pl.when(lens[j] > starts[2])(functools.partial(act, j, part))
+
+    def block_of(j, part):
+        return start.at[j] if part == 0 else staged.at[j, places[part]]
+
+    def read(j, part):
+        block = block_of(j, part)
+        for p in range(sizes[part] // page):
             pltpu.make_async_copy(
-                pool.at[table[j, c * (SPAN // page) + p]],
+                pool.at[table[j, starts[part] // page + p]],
                 block.at[pl.ds(p * page, page)],
-                sems.at[j, c],
+                sems.at[j, part],
             ).start()
 
-    def write(j, c):
-        place = out.at[j, pl.ds((c - 1) * SPAN, SPAN)]
-        return pltpu.make_async_copy(block_of(j, c), place, back.at[j, c])
-
-    def forward(j, c):
-        block = block_of(j, c)
-        pltpu.make_async_copy(block, block, sems.at[j, c]).wait()
-        if c:
-            write(j, c).start()
-
-    def finish(j, c):
-        if c:
-            write(j, c).wait()
+    def write(j, part):
+        return pltpu.make_async_copy(block_of(j, part), out.at[j, places[part]], back.at[j, part])
+
+    def forward(j, part):
+        block = block_of(j, part)
+        pltpu.make_async_copy(block, block, sems.at[j, part]).wait()
+        if part:
+            write(j, part).start()
+
+    def finish(j, part):
+        if part:
+            write(j, part).wait()
 
     each(read)
     each(forward)
@@ -203,39 +215,37 @@
 def pages_call(table, lens, pool):
     mine, pages = table.shape
     length = pages * pool.shape[1]
-    tail = (mine, length - SPAN) + pool.shape[2:]
+    tail = (mine, length - HEAD) + pool.shape[2:]
     return call(
         page_kernel,
-        [pltpu.VMEM((mine, SPAN) + pool.shape[2:], BF16), pltpu.HBM(tail, BF16)],
+        [pltpu.VMEM((mine, HEAD) + pool.shape[2:], BF16), pltpu.HBM(tail, BF16)],
         [FAR] * 3,
         [
             pltpu.SMEM(table.shape, jnp.int32),
             pltpu.SMEM(lens.shape, jnp.int32),
             pltpu.VMEM(tail, BF16),
-            pltpu.SemaphoreType.DMA((mine, length // SPAN)),
-            pltpu.SemaphoreType.DMA((mine, length // SPAN)),
+            pltpu.SemaphoreType.DMA((mine, 3)),
+            pltpu.SemaphoreType.DMA((mine, 3)),
             pltpu.SemaphoreType.DMA((2,)),
         ],
         outs=[VM, FAR],
     )(in_hbm(table), in_hbm(lens), in_hbm(pool))
 
 
-def attention_kernel(lens, sel, arrived, fresh, start, far, out, cache, qs, os, sc, ef, sems):
-    count, tail, _, wide = cache.shape
+def attention_kernel(
+    lens, sel, arrived, fresh, start, middle, far, out, cache, qs, os, sc, ef, sems
+):
+    count, rest, _, wide = cache.shape
     requests = range(count)
-    spans = (pl.ds(0, SPAN), pl.ds(SPAN, tail - SPAN))
-
-    def copy_of(j, part):
-        span = spans[part]
-        return pltpu.make_async_copy(far.at[j, span], cache.at[j, span], sems.at[j, part])
+
+    def copy_of(j):
+        return pltpu.make_async_copy(far.at[j, pl.ds(MIDDLE, rest)], cache.at[j], sems.at[j])
 
     for j in requests:
-        copy_of(j, 0).start()
-    for j in requests:
-
-        @pl.when(lens[j] > 2 * SPAN)
+
+        @pl.when(lens[j] > HEAD + MIDDLE)
         def _(j=j):
-            copy_of(j, 1).start()
+            copy_of(j).start()
 
     peers, rows, _ = arrived.shape
     heads = wide // HD
@@ -259,18 +269,20 @@
     e_col = lax.broadcasted_iota(jnp.int32, (2 * group, HD), 1)
     e_row = lax.broadcasted_iota(jnp.int32, (2 * group, HD), 0)
 
+    starts = (0, HEAD, HEAD + MIDDLE)
+
     def rows_of(j, part):
         if part == 0:
-            return start[j].reshape(2 * SPAN, wide)
+            return start[j].reshape(2 * HEAD, wide)
         if part == 1:
-            return cache[j, :SPAN].reshape(2 * SPAN, wide)
-        return cache[j, SPAN:].reshape(2 * (tail - SPAN), wide)
+            return middle[j].reshape(2 * MIDDLE, wide)
+        return cache[j].reshape(2 * rest, wide)
 
     def masked_scores(q, j, part):
         s = dot_rows(q, rows_of(j, part)) * inv_scale
         column = lax.broadcasted_iota(jnp.int32, s.shape, 1)
         return jnp.where(
-            (column % 2 == 0) & (column < 2 * (lens[j] - part * SPAN)), s, MASKED
+            (column % 2 == 0) & (column < 2 * (lens[j] - starts[part])), s, MASKED
         )
 
     def highest(s):
@@ -282,7 +294,7 @@
     def onto_values(p, distance=1):
         return pltpu.roll(p, distance, 1).astype(BF16)
 
-    longer = [jnp.where(lens[j] > 2 * SPAN, 1, 0) for j in requests]
+    longer = [jnp.where(lens[j] > starts[2], 1, 0) for j in requests]
     queries, extras, firsts, seconds, tops = [], [], [], [], []
     for j in requests:
         q = jnp.concatenate([qs[:, 2 * j, :], qs[:, 2 * j + 1, :]], axis=0)
@@ -291,9 +303,6 @@
         queries.append(q)
         extras.append(jnp.where(live, dot_rows(q, extra) * inv_scale, MASKED))
         firsts.append(masked_scores(q, j, 0))
-    for j in requests:
-        copy_of(j, 0).wait()
-    for j in requests:
         seconds.append(masked_scores(queries[j], j, 1))
         top = jnp.maximum(highest(extras[j]), highest(firsts[j]))
         tops.append(jnp.maximum(top, highest(seconds[j])))
@@ -301,7 +310,7 @@
     for j in requests:
 
         def score(_, top, j=j):
-            copy_of(j, 1).wait()
+            copy_of(j).wait()
             s = masked_scores(queries[j], j, 2)
             sc[j] = s
             return jnp.maximum(top, highest(s))
@@ -341,24 +350,25 @@
             out[e * heads + h] = value.astype(BF16)
 
 
-def attention_call(lens, sel, arrived, fresh, start, cache):
+def attention_call(lens, sel, arrived, fresh, start, middle, cache):
     rows, wide = arrived.shape[1], cache.shape[-1]
-    mine, tail = cache.shape[:2]
+    mine = cache.shape[0]
+    rest = cache.shape[1] - MIDDLE
     pairs = 2 * wide // HD
     return call(
         attention_kernel,
         shape_of(arrived.shape),
-        [SM, VM, VM, VM, VM, FAR],
+        [SM, VM, VM, VM, VM, VM, FAR],
         [
-            pltpu.VMEM(cache.shape, BF16),
+            pltpu.VMEM((mine, rest) + cache.shape[2:], BF16),
             pltpu.VMEM((pairs, rows, HD), F32),
             pltpu.VMEM((pairs, rows, HD), F32),
-            pltpu.VMEM((mine, 2 * pairs, 2 * (tail - SPAN)), F32),
+            pltpu.VMEM((mine, 2 * pairs, 2 * rest), F32),
             pltpu.VMEM((HD, wide), BF16),
-            pltpu.SemaphoreType.DMA((mine, 2)),
+            pltpu.SemaphoreType.DMA((mine,)),
         ],
         16,
-    )(lens, sel, arrived, fresh, in_vmem(start), in_hbm(cache))
+    )(lens, sel, arrived, fresh, in_vmem(start), in_vmem(middle), in_hbm(cache))
 
 
 def columns_of(z, core, quarter):
@@ -536,17 +546,30 @@
         query_kernel, [shape_of((req_count, rows, HD)), shape_of((total, HD))], [VM] * 4
     )(near, far, in_vmem(wq), begun)
     arrived = spread_req(ordered)
+    rows_shape = (rep_count // 2, w_out.shape[1], quarter)
     sel, fresh, picked = call(
         own_kernel,
         [
             shape_of((rows, HD), F32),
             shape_of((2 * rows, wide)),
-            shape_of((rep_count // 2, w_out.shape[1], quarter)),
+            pltpu.HBM(rows_shape, BF16),
         ],
         [VM, VM, VM, FAR],
-        [pltpu.SemaphoreType.DMA((rep_count // 2,))],
+        [
+            pltpu.VMEM(rows_shape, BF16),
+            pltpu.SemaphoreType.DMA((rep_count // 2,)),
+            pltpu.SemaphoreType.DMA,
+        ],
+        outs=[VM, VM, FAR],
     )(near, far, w_kv, in_hbm(w_out))
-    back = attention_call(cache_len, sel, arrived, fresh, start, cache)
+    sel, cache = lax.optimization_barrier((sel, cache))
+    middle = call(
+        middle_kernel,
+        pltpu.VMEM((mine, MIDDLE) + cache.shape[2:], BF16),
+        [FAR],
+        [pltpu.SemaphoreType.DMA],
+    )(in_hbm(cache))
+    back = attention_call(cache_len, sel, arrived, fresh, start, middle, cache)
     returned = spread_req(back)
     returned, picked = lax.optimization_barrier((returned, picked))
     returned_x, out_x = other_core(returned), other_core(picked)

time: 131 us -> 131 us (level)
  local copies, waits for them, and re-layouts: 4.95 us -> 2.83 us
    all_to_all x1, blocking collectives: 15.4 us -> 16.8 us  [spread_req(): return lax.all_to_all(value, 'req', split_axis=0, concat_axis=0, tiled=True)]
    unnamed x18 -> x22, local copies, waits for them, and re-layouts: 2.91 us -> 2.23 us
    pallas_call x2 -> x3, Pallas kernels: 7.8 us -> 7.47 us  [the longest x1 3.53 us: pages_call(): call(page_kernel, [pltpu.VMEM((mine, HEAD) + pool.shape[2:], BF16), pltpu...]
  transfers between devices with their start and end apart: 10 -> 10, of which waited for: 8 -> 8; matrix products, arithmetic and copies ran while one was open for 2% -> 1% of each run, Pallas kernels for 7% -> 8%
where the time goes in v5:
time: 131 us; the launch traced here: 130 us
  blocking collectives  65.4 us (50%)
  starting transfers between devices  26.9 us (21%)
  Pallas kernels  18.3 us (14%)
  waiting for transfers between devices  15.8 us (12%)
  local copies, waits for them, and re-layouts  2.83 us (2%)
    all_to_all x3, blocking collectives, spread_wide(): lax.all_to_all(value, ('req', 'rep'), split_axis=0, concat_axis=0, tiled=...  48.6 us
    all_to_all x1, blocking collectives, spread_req(): return lax.all_to_all(value, 'req', split_axis=0, concat_axis=0, tiled=True)  16.8 us
    all_to_all x2, starting transfers between devices, spread_req(): return lax.all_to_all(value, 'req', split_axis=0, concat_axis=0, tiled=True)  15 us
    all_to_all x2, waiting for transfers between devices, spread_req(): return lax.all_to_all(value, 'req', split_axis=0, concat_axis=0, tiled=True)  11.1 us
    ppermute x5, starting transfers between devices, other_core(): return lax.ppermute(value, 'rep', swap)  8 us
    ppermute x3, starting transfers between devices, shards(): lax.ppermute(piece, 'rep', [(p, p ^ m) for p in range(rep_count)])  3.88 us
    pallas_call x1, Pallas kernels, pages_call(): call(page_kernel, [pltpu.VMEM((mine, HEAD) + pool.shape[2:], BF16), pltpu...  3.53 us
    ppermute x5, waiting for transfers between devices, other_core(): return lax.ppermute(value, 'rep', swap)  2.89 us
  transfers between devices with their start and end apart: 10, of which 8 were waited for; matrix products, arithmetic and copies ran while one was open for 1% of the time, Pallas kernels for 8%

profile of v5, /device:TPU:1, one launch (start us, length us, event | category | flops | bytes accessed | tf_op | source)
XLA Modules:
  0.0 130.1 jit_solution(14378995818370990111)
XLA Ops:
  0.0 1.9 %shard_map.136 = bf16[32,8,1152]{2,1,0:T(8,128)(2,1)} custom-call(s32[4]{0:T(128)} %slots_far.1, s32[2,2,2,4]{3,2,1,0:T(2,128)} %bitcast.34, bf16[4,2,2048]{2,1,0:T(2,128)(2,1)} %tokens_far.1, f32[2,2048]{1,0:T(2,128)} %gains.3), custom_call_target="tpu_custom_call" | custom-call | tf_op jit(solution)/shard_map/pallas_call | solution.py:521
  1.9 11.2 %all-to-all-start = ((bf16[32,8,1152]{2,1,0:T(8,128)(2,1)}), bf16[32,8,1152]{2,1,0:T(8,128)(2,1)S(1)}, u32[]{:S(2)}, u32[]{:S(2)}) async-start(bf16[32,8,1152]{2,1,0:T(8,128)(2,1)} %shard_map.136), calls=%async_computation | async-start | bytes 1179648 | tf_op jit(solution)/shard_map/all_to_all | solution.py:496
  13.1 0.0 copy-done.7
  13.1 0.0 copy-done.9
  13.2 0.1 copy.24
  13.3 0.1 reshape.33
  13.4 0.0 copy-done.8
  13.4 0.1 copy.23
  13.5 0.1 eq.15
  13.6 0.1 select_reduce_fusion
  13.6 0.1 copy.25
  13.7 0.1 copy.26
  13.8 3.5 %shard_map.137 = (bf16[4,192,2,512]{3,2,1,0:T(2,128)(2,1)S(1)}, bf16[4,832,2,512]{3,2,1,0:T(2,128)(2,1)}) custom-call(s32[4,64]{1,0:T(4,128)} %table_far.1, s32[4]{0:T(128)} %lens.1, bf16[256,16,2,512]{3,2,1,0:T(2,128)(2,1)} %pool.1), custom_call_target="tpu_custom_call" | custom-call | tf_op jit(solution)/shard_map/pallas_call | solution.py:219
  17.3 8.8 %all-to-all-done.near = bf16[32,8,1152]{2,1,0:T(8,128)(2,1)S(1)} async-done(((bf16[32,8,1152]{2,1,0:T(8,128)(2,1)}), bf16[32,8,1152]{2,1,0:T(8,128)(2,1)S(1)}, u32[]{:S(2)}, u32[]{:S(2)}) %all-to-all-start) | async-done | bytes 589856 | tf_op jit(solution)/shard_map/all_to_all | solution.py:496
  26.1 2.2 %collective-permute-start = (bf16[32,8,1152]{2,1,0:T(8,128)(2,1)S(1)}, bf16[32,8,1152]{2,1,0:T(8,128)(2,1)S(1)}, u32[]{:S(2)}, u32[]{:S(2)}) collective-permute-start(bf16[32,8,1152]{2,1,0:T(8,128)(2,1)S(1)} %all-to-all-done.near), channel_id=1, source_target_pairs={{0,1},{1,0},{2,3},{3,2},{4,5},{5,4},{6,7},{7,6},{8,9},{9,8},{10,11... | collective-permute-start | bytes 1769480 | tf_op jit(solution)/shard_map/ppermute | solution.py:509
  28.3 1.3 %shard_map.138 = (bf16[1,2048,128]{2,1,0:T(8,128)(2,1)S(1)}, f32[256,128]{1,0:T(8,128)S(1)}) custom-call(bf16[32,8,1152]{2,1,0:T(8,128)(2,1)S(1)} %all-to-all-done.near, bf16[1,2048,128]{2,1,0:T(8,128)(2,1)} %wq_far.1), custom_call_target="tpu_custom_call" | custom-call | tf_op jit(solution)/shard_map/pallas_call | solution.py:539
  29.6 0.3 collective-permute-done.far
  29.9 1.1 shard_map.139
  31.1 3.8 %all-to-all-start.1 = ((bf16[32,8,128]{2,1,0:T(8,128)(2,1)}), bf16[32,8,128]{2,1,0:T(8,128)(2,1)S(1)}, u32[]{:S(2)}, u32[]{:S(2)}) async-start(bf16[32,8,128]{2,1,0:T(8,128)(2,1)} %get-tuple-element.39), calls=%async_computation.1 | async-start | bytes 131072 | tf_op jit(solution)/shard_map/all_to_all | solution.py:496
  34.9 0.0 copy-start.3
  34.9 2.2 %copy-done.3 = bf16[2048,2,512]{2,1,0:T(2,128)(2,1)S(1)} copy-done((bf16[2048,2,512]{2,1,0:T(2,128)(2,1)S(1)}, bf16[2048,2,512]{2,1,0:T(2,128)(2,1)}, u32[]{:S(2)}) %copy-start.3) | copy-done | bytes 4194328
  37.1 2.6 %shard_map.140 = (f32[8,128]{1,0:T(8,128)S(1)}, bf16[16,512]{1,0:T(8,128)(2,1)S(1)}, bf16[2,128,512]{2,1,0:T(8,128)(2,1)}) custom-call(bf16[32,8,1152]{2,1,0:T(8,128)(2,1)S(1)} %all-to-all-done.near, bf16[32,8,1152]{2,1,0:T(8,128)(2,1)S(1)} %collective-permute-done.far, bf16[2048,2,512]{2,1,0:T(2,128)(2,1)S(1)} %copy-done.3, bf16[1,128,2048]{2,1,0:T(8,128)(2,1)} %weight.4), custom_call_target="tpu_custom_call" | custom-call | tf_op jit(solution)/shard_map/pallas_call | solution.py:550
  39.7 0.0 copy-start.6
  39.7 1.4 %shard_map.141.middle = bf16[4,192,2,512]{3,2,1,0:T(2,128)(2,1)S(1)} custom-call(bf16[4,832,2,512]{3,2,1,0:T(2,128)(2,1)} %get-tuple-element.42.cache.far), custom_call_target="tpu_custom_call" | custom-call | tf_op jit(solution)/shard_map/pallas_call | solution.py:566
  41.1 2.4 %all-to-all-done.1.arrived = bf16[32,8,128]{2,1,0:T(8,128)(2,1)S(1)} async-done(((bf16[32,8,128]{2,1,0:T(8,128)(2,1)}), bf16[32,8,128]{2,1,0:T(8,128)(2,1)S(1)}, u32[]{:S(2)}, u32[]{:S(2)}) %all-to-all-start.1) | async-done | bytes 65568 | tf_op jit(solution)/shard_map/all_to_all | solution.py:496
  43.5 0.0 copy-done.6
  43.5 2.5 %shard_map.142 = bf16[32,8,128]{2,1,0:T(8,128)(2,1)S(1)} custom-call(s32[4]{0:T(128)S(1)} %copy-done.6, f32[8,128]{1,0:T(8,128)S(1)} %get-tuple-element.38.sel, bf16[32,8,128]{2,1,0:T(8,128)(2,1)S(1)} %all-to-all-done.1.arrived, bf16[16,512]{1,0:T(8,128)(2,1)S(1)} %get-tuple-element.40.fresh, bf16[4,192,2,512]{3,2,1,0:T(2,128)(2,1)S(1)} %get-tuple-element.41.start, ...), custom_call_target="tpu_custom_call" | custom-call | tf_op jit(solution)/shard_map/pallas_call | solution.py:358
  46.1 16.8 %all_to_all.30.returned = bf16[32,8,128]{2,1,0:T(8,128)(2,1)S(1)} all-to-all(bf16[32,8,128]{2,1,0:T(8,128)(2,1)S(1)} %shard_map.142), channel_id=1, replica_groups=mesh['req'=32,'rep'=4] {'req'}, dimensions={0} | all-to-all | bytes 131072 | tf_op jit(solution)/shard_map/all_to_all | solution.py:496
  62.9 0.0 copy-done.10
  62.9 2.1 %collective-permute-start.2 = (bf16[2,128,512]{2,1,0:T(8,128)(2,1)S(1)}, bf16[2,128,512]{2,1,0:T(8,128)(2,1)S(1)}, u32[]{:S(2)}, u32[]{:S(2)}) collective-permute-start(bf16[2,128,512]{2,1,0:T(8,128)(2,1)S(1)} %copy-done.10), channel_id=1, source_target_pairs={{0,1},{1,0},{2,3},{3,2},{4,5},{5,4},{6,7},{7,6},{8,9},{9,8},{10,11... | collective-permute-start | bytes 786440 | tf_op jit(solution)/shard_map/ppermute | solution.py:509
  65.0 0.0 collective-permute-start.1
  65.0 0.0 copy-done.4
  65.0 0.5 shard_map.143.part
  65.5 0.7 collective-permute-done.1.returned
  66.2 0.0 collective-permute-done.2.weight
  66.2 0.5 shard_map.144
  66.7 0.0 copy-start
  66.8 0.0 copy-start.1
  66.8 0.0 copy-start.5
  66.8 16.6 %all_to_all.31 = bf16[64,8,512]{2,1,0:T(8,128)(2,1)S(1)} all-to-all(bf16[64,8,512]{2,1,0:T(8,128)(2,1)S(1)} %bitcast.30), channel_id=1, replica_groups={{0,2,4,6,8,10,12,14,16,18,20,22,24,26,28,30,32,34,36,38,40,42,44,46,48,..., dimensions={0} | all-to-all | bytes 1048576 | tf_op jit(solution)/shard_map/all_to_all | solution.py:499
  83.4 0.1 convert_reduce_fusion.1
  83.5 0.1 multiply_reduce_fusion.1
  83.6 15.5 %all_to_all.32 = bf16[64,8,512]{2,1,0:T(8,128)(2,1)S(1)} all-to-all(bf16[64,8,512]{2,1,0:T(8,128)(2,1)S(1)} %broadcast_in_dim.29), channel_id=1, replica_groups={{0,2,4,6,8,10,12,14,16,18,20,22,24,26,28,30,32,34,36,38,40,42,44,46,48,..., dimensions={0} | all-to-all | bytes 1048576 | tf_op jit(solution)/shard_map/all_to_all | solution.py:499
  99.2 3.2 %collective-permute-start.3 = (bf16[64,8,512]{2,1,0:T(8,128)(2,1)S(1)}, bf16[64,8,512]{2,1,0:T(8,128)(2,1)S(1)}, u32[]{:S(2)}, u32[]{:S(2)}) collective-permute-start(bf16[64,8,512]{2,1,0:T(8,128)(2,1)S(1)} %all_to_all.32), channel_id=1, source_target_pairs={{0,1},{1,0},{2,3},{3,2},{4,5},{5,4},{6,7},{7,6},{8,9},{9,8},{10,11... | collective-permute-start | bytes 1572872 | tf_op jit(solution)/shard_map/ppermute | solution.py:509
  102.4 0.0 copy-done
  102.4 0.0 copy-done.1
  102.4 0.0 copy-done.5
  102.4 0.7 shard_map.145
  103.1 0.8 collective-permute-done.3
  103.9 1.1 shard_map.146
  105.0 0.5 collective-permute-start.4
  105.5 0.4 shard_map.147
  105.9 1.1 collective-permute-done.4
  107.0 0.2 add_convert_fusion
  107.2 16.4 %all_to_all.33 = bf16[64,8,512]{2,1,0:T(8,128)(2,1)S(1)} all-to-all(bf16[64,8,512]{2,1,0:T(8,128)(2,1)S(1)} %bitcast.32), channel_id=1, replica_groups={{0,2,4,6,8,10,12,14,16,18,20,22,24,26,28,30,32,34,36,38,40,42,44,46,48,..., dimensions={0} | all-to-all | bytes 1048576 | tf_op jit(solution)/shard_map/all_to_all | solution.py:499
  123.6 0.1 convert_reduce_fusion
  123.7 0.1 multiply_reduce_fusion
  123.8 2.2 %collective-permute-start.5 = (bf16[8,512]{1,0:T(8,128)(2,1)S(1)}, bf16[8,512]{1,0:T(8,128)(2,1)S(1)}, u32[]{:S(2)}, u32[]{:S(2)}) collective-permute-start(bf16[8,512]{1,0:T(8,128)(2,1)S(1)} %add_convert_fusion.1.refs_0_), channel_id=1, source_target_pairs={{0,1},{1,0},{2,3},{3,2},{4,5},{5,4},{6,7},{7,6},{8,9},{9,8},{10,11... | collective-permute-start | bytes 24584 | tf_op jit(solution)/shard_map/ppermute | solution.py:605
  126.0 0.4 collective-permute-start.6
  126.3 1.3 %collective-permute-start.7 = (bf16[8,512]{1,0:T(8,128)(2,1)S(1)}, bf16[8,512]{1,0:T(8,128)(2,1)S(1)}, u32[]{:S(2)}, u32[]{:S(2)}) collective-permute-start(bf16[8,512]{1,0:T(8,128)(2,1)S(1)} %add_convert_fusion.1.refs_0_), channel_id=1, source_target_pairs={{0,3},{1,2},{2,1},{3,0},{4,7},{5,6},{6,5},{7,4},{8,11},{9,10},{10,... | collective-permute-start | bytes 24584 | tf_op jit(solution)/shard_map/ppermute | solution.py:605
  127.7 0.0 collective-permute-done.5.refs_1_
  127.7 0.8 collective-permute-done.6.refs_2_
  128.5 1.0 collective-permute-done.7.refs_3_
  129.4 0.6 shard_map.148
  (14 shorter events, 0.1 us)
Async XLA Ops:
  0.0 13.4 %copy-start.8 = (s32[4,2,2,2]{0,3,2,1:T(2,128)S(1)}, s32[4,2,2,2]{0,3,2,1:T(2,128)}, u32[]{:S(2)}) copy-start(s32[4,2,2,2]{0,3,2,1:T(2,128)} %param.25) | copy-start | bytes 388
  0.0 13.1 %copy-start.7 = (bf16[4,2,2048]{2,1,0:T(2,128)(2,1)S(1)}, bf16[4,2,2048]{2,1,0:T(2,128)(2,1)}, u32[]{:S(2)}) copy-start(bf16[4,2,2048]{2,1,0:T(2,128)(2,1)} %tokens_far.1) | copy-start | bytes 98308
  0.0 13.1 %copy-start.9 = (bf16[4,2,2,2]{0,3,2,1:T(2,128)(2,1)S(1)}, bf16[4,2,2,2]{0,3,2,1:T(2,128)(2,1)}, u32[]{:S(2)}) copy-start(bf16[4,2,2,2]{0,3,2,1:T(2,128)(2,1)} %param.26) | copy-start | bytes 196
  1.9 24.2 %all-to-all-start = ((bf16[32,8,1152]{2,1,0:T(8,128)(2,1)}), bf16[32,8,1152]{2,1,0:T(8,128)(2,1)S(1)}, u32[]{:S(2)}, u32[]{:S(2)}) async-start(bf16[32,8,1152]{2,1,0:T(8,128)(2,1)} %shard_map.136), calls=%async_computation | async-start | bytes 1179648 | tf_op jit(solution)/shard_map/all_to_all | solution.py:496
  26.1 3.8 %collective-permute-start = (bf16[32,8,1152]{2,1,0:T(8,128)(2,1)S(1)}, bf16[32,8,1152]{2,1,0:T(8,128)(2,1)S(1)}, u32[]{:S(2)}, u32[]{:S(2)}) collective-permute-start(bf16[32,8,1152]{2,1,0:T(8,128)(2,1)S(1)} %all-to-all-done.near), channel_id=1, source_target_pairs={{0,1},{1,0},{2,3},{3,2},{4,5},{5,4},{6,7},{7,6},{8,9},{9,8},{10,11... | collective-permute-start | bytes 1769480 | tf_op jit(solution)/shard_map/ppermute | solution.py:509
  31.1 12.5 %all-to-all-start.1 = ((bf16[32,8,128]{2,1,0:T(8,128)(2,1)}), bf16[32,8,128]{2,1,0:T(8,128)(2,1)S(1)}, u32[]{:S(2)}, u32[]{:S(2)}) async-start(bf16[32,8,128]{2,1,0:T(8,128)(2,1)} %get-tuple-element.39), calls=%async_computation.1 | async-start | bytes 131072 | tf_op jit(solution)/shard_map/all_to_all | solution.py:496
  34.9 2.2 %copy-start.3 = (bf16[2048,2,512]{2,1,0:T(2,128)(2,1)S(1)}, bf16[2048,2,512]{2,1,0:T(2,128)(2,1)}, u32[]{:S(2)}) copy-start(bf16[2048,2,512]{2,1,0:T(2,128)(2,1)} %wkv.1) | copy-start | bytes 12582916
  39.7 3.8 %copy-start.6 = (s32[4]{0:T(128)S(1)}, s32[4]{0:T(128)}, u32[]{:S(2)}) copy-start(s32[4]{0:T(128)} %lens.1) | copy-start | bytes 52
  43.5 19.3 %copy-start.10 = (bf16[2,128,512]{2,1,0:T(8,128)(2,1)S(1)}, bf16[2,128,512]{2,1,0:T(8,128)(2,1)}, u32[]{:S(2)}) copy-start(bf16[2,128,512]{2,1,0:T(8,128)(2,1)} %get-tuple-element.45) | copy-start | bytes 786436
  43.5 21.4 %copy-start.4 = (bf16[1,128,2048]{2,1,0:T(8,128)(2,1)S(1)}, bf16[1,128,2048]{2,1,0:T(8,128)(2,1)}, u32[]{:S(2)}) copy-start(bf16[1,128,2048]{2,1,0:T(8,128)(2,1)} %weight.4) | copy-start | bytes 1572868
  62.9 3.3 %collective-permute-start.2 = (bf16[2,128,512]{2,1,0:T(8,128)(2,1)S(1)}, bf16[2,128,512]{2,1,0:T(8,128)(2,1)S(1)}, u32[]{:S(2)}, u32[]{:S(2)}) collective-permute-start(bf16[2,128,512]{2,1,0:T(8,128)(2,1)S(1)} %copy-done.10), channel_id=1, source_target_pairs={{0,1},{1,0},{2,3},{3,2},{4,5},{5,4},{6,7},{7,6},{8,9},{9,8},{10,11... | collective-permute-start | bytes 786440 | tf_op jit(solution)/shard_map/ppermute | solution.py:509
  65.0 1.3 collective-permute-start.1
  66.7 35.6 %copy-start = (bf16[1,2048,352]{1,2,0:T(8,128)(2,1)S(1)}, bf16[1,2048,352]{1,2,0:T(8,128)(2,1)}, u32[]{:S(2)}) copy-start(bf16[1,2048,352]{1,2,0:T(8,128)(2,1)} %param.19) | copy-start | bytes 4325380
  66.8 35.6 %copy-start.1 = (bf16[1,2048,352]{1,2,0:T(8,128)(2,1)S(1)}, bf16[1,2048,352]{1,2,0:T(8,128)(2,1)}, u32[]{:S(2)}) copy-start(bf16[1,2048,352]{1,2,0:T(8,128)(2,1)} %param.20) | copy-start | bytes 4325380
  66.8 35.6 %copy-start.5 = (f32[2,2048]{1,0:T(2,128)S(1)}, f32[2,2048]{1,0:T(2,128)}, u32[]{:S(2)}) copy-start(f32[2,2048]{1,0:T(2,128)} %gains.3) | copy-start | bytes 49156
  99.2 4.8 %collective-permute-start.3 = (bf16[64,8,512]{2,1,0:T(8,128)(2,1)S(1)}, bf16[64,8,512]{2,1,0:T(8,128)(2,1)S(1)}, u32[]{:S(2)}, u32[]{:S(2)}) collective-permute-start(bf16[64,8,512]{2,1,0:T(8,128)(2,1)S(1)} %all_to_all.32), channel_id=1, source_target_pairs={{0,1},{1,0},{2,3},{3,2},{4,5},{5,4},{6,7},{7,6},{8,9},{9,8},{10,11... | collective-permute-start | bytes 1572872 | tf_op jit(solution)/shard_map/ppermute | solution.py:509
  102.4 1.5 %copy-start.2 = (bf16[1,352,2048]{2,1,0:T(8,128)(2,1)S(1)}, bf16[1,352,2048]{2,1,0:T(8,128)(2,1)}, u32[]{:S(2)}) copy-start(bf16[1,352,2048]{2,1,0:T(8,128)(2,1)} %weight.5) | copy-start | bytes 4325380
  105.0 2.0 %collective-permute-start.4 = (bf16[32,2,8,512]{3,2,1,0:T(8,128)(2,1)S(1)}, bf16[32,2,8,512]{3,2,1,0:T(8,128)(2,1)S(1)}, u32[]{:S(2)}, u32[]{:S(2)}) collective-permute-start(bf16[32,2,8,512]{3,2,1,0:T(8,128)(2,1)S(1)} %get-tuple-element.51), channel_id=1, source_target_pairs={{0,1},{1,0},{2,3},{3,2},{4,5},{5,4},{6,7},{7,6},{8,9},{9,8},{10,11... | collective-permute-start | bytes 1572872 | tf_op jit(solution)/shard_map/ppermute | solution.py:509
  123.8 3.9 %collective-permute-start.5 = (bf16[8,512]{1,0:T(8,128)(2,1)S(1)}, bf16[8,512]{1,0:T(8,128)(2,1)S(1)}, u32[]{:S(2)}, u32[]{:S(2)}) collective-permute-start(bf16[8,512]{1,0:T(8,128)(2,1)S(1)} %add_convert_fusion.1.refs_0_), channel_id=1, source_target_pairs={{0,1},{1,0},{2,3},{3,2},{4,5},{5,4},{6,7},{7,6},{8,9},{9,8},{10,11... | collective-permute-start | bytes 24584 | tf_op jit(solution)/shard_map/ppermute | solution.py:605
  126.0 2.5 %collective-permute-start.6 = (bf16[8,512]{1,0:T(8,128)(2,1)S(1)}, bf16[8,512]{1,0:T(8,128)(2,1)S(1)}, u32[]{:S(2)}, u32[]{:S(2)}) collective-permute-start(bf16[8,512]{1,0:T(8,128)(2,1)S(1)} %add_convert_fusion.1.refs_0_), channel_id=1, source_target_pairs={{0,2},{1,3},{2,0},{3,1},{4,6},{5,7},{6,4},{7,5},{8,10},{9,11},{10,... | collective-permute-start | bytes 24584 | tf_op jit(solution)/shard_map/ppermute | solution.py:605
  126.3 3.1 %collective-permute-start.7 = (bf16[8,512]{1,0:T(8,128)(2,1)S(1)}, bf16[8,512]{1,0:T(8,128)(2,1)S(1)}, u32[]{:S(2)}, u32[]{:S(2)}) collective-permute-start(bf16[8,512]{1,0:T(8,128)(2,1)S(1)} %add_convert_fusion.1.refs_0_), channel_id=1, source_target_pairs={{0,3},{1,2},{2,1},{3,0},{4,7},{5,6},{6,5},{7,4},{8,11},{9,10},{10,... | collective-permute-start | bytes 24584 | tf_op jit(solution)/shard_map/ppermute | solution.py:605

commit v6 on v5

--- a/solution.py
+++ b/solution.py
@@ -10,8 +10,8 @@
 
 HD = 128
 EXPERTS = 8
-HEAD = 192
-MIDDLE = 192
+HEAD = 256
+MIDDLE = 128
 EPSILON = 1e-06
 MASKED = -1e30
 F32 = jnp.float32
@@ -113,18 +113,12 @@
     out[...] = dot(order_of(marks), q.astype(BF16)).astype(BF16).reshape(out.shape)
 
 
-def middle_kernel(cache, out, sem):
-    fetch = pltpu.make_async_copy(cache.at[:, pl.ds(0, MIDDLE)], out, sem)
-    fetch.start()
-    fetch.wait()
-
-
-def own_kernel(near, far, wkv, weight, sel, fresh, picked_far, picked, sems, one):
-    halves, _, quarter = picked.shape
-    side = 1 - lax.axis_index("rep") % 2
+def own_kernel(near, far, wkv_far, sel, fresh, wkv, sems):
+    pieces = sems.shape[0]
+    size = wkv.shape[0] // pieces
     copies = [
-        pltpu.make_async_copy(weight.at[0, :, columns_of(z, side, quarter)], picked.at[z], sems.at[z])
-        for z in range(halves)
+        pltpu.make_async_copy(wkv_far.at[pl.ds(i * size, size)], wkv.at[pl.ds(i * size, size)], sems.at[i])
+        for i in range(pieces)
     ]
     for copy in copies:
         copy.start()
@@ -148,19 +142,26 @@
     even = lax.broadcasted_iota(jnp.int32, (rows, 2 * HD), 1) % 2 == 0
     total = jnp.zeros(fresh.shape, F32)
     for c in range(2 * spans):
+        if c * HD % size == 0:
+            copies[c * HD // size].wait()
         v = doubled[c * rows : (c + 1) * rows]
         v = jnp.concatenate([jnp.where(even, v, 0.0), jnp.where(even, 0.0, v)], axis=0)
         w = wkv[c * HD : (c + 1) * HD].reshape(2 * HD, fresh.shape[1])
         total = total + dot(v.astype(BF16), w)
-    for copy in copies:
-        copy.wait()
-    send = pltpu.make_async_copy(picked, picked_far, one)
-    send.start()
     fresh[...] = total.astype(BF16)
-    send.wait()
-
-
-def page_kernel(table_far, lens_far, pool, start, out, table, lens, staged, sems, back, small):
+
+
+def page_kernel(
+    table_far, lens_far, pool, weight, start, out, picked_far, table, lens, staged, picked, sems, back, small, pick
+):
+    halves, _, quarter = picked.shape
+    side = 1 - lax.axis_index("rep") % 2
+    picks = [
+        pltpu.make_async_copy(weight.at[0, :, columns_of(z, side, quarter)], picked.at[z], pick.at[z])
+        for z in range(halves)
+    ]
+    for copy in picks:
+        copy.start()
     first = pltpu.make_async_copy(table_far, table, small.at[0])
     second = pltpu.make_async_copy(lens_far, lens, small.at[1])
     first.start()
@@ -208,33 +209,47 @@
             write(j, part).wait()
 
     each(read)
+    for copy in picks:
+        copy.wait()
+    send = pltpu.make_async_copy(picked, picked_far, pick.at[halves])
+    send.start()
     each(forward)
     each(finish)
-
-
-def pages_call(table, lens, pool):
+    send.wait()
+
+
+def pages_call(table, lens, pool, weight, quarter):
     mine, pages = table.shape
     length = pages * pool.shape[1]
     tail = (mine, length - HEAD) + pool.shape[2:]
+    rows_shape = (weight.shape[2] // (2 * quarter), weight.shape[1], quarter)
     return call(
         page_kernel,
-        [pltpu.VMEM((mine, HEAD) + pool.shape[2:], BF16), pltpu.HBM(tail, BF16)],
-        [FAR] * 3,
+        [
+            pltpu.VMEM((mine, HEAD) + pool.shape[2:], BF16),
+            pltpu.HBM(tail, BF16),
+            pltpu.HBM(rows_shape, BF16),
+        ],
+        [FAR] * 4,
         [
             pltpu.SMEM(table.shape, jnp.int32),
             pltpu.SMEM(lens.shape, jnp.int32),
             pltpu.VMEM(tail, BF16),
+            pltpu.VMEM(rows_shape, BF16),
             pltpu.SemaphoreType.DMA((mine, 3)),
             pltpu.SemaphoreType.DMA((mine, 3)),
             pltpu.SemaphoreType.DMA((2,)),
+            pltpu.SemaphoreType.DMA((rows_shape[0] + 1,)),
         ],
-        outs=[VM, FAR],
-    )(in_hbm(table), in_hbm(lens), in_hbm(pool))
+        outs=[VM, FAR, FAR],
+    )(in_hbm(table), in_hbm(lens), in_hbm(pool), in_hbm(weight))
 
 
 def attention_kernel(
-    lens, sel, arrived, fresh, start, middle, far, out, cache, qs, os, sc, ef, sems
+    lens, sel, arrived, fresh, start, far, out, middle, cache, qs, os, sc, ef, sems, one
 ):
+    fetch = pltpu.make_async_copy(far.at[:, pl.ds(0, MIDDLE)], middle, one)
+    fetch.start()
     count, rest, _, wide = cache.shape
     requests = range(count)
 
@@ -303,6 +318,8 @@
         queries.append(q)
         extras.append(jnp.where(live, dot_rows(q, extra) * inv_scale, MASKED))
         firsts.append(masked_scores(q, j, 0))
+    fetch.wait()
+    for j in requests:
         seconds.append(masked_scores(queries[j], j, 1))
         top = jnp.maximum(highest(extras[j]), highest(firsts[j]))
         tops.append(jnp.maximum(top, highest(seconds[j])))
@@ -350,7 +367,7 @@
             out[e * heads + h] = value.astype(BF16)
 
 
-def attention_call(lens, sel, arrived, fresh, start, middle, cache):
+def attention_call(lens, sel, arrived, fresh, start, cache):
     rows, wide = arrived.shape[1], cache.shape[-1]
     mine = cache.shape[0]
     rest = cache.shape[1] - MIDDLE
@@ -358,17 +375,19 @@
     return call(
         attention_kernel,
         shape_of(arrived.shape),
-        [SM, VM, VM, VM, VM, VM, FAR],
+        [SM, VM, VM, VM, VM, FAR],
         [
+            pltpu.VMEM((mine, MIDDLE) + cache.shape[2:], BF16),
             pltpu.VMEM((mine, rest) + cache.shape[2:], BF16),
             pltpu.VMEM((pairs, rows, HD), F32),
             pltpu.VMEM((pairs, rows, HD), F32),
             pltpu.VMEM((mine, 2 * pairs, 2 * rest), F32),
             pltpu.VMEM((HD, wide), BF16),
             pltpu.SemaphoreType.DMA((mine,)),
+            pltpu.SemaphoreType.DMA,
         ],
         16,
-    )(lens, sel, arrived, fresh, in_vmem(start), in_vmem(middle), in_hbm(cache))
+    )(lens, sel, arrived, fresh, in_vmem(start), in_hbm(cache))
 
 
 def columns_of(z, core, quarter):
@@ -531,9 +550,9 @@
         ],
     )(in_hbm(new_slot), in_hbm(routes), in_hbm(tokens), in_hbm(norm_gains))
     near = spread_req(message)
-    start, cache = pages_call(page_table, cache_len, kv_pages)
-    near, start, cache, shares, kept = lax.optimization_barrier(
-        (near, start, cache, shares, kept)
+    start, cache, picked = pages_call(page_table, cache_len, kv_pages, w_out, quarter)
+    near, start, cache, picked, shares, kept = lax.optimization_barrier(
+        (near, start, cache, picked, shares, kept)
     )
     far = other_core(near)
     wq, begun = call(
@@ -546,30 +565,13 @@
         query_kernel, [shape_of((req_count, rows, HD)), shape_of((total, HD))], [VM] * 4
     )(near, far, in_vmem(wq), begun)
     arrived = spread_req(ordered)
-    rows_shape = (rep_count // 2, w_out.shape[1], quarter)
-    sel, fresh, picked = call(
+    sel, fresh = call(
         own_kernel,
-        [
-            shape_of((rows, HD), F32),
-            shape_of((2 * rows, wide)),
-            pltpu.HBM(rows_shape, BF16),
-        ],
-        [VM, VM, VM, FAR],
-        [
-            pltpu.VMEM(rows_shape, BF16),
-            pltpu.SemaphoreType.DMA((rep_count // 2,)),
-            pltpu.SemaphoreType.DMA,
-        ],
-        outs=[VM, VM, FAR],
-    )(near, far, w_kv, in_hbm(w_out))
-    sel, cache = lax.optimization_barrier((sel, cache))
-    middle = call(
-        middle_kernel,
-        pltpu.VMEM((mine, MIDDLE) + cache.shape[2:], BF16),
-        [FAR],
-        [pltpu.SemaphoreType.DMA],
-    )(in_hbm(cache))
-    back = attention_call(cache_len, sel, arrived, fresh, start, middle, cache)
+        [shape_of((rows, HD), F32), shape_of((2 * rows, wide))],
+        [VM, VM, FAR],
+        [pltpu.VMEM(w_kv.shape, BF16), pltpu.SemaphoreType.DMA((8,))],
+    )(near, far, in_hbm(w_kv))
+    back = attention_call(cache_len, sel, arrived, fresh, start, cache)
     returned = spread_req(back)
     returned, picked = lax.optimization_barrier((returned, picked))
     returned_x, out_x = other_core(returned), other_core(picked)

time: 131 us -> 130 us (level)
  blocking collectives: 65.4 us -> 61.9 us
  Pallas kernels: 18.3 us -> 19.9 us
    all_to_all x1, blocking collectives: 16.8 us -> 13.2 us  [spread_req(): return lax.all_to_all(value, 'req', split_axis=0, concat_axis=0, tiled=True)]
    unnamed x22 -> x14, local copies, waits for them, and re-layouts: 2.23 us -> 0.04 us
    pallas_call x3 -> x2, Pallas kernels: 6.54 us -> 7.44 us  [the longest x1 4.79 us: attention_call(): call(attention_kernel, shape_of(arrived.shape), [SM, VM, VM, VM, VM, FAR]...]
  transfers between devices with their start and end apart: 10 -> 10, of which waited for: 8 -> 8; matrix products, arithmetic and copies ran while one was open for 1% -> 2% of each run, Pallas kernels for 8% -> 8%
where the time goes in v6:
time: 130 us
  blocking collectives  61.9 us (48%)
  starting transfers between devices  27.7 us (21%)
  Pallas kernels  19.9 us (15%)
  waiting for transfers between devices  16.5 us (13%)
  local copies, waits for them, and re-layouts  2.08 us (2%)
    all_to_all x3, blocking collectives, spread_wide(): lax.all_to_all(value, ('req', 'rep'), split_axis=0, concat_axis=0, tiled=...  48.7 us
    all_to_all x2, starting transfers between devices, spread_req(): return lax.all_to_all(value, 'req', split_axis=0, concat_axis=0, tiled=True)  15 us
    all_to_all x1, blocking collectives, spread_req(): return lax.all_to_all(value, 'req', split_axis=0, concat_axis=0, tiled=True)  13.2 us
    all_to_all x2, waiting for transfers between devices, spread_req(): return lax.all_to_all(value, 'req', split_axis=0, concat_axis=0, tiled=True)  11.9 us
    ppermute x5, starting transfers between devices, other_core(): return lax.ppermute(value, 'rep', swap)  8.81 us
    pallas_call x1, Pallas kernels, attention_call(): call(attention_kernel, shape_of(arrived.shape), [SM, VM, VM, VM, VM, FAR]...  4.79 us
    pallas_call x1, Pallas kernels, pages_call(): call(page_kernel, [pltpu.VMEM((mine, HEAD) + pool.shape[2:], BF16), pltpu...  4.28 us
    ppermute x3, starting transfers between devices, shards(): lax.ppermute(piece, 'rep', [(p, p ^ m) for p in range(rep_count)])  3.88 us
  transfers between devices with their start and end apart: 10, of which 8 were waited for; matrix products, arithmetic and copies ran while one was open for 2% of the time, Pallas kernels for 8%

profile of v6, /device:TPU:1, one launch (start us, length us, event | category | flops | bytes accessed | tf_op | source)
XLA Modules:
  0.0 129.5 jit_solution(10106001239092507092)
XLA Ops:
  0.0 1.8 %shard_map.136 = bf16[32,8,1152]{2,1,0:T(8,128)(2,1)} custom-call(s32[4]{0:T(128)} %slots_far.1, s32[2,2,2,4]{3,2,1,0:T(2,128)} %bitcast.34, bf16[4,2,2048]{2,1,0:T(2,128)(2,1)} %tokens_far.1, f32[2,2048]{1,0:T(2,128)} %gains.3), custom_call_target="tpu_custom_call" | custom-call | tf_op jit(solution)/shard_map/pallas_call | solution.py:540
  1.8 11.2 %all-to-all-start = ((bf16[32,8,1152]{2,1,0:T(8,128)(2,1)}), bf16[32,8,1152]{2,1,0:T(8,128)(2,1)S(1)}, u32[]{:S(2)}, u32[]{:S(2)}) async-start(bf16[32,8,1152]{2,1,0:T(8,128)(2,1)} %shard_map.136), calls=%async_computation | async-start | bytes 1179648 | tf_op jit(solution)/shard_map/all_to_all | solution.py:515
  13.0 0.8 reshape.28
  13.8 0.7 convert_bitcast_fusion
  14.5 0.1 copy.24
  14.6 0.1 reshape.33
  14.7 0.8 copy.23
  15.5 0.1 eq.15
  15.5 0.1 select_reduce_fusion
  15.6 0.1 copy.25
  15.7 0.1 copy.26
  15.8 4.3 %shard_map.137 = (bf16[4,256,2,512]{3,2,1,0:T(2,128)(2,1)S(1)}, bf16[4,768,2,512]{3,2,1,0:T(2,128)(2,1)}, bf16[2,128,512]{2,1,0:T(8,128)(2,1)}) custom-call(s32[4,64]{1,0:T(4,128)} %table_far.1, s32[4]{0:T(128)} %lens.1, bf16[256,16,2,512]{3,2,1,0:T(2,128)(2,1)} %pool.1, bf16[1,128,2048]{2,1,0:T(8,128)(2,1)} %weight.4), custom_call_target="tpu_custom_call" | custom-call | tf_op jit(solution)/shard_map/pallas_call | solution.py:226
  20.1 5.9 %all-to-all-done.near = bf16[32,8,1152]{2,1,0:T(8,128)(2,1)S(1)} async-done(((bf16[32,8,1152]{2,1,0:T(8,128)(2,1)}), bf16[32,8,1152]{2,1,0:T(8,128)(2,1)S(1)}, u32[]{:S(2)}, u32[]{:S(2)}) %all-to-all-start) | async-done | bytes 589856 | tf_op jit(solution)/shard_map/all_to_all | solution.py:515
  26.0 2.2 %collective-permute-start = (bf16[32,8,1152]{2,1,0:T(8,128)(2,1)S(1)}, bf16[32,8,1152]{2,1,0:T(8,128)(2,1)S(1)}, u32[]{:S(2)}, u32[]{:S(2)}) collective-permute-start(bf16[32,8,1152]{2,1,0:T(8,128)(2,1)S(1)} %all-to-all-done.near), channel_id=1, source_target_pairs={{0,1},{1,0},{2,3},{3,2},{4,5},{5,4},{6,7},{7,6},{8,9},{9,8},{10,11... | collective-permute-start | bytes 1769480 | tf_op jit(solution)/shard_map/ppermute | solution.py:528
  28.2 1.3 %shard_map.138 = (bf16[1,2048,128]{2,1,0:T(8,128)(2,1)S(1)}, f32[256,128]{1,0:T(8,128)S(1)}) custom-call(bf16[32,8,1152]{2,1,0:T(8,128)(2,1)S(1)} %all-to-all-done.near, bf16[1,2048,128]{2,1,0:T(8,128)(2,1)} %wq_far.1), custom_call_target="tpu_custom_call" | custom-call | tf_op jit(solution)/shard_map/pallas_call | solution.py:558
  29.5 0.3 collective-permute-done.far
  29.8 1.1 shard_map.139
  30.9 3.8 %all-to-all-start.1 = ((bf16[32,8,128]{2,1,0:T(8,128)(2,1)}), bf16[32,8,128]{2,1,0:T(8,128)(2,1)S(1)}, u32[]{:S(2)}, u32[]{:S(2)}) async-start(bf16[32,8,128]{2,1,0:T(8,128)(2,1)} %get-tuple-element.37), calls=%async_computation.1 | async-start | bytes 131072 | tf_op jit(solution)/shard_map/all_to_all | solution.py:515
  34.8 0.0 copy-start.5
  34.8 2.7 %shard_map.140 = (f32[8,128]{1,0:T(8,128)S(1)}, bf16[16,512]{1,0:T(8,128)(2,1)S(1)}) custom-call(bf16[32,8,1152]{2,1,0:T(8,128)(2,1)S(1)} %all-to-all-done.near, bf16[32,8,1152]{2,1,0:T(8,128)(2,1)S(1)} %collective-permute-done.far, bf16[2048,2,512]{2,1,0:T(2,128)(2,1)} %wkv_far.1), custom_call_target="tpu_custom_call" | custom-call | tf_op jit(solution)/shard_map/pallas_call | solution.py:568
  37.5 6.0 %all-to-all-done.1.arrived = bf16[32,8,128]{2,1,0:T(8,128)(2,1)S(1)} async-done(((bf16[32,8,128]{2,1,0:T(8,128)(2,1)}), bf16[32,8,128]{2,1,0:T(8,128)(2,1)S(1)}, u32[]{:S(2)}, u32[]{:S(2)}) %all-to-all-start.1) | async-done | bytes 65568 | tf_op jit(solution)/shard_map/all_to_all | solution.py:515
  43.4 0.0 copy-done.5
  43.4 0.0 copy-start.6
  43.4 0.0 copy-start.3
  43.4 4.8 %shard_map.141 = bf16[32,8,128]{2,1,0:T(8,128)(2,1)S(1)} custom-call(s32[4]{0:T(128)S(1)} %copy-done.5, f32[8,128]{1,0:T(8,128)S(1)} %get-tuple-element.36.sel, bf16[32,8,128]{2,1,0:T(8,128)(2,1)S(1)} %all-to-all-done.1.arrived, bf16[16,512]{1,0:T(8,128)(2,1)S(1)} %get-tuple-element.38.fresh, bf16[4,256,2,512]{3,2,1,0:T(2,128)(2,1)S(1)} %get-tuple-element.39.start, ...), custom_call_target="tpu_custom_call" | custom-call | tf_op jit(solution)/shard_map/pallas_call | solution.py:375
  48.2 13.2 %all_to_all.30.returned = bf16[32,8,128]{2,1,0:T(8,128)(2,1)S(1)} all-to-all(bf16[32,8,128]{2,1,0:T(8,128)(2,1)S(1)} %shard_map.141), channel_id=1, replica_groups=mesh['req'=32,'rep'=4] {'req'}, dimensions={0} | all-to-all | bytes 131072 | tf_op jit(solution)/shard_map/all_to_all | solution.py:515
  61.4 0.0 copy-done.6
  61.4 2.9 %collective-permute-start.2 = (bf16[2,128,512]{2,1,0:T(8,128)(2,1)S(1)}, bf16[2,128,512]{2,1,0:T(8,128)(2,1)S(1)}, u32[]{:S(2)}, u32[]{:S(2)}) collective-permute-start(bf16[2,128,512]{2,1,0:T(8,128)(2,1)S(1)} %copy-done.6), channel_id=1, source_target_pairs={{0,1},{1,0},{2,3},{3,2},{4,5},{5,4},{6,7},{7,6},{8,9},{9,8},{10,11... | collective-permute-start | bytes 786440 | tf_op jit(solution)/shard_map/ppermute | solution.py:528
  64.3 0.0 collective-permute-start.1
  64.3 0.0 copy-done.3
  64.3 0.5 shard_map.142.part
  64.8 0.7 collective-permute-done.1.returned
  65.5 0.0 collective-permute-done.2.weight
  65.5 0.5 shard_map.143
  66.1 0.0 copy-start
  66.1 0.0 copy-start.1
  66.1 0.0 copy-start.4
  66.1 16.6 %all_to_all.31 = bf16[64,8,512]{2,1,0:T(8,128)(2,1)S(1)} all-to-all(bf16[64,8,512]{2,1,0:T(8,128)(2,1)S(1)} %bitcast.30), channel_id=1, replica_groups={{0,2,4,6,8,10,12,14,16,18,20,22,24,26,28,30,32,34,36,38,40,42,44,46,48,..., dimensions={0} | all-to-all | bytes 1048576 | tf_op jit(solution)/shard_map/all_to_all | solution.py:518
  82.8 0.1 convert_reduce_fusion.1
  82.8 0.1 multiply_reduce_fusion.1
  83.0 0.0 copy-start.2
  83.0 15.6 %all_to_all.32 = bf16[64,8,512]{2,1,0:T(8,128)(2,1)S(1)} all-to-all(bf16[64,8,512]{2,1,0:T(8,128)(2,1)S(1)} %broadcast_in_dim.29), channel_id=1, replica_groups={{0,2,4,6,8,10,12,14,16,18,20,22,24,26,28,30,32,34,36,38,40,42,44,46,48,..., dimensions={0} | all-to-all | bytes 1048576 | tf_op jit(solution)/shard_map/all_to_all | solution.py:518
  98.6 3.2 %collective-permute-start.3 = (bf16[64,8,512]{2,1,0:T(8,128)(2,1)S(1)}, bf16[64,8,512]{2,1,0:T(8,128)(2,1)S(1)}, u32[]{:S(2)}, u32[]{:S(2)}) collective-permute-start(bf16[64,8,512]{2,1,0:T(8,128)(2,1)S(1)} %all_to_all.32), channel_id=1, source_target_pairs={{0,1},{1,0},{2,3},{3,2},{4,5},{5,4},{6,7},{7,6},{8,9},{9,8},{10,11... | collective-permute-start | bytes 1572872 | tf_op jit(solution)/shard_map/ppermute | solution.py:528
  101.8 0.0 copy-done
  101.8 0.0 copy-done.1
  101.8 0.0 copy-done.4
  101.8 0.7 shard_map.144
  102.6 0.8 collective-permute-done.3
  103.4 0.0 copy-done.2
  103.4 1.1 shard_map.145
  104.5 0.5 collective-permute-start.4
  105.0 0.4 shard_map.146
  105.4 1.1 collective-permute-done.4
  106.5 0.2 add_convert_fusion
  106.7 16.4 %all_to_all.33 = bf16[64,8,512]{2,1,0:T(8,128)(2,1)S(1)} all-to-all(bf16[64,8,512]{2,1,0:T(8,128)(2,1)S(1)} %bitcast.32), channel_id=1, replica_groups={{0,2,4,6,8,10,12,14,16,18,20,22,24,26,28,30,32,34,36,38,40,42,44,46,48,..., dimensions={0} | all-to-all | bytes 1048576 | tf_op jit(solution)/shard_map/all_to_all | solution.py:518
  123.1 0.1 convert_reduce_fusion
  123.2 0.1 multiply_reduce_fusion
  123.3 2.2 %collective-permute-start.5 = (bf16[8,512]{1,0:T(8,128)(2,1)S(1)}, bf16[8,512]{1,0:T(8,128)(2,1)S(1)}, u32[]{:S(2)}, u32[]{:S(2)}) collective-permute-start(bf16[8,512]{1,0:T(8,128)(2,1)S(1)} %add_convert_fusion.1.refs_0_), channel_id=1, source_target_pairs={{0,1},{1,0},{2,3},{3,2},{4,5},{5,4},{6,7},{7,6},{8,9},{9,8},{10,11... | collective-permute-start | bytes 24584 | tf_op jit(solution)/shard_map/ppermute | solution.py:607
  125.4 0.4 collective-permute-start.6
  125.8 1.3 %collective-permute-start.7 = (bf16[8,512]{1,0:T(8,128)(2,1)S(1)}, bf16[8,512]{1,0:T(8,128)(2,1)S(1)}, u32[]{:S(2)}, u32[]{:S(2)}) collective-permute-start(bf16[8,512]{1,0:T(8,128)(2,1)S(1)} %add_convert_fusion.1.refs_0_), channel_id=1, source_target_pairs={{0,3},{1,2},{2,1},{3,0},{4,7},{5,6},{6,5},{7,4},{8,11},{9,10},{10,... | collective-permute-start | bytes 24584 | tf_op jit(solution)/shard_map/ppermute | solution.py:607
  127.1 0.0 collective-permute-done.5.refs_1_
  127.1 0.8 collective-permute-done.6.refs_2_
  127.9 1.0 collective-permute-done.7.refs_3_
  128.9 0.6 shard_map.147
  (5 shorter events, 0.1 us)
Async XLA Ops:
  1.8 24.2 %all-to-all-start = ((bf16[32,8,1152]{2,1,0:T(8,128)(2,1)}), bf16[32,8,1152]{2,1,0:T(8,128)(2,1)S(1)}, u32[]{:S(2)}, u32[]{:S(2)}) async-start(bf16[32,8,1152]{2,1,0:T(8,128)(2,1)} %shard_map.136), calls=%async_computation | async-start | bytes 1179648 | tf_op jit(solution)/shard_map/all_to_all | solution.py:515
  26.0 3.8 %collective-permute-start = (bf16[32,8,1152]{2,1,0:T(8,128)(2,1)S(1)}, bf16[32,8,1152]{2,1,0:T(8,128)(2,1)S(1)}, u32[]{:S(2)}, u32[]{:S(2)}) collective-permute-start(bf16[32,8,1152]{2,1,0:T(8,128)(2,1)S(1)} %all-to-all-done.near), channel_id=1, source_target_pairs={{0,1},{1,0},{2,3},{3,2},{4,5},{5,4},{6,7},{7,6},{8,9},{9,8},{10,11... | collective-permute-start | bytes 1769480 | tf_op jit(solution)/shard_map/ppermute | solution.py:528
  30.9 12.5 %all-to-all-start.1 = ((bf16[32,8,128]{2,1,0:T(8,128)(2,1)}), bf16[32,8,128]{2,1,0:T(8,128)(2,1)S(1)}, u32[]{:S(2)}, u32[]{:S(2)}) async-start(bf16[32,8,128]{2,1,0:T(8,128)(2,1)} %get-tuple-element.37), calls=%async_computation.1 | async-start | bytes 131072 | tf_op jit(solution)/shard_map/all_to_all | solution.py:515
  34.8 8.6 %copy-start.5 = (s32[4]{0:T(128)S(1)}, s32[4]{0:T(128)}, u32[]{:S(2)}) copy-start(s32[4]{0:T(128)} %lens.1) | copy-start | bytes 52
  43.4 18.0 %copy-start.6 = (bf16[2,128,512]{2,1,0:T(8,128)(2,1)S(1)}, bf16[2,128,512]{2,1,0:T(8,128)(2,1)}, u32[]{:S(2)}) copy-start(bf16[2,128,512]{2,1,0:T(8,128)(2,1)} %get-tuple-element.43) | copy-start | bytes 786436
  43.4 20.9 %copy-start.3 = (bf16[1,128,2048]{2,1,0:T(8,128)(2,1)S(1)}, bf16[1,128,2048]{2,1,0:T(8,128)(2,1)}, u32[]{:S(2)}) copy-start(bf16[1,128,2048]{2,1,0:T(8,128)(2,1)} %weight.4) | copy-start | bytes 1572868
  61.4 4.1 %collective-permute-start.2 = (bf16[2,128,512]{2,1,0:T(8,128)(2,1)S(1)}, bf16[2,128,512]{2,1,0:T(8,128)(2,1)S(1)}, u32[]{:S(2)}, u32[]{:S(2)}) collective-permute-start(bf16[2,128,512]{2,1,0:T(8,128)(2,1)S(1)} %copy-done.6), channel_id=1, source_target_pairs={{0,1},{1,0},{2,3},{3,2},{4,5},{5,4},{6,7},{7,6},{8,9},{9,8},{10,11... | collective-permute-start | bytes 786440 | tf_op jit(solution)/shard_map/ppermute | solution.py:528
  64.3 1.3 collective-permute-start.1
  66.1 35.8 %copy-start = (bf16[1,2048,352]{1,2,0:T(8,128)(2,1)S(1)}, bf16[1,2048,352]{1,2,0:T(8,128)(2,1)}, u32[]{:S(2)}) copy-start(bf16[1,2048,352]{1,2,0:T(8,128)(2,1)} %param.19) | copy-start | bytes 4325380
  66.1 35.8 %copy-start.1 = (bf16[1,2048,352]{1,2,0:T(8,128)(2,1)S(1)}, bf16[1,2048,352]{1,2,0:T(8,128)(2,1)}, u32[]{:S(2)}) copy-start(bf16[1,2048,352]{1,2,0:T(8,128)(2,1)} %param.20) | copy-start | bytes 4325380
  66.1 35.7 %copy-start.4 = (f32[2,2048]{1,0:T(2,128)S(1)}, f32[2,2048]{1,0:T(2,128)}, u32[]{:S(2)}) copy-start(f32[2,2048]{1,0:T(2,128)} %gains.3) | copy-start | bytes 49156
  83.0 20.4 %copy-start.2 = (bf16[1,352,2048]{2,1,0:T(8,128)(2,1)S(1)}, bf16[1,352,2048]{2,1,0:T(8,128)(2,1)}, u32[]{:S(2)}) copy-start(bf16[1,352,2048]{2,1,0:T(8,128)(2,1)} %weight.5) | copy-start | bytes 4325380
  98.6 4.8 %collective-permute-start.3 = (bf16[64,8,512]{2,1,0:T(8,128)(2,1)S(1)}, bf16[64,8,512]{2,1,0:T(8,128)(2,1)S(1)}, u32[]{:S(2)}, u32[]{:S(2)}) collective-permute-start(bf16[64,8,512]{2,1,0:T(8,128)(2,1)S(1)} %all_to_all.32), channel_id=1, source_target_pairs={{0,1},{1,0},{2,3},{3,2},{4,5},{5,4},{6,7},{7,6},{8,9},{9,8},{10,11... | collective-permute-start | bytes 1572872 | tf_op jit(solution)/shard_map/ppermute | solution.py:528
  104.5 2.0 %collective-permute-start.4 = (bf16[32,2,8,512]{3,2,1,0:T(8,128)(2,1)S(1)}, bf16[32,2,8,512]{3,2,1,0:T(8,128)(2,1)S(1)}, u32[]{:S(2)}, u32[]{:S(2)}) collective-permute-start(bf16[32,2,8,512]{3,2,1,0:T(8,128)(2,1)S(1)} %get-tuple-element.49), channel_id=1, source_target_pairs={{0,1},{1,0},{2,3},{3,2},{4,5},{5,4},{6,7},{7,6},{8,9},{9,8},{10,11... | collective-permute-start | bytes 1572872 | tf_op jit(solution)/shard_map/ppermute | solution.py:528
  123.3 3.9 %collective-permute-start.5 = (bf16[8,512]{1,0:T(8,128)(2,1)S(1)}, bf16[8,512]{1,0:T(8,128)(2,1)S(1)}, u32[]{:S(2)}, u32[]{:S(2)}) collective-permute-start(bf16[8,512]{1,0:T(8,128)(2,1)S(1)} %add_convert_fusion.1.refs_0_), channel_id=1, source_target_pairs={{0,1},{1,0},{2,3},{3,2},{4,5},{5,4},{6,7},{7,6},{8,9},{9,8},{10,11... | collective-permute-start | bytes 24584 | tf_op jit(solution)/shard_map/ppermute | solution.py:607
  125.4 2.5 %collective-permute-start.6 = (bf16[8,512]{1,0:T(8,128)(2,1)S(1)}, bf16[8,512]{1,0:T(8,128)(2,1)S(1)}, u32[]{:S(2)}, u32[]{:S(2)}) collective-permute-start(bf16[8,512]{1,0:T(8,128)(2,1)S(1)} %add_convert_fusion.1.refs_0_), channel_id=1, source_target_pairs={{0,2},{1,3},{2,0},{3,1},{4,6},{5,7},{6,4},{7,5},{8,10},{9,11},{10,... | collective-permute-start | bytes 24584 | tf_op jit(solution)/shard_map/ppermute | solution.py:607
  125.8 3.1 %collective-permute-start.7 = (bf16[8,512]{1,0:T(8,128)(2,1)S(1)}, bf16[8,512]{1,0:T(8,128)(2,1)S(1)}, u32[]{:S(2)}, u32[]{:S(2)}) collective-permute-start(bf16[8,512]{1,0:T(8,128)(2,1)S(1)} %add_convert_fusion.1.refs_0_), channel_id=1, source_target_pairs={{0,3},{1,2},{2,1},{3,0},{4,7},{5,6},{6,5},{7,4},{8,11},{9,10},{10,... | collective-permute-start | bytes 24584 | tf_op jit(solution)/shard_map/ppermute | solution.py:607

commit v7 on v6

--- a/solution.py
+++ b/solution.py
@@ -11,7 +11,7 @@
 HD = 128
 EXPERTS = 8
 HEAD = 256
-MIDDLE = 128
+MIDDLE = 256
 EPSILON = 1e-06
 MASKED = -1e30
 F32 = jnp.float32
@@ -248,10 +248,14 @@
 def attention_kernel(
     lens, sel, arrived, fresh, start, far, out, middle, cache, qs, os, sc, ef, sems, one
 ):
-    fetch = pltpu.make_async_copy(far.at[:, pl.ds(0, MIDDLE)], middle, one)
-    fetch.start()
     count, rest, _, wide = cache.shape
     requests = range(count)
+
+    def middle_of(j):
+        return pltpu.make_async_copy(far.at[j, pl.ds(0, MIDDLE)], middle.at[j], one.at[j])
+
+    for j in requests:
+        middle_of(j).start()
 
     def copy_of(j):
         return pltpu.make_async_copy(far.at[j, pl.ds(MIDDLE, rest)], cache.at[j], sems.at[j])
@@ -318,7 +322,8 @@
         queries.append(q)
         extras.append(jnp.where(live, dot_rows(q, extra) * inv_scale, MASKED))
         firsts.append(masked_scores(q, j, 0))
-    fetch.wait()
+    for j in requests:
+        middle_of(j).wait()
     for j in requests:
         seconds.append(masked_scores(queries[j], j, 1))
         top = jnp.maximum(highest(extras[j]), highest(firsts[j]))
@@ -384,7 +389,7 @@
             pltpu.VMEM((mine, 2 * pairs, 2 * rest), F32),
             pltpu.VMEM((HD, wide), BF16),
             pltpu.SemaphoreType.DMA((mine,)),
-            pltpu.SemaphoreType.DMA,
+            pltpu.SemaphoreType.DMA((mine,)),
         ],
         16,
     )(lens, sel, arrived, fresh, in_vmem(start), in_hbm(cache))

time: 130 us -> 130 us (level)
  Pallas kernels: 19.9 us -> 22.2 us
  blocking collectives: 61.9 us -> 60.3 us
    all_to_all x1, blocking collectives: 13.2 us -> 11.6 us  [spread_req(): return lax.all_to_all(value, 'req', split_axis=0, concat_axis=0, tiled=True)]
  transfers between devices with their start and end apart: 10 -> 10, of which waited for: 8 -> 8; matrix products, arithmetic and copies ran while one was open for 2% -> 2% of each run, Pallas kernels for 8% -> 9%
where the time goes in v7:
time: 130 us; the launch traced here: 129 us
  blocking collectives  60.3 us (46%)
  starting transfers between devices  27.5 us (21%)
  Pallas kernels  22.2 us (17%)
  waiting for transfers between devices  15.4 us (12%)
  local copies, waits for them, and re-layouts  2.08 us (2%)
    all_to_all x3, blocking collectives, spread_wide(): lax.all_to_all(value, ('req', 'rep'), split_axis=0, concat_axis=0, tiled=...  48.7 us
    all_to_all x2, starting transfers between devices, spread_req(): return lax.all_to_all(value, 'req', split_axis=0, concat_axis=0, tiled=True)  15 us
    all_to_all x1, blocking collectives, spread_req(): return lax.all_to_all(value, 'req', split_axis=0, concat_axis=0, tiled=True)  11.6 us
    all_to_all x2, waiting for transfers between devices, spread_req(): return lax.all_to_all(value, 'req', split_axis=0, concat_axis=0, tiled=True)  10.8 us
    ppermute x5, starting transfers between devices, other_core(): return lax.ppermute(value, 'rep', swap)  8.59 us
    pallas_call x1, Pallas kernels, attention_call(): call(attention_kernel, shape_of(arrived.shape), [SM, VM, VM, VM, VM, FAR]...  5.98 us
    pallas_call x1, Pallas kernels, pages_call(): call(page_kernel, [pltpu.VMEM((mine, HEAD) + pool.shape[2:], BF16), pltpu...  5.34 us
    ppermute x3, starting transfers between devices, shards(): lax.ppermute(piece, 'rep', [(p, p ^ m) for p in range(rep_count)])  3.88 us
  transfers between devices with their start and end apart: 10, of which 8 were waited for; matrix products, arithmetic and copies ran while one was open for 2% of the time, Pallas kernels for 9%

profile of v7, /device:TPU:1, one launch (start us, length us, event | category | flops | bytes accessed | tf_op | source)
XLA Modules:
  0.0 128.9 jit_solution(16864228468658969755)
XLA Ops:
  0.0 1.8 %shard_map.136 = bf16[32,8,1152]{2,1,0:T(8,128)(2,1)} custom-call(s32[4]{0:T(128)} %slots_far.1, s32[2,2,2,4]{3,2,1,0:T(2,128)} %bitcast.34, bf16[4,2,2048]{2,1,0:T(2,128)(2,1)} %tokens_far.1, f32[2,2048]{1,0:T(2,128)} %gains.3), custom_call_target="tpu_custom_call" | custom-call | tf_op jit(solution)/shard_map/pallas_call | solution.py:545
  1.8 11.2 %all-to-all-start = ((bf16[32,8,1152]{2,1,0:T(8,128)(2,1)}), bf16[32,8,1152]{2,1,0:T(8,128)(2,1)S(1)}, u32[]{:S(2)}, u32[]{:S(2)}) async-start(bf16[32,8,1152]{2,1,0:T(8,128)(2,1)} %shard_map.136), calls=%async_computation | async-start | bytes 1179648 | tf_op jit(solution)/shard_map/all_to_all | solution.py:520
  13.0 0.8 reshape.28
  13.8 0.7 convert_bitcast_fusion
  14.5 0.1 copy.24
  14.6 0.1 reshape.33
  14.7 0.8 copy.23
  15.5 0.1 eq.15
  15.5 0.1 select_reduce_fusion
  15.6 0.1 copy.25
  15.7 0.1 copy.26
  15.8 5.3 %shard_map.137 = (bf16[4,256,2,512]{3,2,1,0:T(2,128)(2,1)S(1)}, bf16[4,768,2,512]{3,2,1,0:T(2,128)(2,1)}, bf16[2,128,512]{2,1,0:T(8,128)(2,1)}) custom-call(s32[4,64]{1,0:T(4,128)} %table_far.1, s32[4]{0:T(128)} %lens.1, bf16[256,16,2,512]{3,2,1,0:T(2,128)(2,1)} %pool.1, bf16[1,128,2048]{2,1,0:T(8,128)(2,1)} %weight.4), custom_call_target="tpu_custom_call" | custom-call | tf_op jit(solution)/shard_map/pallas_call | solution.py:226
  21.1 4.8 %all-to-all-done.near = bf16[32,8,1152]{2,1,0:T(8,128)(2,1)S(1)} async-done(((bf16[32,8,1152]{2,1,0:T(8,128)(2,1)}), bf16[32,8,1152]{2,1,0:T(8,128)(2,1)S(1)}, u32[]{:S(2)}, u32[]{:S(2)}) %all-to-all-start) | async-done | bytes 589856 | tf_op jit(solution)/shard_map/all_to_all | solution.py:520
  26.0 2.2 %collective-permute-start = (bf16[32,8,1152]{2,1,0:T(8,128)(2,1)S(1)}, bf16[32,8,1152]{2,1,0:T(8,128)(2,1)S(1)}, u32[]{:S(2)}, u32[]{:S(2)}) collective-permute-start(bf16[32,8,1152]{2,1,0:T(8,128)(2,1)S(1)} %all-to-all-done.near), channel_id=1, source_target_pairs={{0,1},{1,0},{2,3},{3,2},{4,5},{5,4},{6,7},{7,6},{8,9},{9,8},{10,11... | collective-permute-start | bytes 1769480 | tf_op jit(solution)/shard_map/ppermute | solution.py:533
  28.2 1.3 %shard_map.138 = (bf16[1,2048,128]{2,1,0:T(8,128)(2,1)S(1)}, f32[256,128]{1,0:T(8,128)S(1)}) custom-call(bf16[32,8,1152]{2,1,0:T(8,128)(2,1)S(1)} %all-to-all-done.near, bf16[1,2048,128]{2,1,0:T(8,128)(2,1)} %wq_far.1), custom_call_target="tpu_custom_call" | custom-call | tf_op jit(solution)/shard_map/pallas_call | solution.py:563
  29.5 0.3 collective-permute-done.far
  29.8 1.1 shard_map.139
  30.9 3.8 %all-to-all-start.1 = ((bf16[32,8,128]{2,1,0:T(8,128)(2,1)}), bf16[32,8,128]{2,1,0:T(8,128)(2,1)S(1)}, u32[]{:S(2)}, u32[]{:S(2)}) async-start(bf16[32,8,128]{2,1,0:T(8,128)(2,1)} %get-tuple-element.37), calls=%async_computation.1 | async-start | bytes 131072 | tf_op jit(solution)/shard_map/all_to_all | solution.py:520
  34.8 0.0 copy-start.5
  34.8 2.7 %shard_map.140 = (f32[8,128]{1,0:T(8,128)S(1)}, bf16[16,512]{1,0:T(8,128)(2,1)S(1)}) custom-call(bf16[32,8,1152]{2,1,0:T(8,128)(2,1)S(1)} %all-to-all-done.near, bf16[32,8,1152]{2,1,0:T(8,128)(2,1)S(1)} %collective-permute-done.far, bf16[2048,2,512]{2,1,0:T(2,128)(2,1)} %wkv_far.1), custom_call_target="tpu_custom_call" | custom-call | tf_op jit(solution)/shard_map/pallas_call | solution.py:573
  37.5 6.0 %all-to-all-done.1.arrived = bf16[32,8,128]{2,1,0:T(8,128)(2,1)S(1)} async-done(((bf16[32,8,128]{2,1,0:T(8,128)(2,1)}), bf16[32,8,128]{2,1,0:T(8,128)(2,1)S(1)}, u32[]{:S(2)}, u32[]{:S(2)}) %all-to-all-start.1) | async-done | bytes 65568 | tf_op jit(solution)/shard_map/all_to_all | solution.py:520
  43.4 0.0 copy-done.5
  43.4 0.0 copy-start.6
  43.4 0.0 copy-start.3
  43.4 6.0 %shard_map.141 = bf16[32,8,128]{2,1,0:T(8,128)(2,1)S(1)} custom-call(s32[4]{0:T(128)S(1)} %copy-done.5, f32[8,128]{1,0:T(8,128)S(1)} %get-tuple-element.36.sel, bf16[32,8,128]{2,1,0:T(8,128)(2,1)S(1)} %all-to-all-done.1.arrived, bf16[16,512]{1,0:T(8,128)(2,1)S(1)} %get-tuple-element.38.fresh, bf16[4,256,2,512]{3,2,1,0:T(2,128)(2,1)S(1)} %get-tuple-element.39.start, ...), custom_call_target="tpu_custom_call" | custom-call | tf_op jit(solution)/shard_map/pallas_call | solution.py:380
  49.4 11.6 %all_to_all.30.returned = bf16[32,8,128]{2,1,0:T(8,128)(2,1)S(1)} all-to-all(bf16[32,8,128]{2,1,0:T(8,128)(2,1)S(1)} %shard_map.141), channel_id=1, replica_groups=mesh['req'=32,'rep'=4] {'req'}, dimensions={0} | all-to-all | bytes 131072 | tf_op jit(solution)/shard_map/all_to_all | solution.py:520
  61.0 0.0 copy-done.6
  61.0 2.7 %collective-permute-start.2 = (bf16[2,128,512]{2,1,0:T(8,128)(2,1)S(1)}, bf16[2,128,512]{2,1,0:T(8,128)(2,1)S(1)}, u32[]{:S(2)}, u32[]{:S(2)}) collective-permute-start(bf16[2,128,512]{2,1,0:T(8,128)(2,1)S(1)} %copy-done.6), channel_id=1, source_target_pairs={{0,1},{1,0},{2,3},{3,2},{4,5},{5,4},{6,7},{7,6},{8,9},{9,8},{10,11... | collective-permute-start | bytes 786440 | tf_op jit(solution)/shard_map/ppermute | solution.py:533
  63.7 0.0 collective-permute-start.1
  63.7 0.0 copy-done.3
  63.7 0.5 shard_map.142.part
  64.2 0.7 collective-permute-done.1.returned
  64.9 0.0 collective-permute-done.2.weight
  65.0 0.5 shard_map.143
  65.5 0.0 copy-start
  65.5 0.0 copy-start.1
  65.5 0.0 copy-start.4
  65.5 16.6 %all_to_all.31 = bf16[64,8,512]{2,1,0:T(8,128)(2,1)S(1)} all-to-all(bf16[64,8,512]{2,1,0:T(8,128)(2,1)S(1)} %bitcast.30), channel_id=1, replica_groups={{0,2,4,6,8,10,12,14,16,18,20,22,24,26,28,30,32,34,36,38,40,42,44,46,48,..., dimensions={0} | all-to-all | bytes 1048576 | tf_op jit(solution)/shard_map/all_to_all | solution.py:523
  82.2 0.1 convert_reduce_fusion.1
  82.2 0.1 multiply_reduce_fusion.1
  82.4 0.0 copy-start.2
  82.4 15.6 %all_to_all.32 = bf16[64,8,512]{2,1,0:T(8,128)(2,1)S(1)} all-to-all(bf16[64,8,512]{2,1,0:T(8,128)(2,1)S(1)} %broadcast_in_dim.29), channel_id=1, replica_groups={{0,2,4,6,8,10,12,14,16,18,20,22,24,26,28,30,32,34,36,38,40,42,44,46,48,..., dimensions={0} | all-to-all | bytes 1048576 | tf_op jit(solution)/shard_map/all_to_all | solution.py:523
  98.0 3.2 %collective-permute-start.3 = (bf16[64,8,512]{2,1,0:T(8,128)(2,1)S(1)}, bf16[64,8,512]{2,1,0:T(8,128)(2,1)S(1)}, u32[]{:S(2)}, u32[]{:S(2)}) collective-permute-start(bf16[64,8,512]{2,1,0:T(8,128)(2,1)S(1)} %all_to_all.32), channel_id=1, source_target_pairs={{0,1},{1,0},{2,3},{3,2},{4,5},{5,4},{6,7},{7,6},{8,9},{9,8},{10,11... | collective-permute-start | bytes 1572872 | tf_op jit(solution)/shard_map/ppermute | solution.py:533
  101.2 0.0 copy-done
  101.3 0.0 copy-done.1
  101.3 0.0 copy-done.4
  101.3 0.7 shard_map.144
  102.0 0.8 collective-permute-done.3
  102.8 0.0 copy-done.2
  102.8 1.1 shard_map.145
  103.9 0.5 collective-permute-start.4
  104.4 0.4 shard_map.146
  104.8 1.1 collective-permute-done.4
  105.9 0.2 add_convert_fusion
  106.1 16.4 %all_to_all.33 = bf16[64,8,512]{2,1,0:T(8,128)(2,1)S(1)} all-to-all(bf16[64,8,512]{2,1,0:T(8,128)(2,1)S(1)} %bitcast.32), channel_id=1, replica_groups={{0,2,4,6,8,10,12,14,16,18,20,22,24,26,28,30,32,34,36,38,40,42,44,46,48,..., dimensions={0} | all-to-all | bytes 1048576 | tf_op jit(solution)/shard_map/all_to_all | solution.py:523
  122.5 0.1 convert_reduce_fusion
  122.6 0.1 multiply_reduce_fusion
  122.7 2.2 %collective-permute-start.5 = (bf16[8,512]{1,0:T(8,128)(2,1)S(1)}, bf16[8,512]{1,0:T(8,128)(2,1)S(1)}, u32[]{:S(2)}, u32[]{:S(2)}) collective-permute-start(bf16[8,512]{1,0:T(8,128)(2,1)S(1)} %add_convert_fusion.1.refs_0_), channel_id=1, source_target_pairs={{0,1},{1,0},{2,3},{3,2},{4,5},{5,4},{6,7},{7,6},{8,9},{9,8},{10,11... | collective-permute-start | bytes 24584 | tf_op jit(solution)/shard_map/ppermute | solution.py:612
  124.8 0.4 collective-permute-start.6
  125.2 1.3 %collective-permute-start.7 = (bf16[8,512]{1,0:T(8,128)(2,1)S(1)}, bf16[8,512]{1,0:T(8,128)(2,1)S(1)}, u32[]{:S(2)}, u32[]{:S(2)}) collective-permute-start(bf16[8,512]{1,0:T(8,128)(2,1)S(1)} %add_convert_fusion.1.refs_0_), channel_id=1, source_target_pairs={{0,3},{1,2},{2,1},{3,0},{4,7},{5,6},{6,5},{7,4},{8,11},{9,10},{10,... | collective-permute-start | bytes 24584 | tf_op jit(solution)/shard_map/ppermute | solution.py:612
  126.6 0.0 collective-permute-done.5.refs_1_
  126.6 0.8 collective-permute-done.6.refs_2_
  127.3 1.0 collective-permute-done.7.refs_3_
  128.3 0.6 shard_map.147
  (5 shorter events, 0.1 us)
Async XLA Ops:
  1.8 24.2 %all-to-all-start = ((bf16[32,8,1152]{2,1,0:T(8,128)(2,1)}), bf16[32,8,1152]{2,1,0:T(8,128)(2,1)S(1)}, u32[]{:S(2)}, u32[]{:S(2)}) async-start(bf16[32,8,1152]{2,1,0:T(8,128)(2,1)} %shard_map.136), calls=%async_computation | async-start | bytes 1179648 | tf_op jit(solution)/shard_map/all_to_all | solution.py:520
  26.0 3.8 %collective-permute-start = (bf16[32,8,1152]{2,1,0:T(8,128)(2,1)S(1)}, bf16[32,8,1152]{2,1,0:T(8,128)(2,1)S(1)}, u32[]{:S(2)}, u32[]{:S(2)}) collective-permute-start(bf16[32,8,1152]{2,1,0:T(8,128)(2,1)S(1)} %all-to-all-done.near), channel_id=1, source_target_pairs={{0,1},{1,0},{2,3},{3,2},{4,5},{5,4},{6,7},{7,6},{8,9},{9,8},{10,11... | collective-permute-start | bytes 1769480 | tf_op jit(solution)/shard_map/ppermute | solution.py:533
  30.9 12.5 %all-to-all-start.1 = ((bf16[32,8,128]{2,1,0:T(8,128)(2,1)}), bf16[32,8,128]{2,1,0:T(8,128)(2,1)S(1)}, u32[]{:S(2)}, u32[]{:S(2)}) async-start(bf16[32,8,128]{2,1,0:T(8,128)(2,1)} %get-tuple-element.37), calls=%async_computation.1 | async-start | bytes 131072 | tf_op jit(solution)/shard_map/all_to_all | solution.py:520
  34.8 8.6 %copy-start.5 = (s32[4]{0:T(128)S(1)}, s32[4]{0:T(128)}, u32[]{:S(2)}) copy-start(s32[4]{0:T(128)} %lens.1) | copy-start | bytes 52
  43.4 17.6 %copy-start.6 = (bf16[2,128,512]{2,1,0:T(8,128)(2,1)S(1)}, bf16[2,128,512]{2,1,0:T(8,128)(2,1)}, u32[]{:S(2)}) copy-start(bf16[2,128,512]{2,1,0:T(8,128)(2,1)} %get-tuple-element.43) | copy-start | bytes 786436
  43.4 20.3 %copy-start.3 = (bf16[1,128,2048]{2,1,0:T(8,128)(2,1)S(1)}, bf16[1,128,2048]{2,1,0:T(8,128)(2,1)}, u32[]{:S(2)}) copy-start(bf16[1,128,2048]{2,1,0:T(8,128)(2,1)} %weight.4) | copy-start | bytes 1572868
  61.0 3.9 %collective-permute-start.2 = (bf16[2,128,512]{2,1,0:T(8,128)(2,1)S(1)}, bf16[2,128,512]{2,1,0:T(8,128)(2,1)S(1)}, u32[]{:S(2)}, u32[]{:S(2)}) collective-permute-start(bf16[2,128,512]{2,1,0:T(8,128)(2,1)S(1)} %copy-done.6), channel_id=1, source_target_pairs={{0,1},{1,0},{2,3},{3,2},{4,5},{5,4},{6,7},{7,6},{8,9},{9,8},{10,11... | collective-permute-start | bytes 786440 | tf_op jit(solution)/shard_map/ppermute | solution.py:533
  63.7 1.3 collective-permute-start.1
  65.5 35.8 %copy-start = (bf16[1,2048,352]{1,2,0:T(8,128)(2,1)S(1)}, bf16[1,2048,352]{1,2,0:T(8,128)(2,1)}, u32[]{:S(2)}) copy-start(bf16[1,2048,352]{1,2,0:T(8,128)(2,1)} %param.19) | copy-start | bytes 4325380
  65.5 35.8 %copy-start.1 = (bf16[1,2048,352]{1,2,0:T(8,128)(2,1)S(1)}, bf16[1,2048,352]{1,2,0:T(8,128)(2,1)}, u32[]{:S(2)}) copy-start(bf16[1,2048,352]{1,2,0:T(8,128)(2,1)} %param.20) | copy-start | bytes 4325380
  65.5 35.7 %copy-start.4 = (f32[2,2048]{1,0:T(2,128)S(1)}, f32[2,2048]{1,0:T(2,128)}, u32[]{:S(2)}) copy-start(f32[2,2048]{1,0:T(2,128)} %gains.3) | copy-start | bytes 49156
  82.4 20.4 %copy-start.2 = (bf16[1,352,2048]{2,1,0:T(8,128)(2,1)S(1)}, bf16[1,352,2048]{2,1,0:T(8,128)(2,1)}, u32[]{:S(2)}) copy-start(bf16[1,352,2048]{2,1,0:T(8,128)(2,1)} %weight.5) | copy-start | bytes 4325380
  98.0 4.8 %collective-permute-start.3 = (bf16[64,8,512]{2,1,0:T(8,128)(2,1)S(1)}, bf16[64,8,512]{2,1,0:T(8,128)(2,1)S(1)}, u32[]{:S(2)}, u32[]{:S(2)}) collective-permute-start(bf16[64,8,512]{2,1,0:T(8,128)(2,1)S(1)} %all_to_all.32), channel_id=1, source_target_pairs={{0,1},{1,0},{2,3},{3,2},{4,5},{5,4},{6,7},{7,6},{8,9},{9,8},{10,11... | collective-permute-start | bytes 1572872 | tf_op jit(solution)/shard_map/ppermute | solution.py:533
  103.9 2.0 %collective-permute-start.4 = (bf16[32,2,8,512]{3,2,1,0:T(8,128)(2,1)S(1)}, bf16[32,2,8,512]{3,2,1,0:T(8,128)(2,1)S(1)}, u32[]{:S(2)}, u32[]{:S(2)}) collective-permute-start(bf16[32,2,8,512]{3,2,1,0:T(8,128)(2,1)S(1)} %get-tuple-element.49), channel_id=1, source_target_pairs={{0,1},{1,0},{2,3},{3,2},{4,5},{5,4},{6,7},{7,6},{8,9},{9,8},{10,11... | collective-permute-start | bytes 1572872 | tf_op jit(solution)/shard_map/ppermute | solution.py:533
  122.7 3.9 %collective-permute-start.5 = (bf16[8,512]{1,0:T(8,128)(2,1)S(1)}, bf16[8,512]{1,0:T(8,128)(2,1)S(1)}, u32[]{:S(2)}, u32[]{:S(2)}) collective-permute-start(bf16[8,512]{1,0:T(8,128)(2,1)S(1)} %add_convert_fusion.1.refs_0_), channel_id=1, source_target_pairs={{0,1},{1,0},{2,3},{3,2},{4,5},{5,4},{6,7},{7,6},{8,9},{9,8},{10,11... | collective-permute-start | bytes 24584 | tf_op jit(solution)/shard_map/ppermute | solution.py:612
  124.8 2.5 %collective-permute-start.6 = (bf16[8,512]{1,0:T(8,128)(2,1)S(1)}, bf16[8,512]{1,0:T(8,128)(2,1)S(1)}, u32[]{:S(2)}, u32[]{:S(2)}) collective-permute-start(bf16[8,512]{1,0:T(8,128)(2,1)S(1)} %add_convert_fusion.1.refs_0_), channel_id=1, source_target_pairs={{0,2},{1,3},{2,0},{3,1},{4,6},{5,7},{6,4},{7,5},{8,10},{9,11},{10,... | collective-permute-start | bytes 24584 | tf_op jit(solution)/shard_map/ppermute | solution.py:612
  125.2 3.1 %collective-permute-start.7 = (bf16[8,512]{1,0:T(8,128)(2,1)S(1)}, bf16[8,512]{1,0:T(8,128)(2,1)S(1)}, u32[]{:S(2)}, u32[]{:S(2)}) collective-permute-start(bf16[8,512]{1,0:T(8,128)(2,1)S(1)} %add_convert_fusion.1.refs_0_), channel_id=1, source_target_pairs={{0,3},{1,2},{2,1},{3,0},{4,7},{5,6},{6,5},{7,4},{8,11},{9,10},{10,... | collective-permute-start | bytes 24584 | tf_op jit(solution)/shard_map/ppermute | solution.py:612

commit v8 on v4

--- a/solution.py
+++ b/solution.py
@@ -112,12 +112,12 @@
     out[...] = dot(order_of(marks), q.astype(BF16)).astype(BF16).reshape(out.shape)
 
 
-def own_kernel(near, far, wkv, weight, sel, fresh, picked, sems):
-    halves, _, quarter = picked.shape
-    side = 1 - lax.axis_index("rep") % 2
+def own_kernel(near, far, wkv_far, sel, fresh, wkv, sems):
+    pieces = sems.shape[0]
+    size = wkv.shape[0] // pieces
     copies = [
-        pltpu.make_async_copy(weight.at[0, :, columns_of(z, side, quarter)], picked.at[z], sems.at[z])
-        for z in range(halves)
+        pltpu.make_async_copy(wkv_far.at[pl.ds(i * size, size)], wkv.at[pl.ds(i * size, size)], sems.at[i])
+        for i in range(pieces)
     ]
     for copy in copies:
         copy.start()
@@ -141,16 +141,26 @@
     even = lax.broadcasted_iota(jnp.int32, (rows, 2 * HD), 1) % 2 == 0
     total = jnp.zeros(fresh.shape, F32)
     for c in range(2 * spans):
+        if c * HD % size == 0:
+            copies[c * HD // size].wait()
         v = doubled[c * rows : (c + 1) * rows]
         v = jnp.concatenate([jnp.where(even, v, 0.0), jnp.where(even, 0.0, v)], axis=0)
         w = wkv[c * HD : (c + 1) * HD].reshape(2 * HD, fresh.shape[1])
         total = total + dot(v.astype(BF16), w)
     fresh[...] = total.astype(BF16)
-    for copy in copies:
-        copy.wait()
-
-
-def page_kernel(table_far, lens_far, pool, start, out, table, lens, staged, sems, back, small):
+
+
+def page_kernel(
+    table_far, lens_far, pool, weight, start, out, picked_far, table, lens, staged, picked, sems, back, small, pick
+):
+    halves, _, quarter = picked.shape
+    side = 1 - lax.axis_index("rep") % 2
+    picks = [
+        pltpu.make_async_copy(weight.at[0, :, columns_of(z, side, quarter)], picked.at[z], pick.at[z])
+        for z in range(halves)
+    ]
+    for copy in picks:
+        copy.start()
     first = pltpu.make_async_copy(table_far, table, small.at[0])
     second = pltpu.make_async_copy(lens_far, lens, small.at[1])
     first.start()
@@ -196,28 +206,40 @@
             write(j, c).wait()
 
     each(read)
+    for copy in picks:
+        copy.wait()
+    send = pltpu.make_async_copy(picked, picked_far, pick.at[halves])
+    send.start()
     each(forward)
     each(finish)
-
-
-def pages_call(table, lens, pool):
+    send.wait()
+
+
+def pages_call(table, lens, pool, weight, quarter):
     mine, pages = table.shape
     length = pages * pool.shape[1]
     tail = (mine, length - SPAN) + pool.shape[2:]
+    rows_shape = (weight.shape[2] // (2 * quarter), weight.shape[1], quarter)
     return call(
         page_kernel,
-        [pltpu.VMEM((mine, SPAN) + pool.shape[2:], BF16), pltpu.HBM(tail, BF16)],
-        [FAR] * 3,
+        [
+            pltpu.VMEM((mine, SPAN) + pool.shape[2:], BF16),
+            pltpu.HBM(tail, BF16),
+            pltpu.HBM(rows_shape, BF16),
+        ],
+        [FAR] * 4,
         [
             pltpu.SMEM(table.shape, jnp.int32),
             pltpu.SMEM(lens.shape, jnp.int32),
             pltpu.VMEM(tail, BF16),
+            pltpu.VMEM(rows_shape, BF16),
             pltpu.SemaphoreType.DMA((mine, length // SPAN)),
             pltpu.SemaphoreType.DMA((mine, length // SPAN)),
             pltpu.SemaphoreType.DMA((2,)),
+            pltpu.SemaphoreType.DMA((rows_shape[0] + 1,)),
         ],
-        outs=[VM, FAR],
-    )(in_hbm(table), in_hbm(lens), in_hbm(pool))
+        outs=[VM, FAR, FAR],
+    )(in_hbm(table), in_hbm(lens), in_hbm(pool), in_hbm(weight))
 
 
 def attention_kernel(lens, sel, arrived, fresh, start, far, out, cache, qs, os, sc, ef, sems):
@@ -521,9 +543,9 @@
         ],
     )(in_hbm(new_slot), in_hbm(routes), in_hbm(tokens), in_hbm(norm_gains))
     near = spread_req(message)
-    start, cache = pages_call(page_table, cache_len, kv_pages)
-    near, start, cache, shares, kept = lax.optimization_barrier(
-        (near, start, cache, shares, kept)
+    start, cache, picked = pages_call(page_table, cache_len, kv_pages, w_out, quarter)
+    near, start, cache, picked, shares, kept = lax.optimization_barrier(
+        (near, start, cache, picked, shares, kept)
     )
     far = other_core(near)
     wq, begun = call(
@@ -536,16 +558,12 @@
         query_kernel, [shape_of((req_count, rows, HD)), shape_of((total, HD))], [VM] * 4
     )(near, far, in_vmem(wq), begun)
     arrived = spread_req(ordered)
-    sel, fresh, picked = call(
+    sel, fresh = call(
         own_kernel,
-        [
-            shape_of((rows, HD), F32),
-            shape_of((2 * rows, wide)),
-            shape_of((rep_count // 2, w_out.shape[1], quarter)),
-        ],
-        [VM, VM, VM, FAR],
-        [pltpu.SemaphoreType.DMA((rep_count // 2,))],
-    )(near, far, w_kv, in_hbm(w_out))
+        [shape_of((rows, HD), F32), shape_of((2 * rows, wide))],
+        [VM, VM, FAR],
+        [pltpu.VMEM(w_kv.shape, BF16), pltpu.SemaphoreType.DMA((8,))],
+    )(near, far, in_hbm(w_kv))
     back = attention_call(cache_len, sel, arrived, fresh, start, cache)
     returned = spread_req(back)
     returned, picked = lax.optimization_barrier((returned, picked))

time: 131 us -> 129 us (0.985)
  blocking collectives: 64.1 us -> 61.1 us
  local copies, waits for them, and re-layouts: 4.95 us -> 2.08 us
  waiting for transfers between devices: 14.7 us -> 16.7 us
    all_to_all x1, blocking collectives: 15.4 us -> 12.4 us  [spread_req(): return lax.all_to_all(value, 'req', split_axis=0, concat_axis=0, tiled=True)]
    unnamed x18 -> x14, local copies, waits for them, and re-layouts: 2.91 us -> 0.04 us
    all_to_all x2, waiting for transfers between devices: 10 us -> 12 us  [spread_req(): return lax.all_to_all(value, 'req', split_axis=0, concat_axis=0, tiled=True)]
  transfers between devices with their start and end apart: 10 -> 10, of which waited for: 8 -> 8; matrix products, arithmetic and copies ran while one was open for 2% -> 2% of each run, Pallas kernels for 7% -> 8%
where the time goes in v8:
time: 129 us; the launch traced here: 128 us
  blocking collectives  61.1 us (47%)
  starting transfers between devices  27.5 us (21%)
  Pallas kernels  18.7 us (14%)
  waiting for transfers between devices  16.7 us (13%)
  local copies, waits for them, and re-layouts  2.08 us (2%)
    all_to_all x3, blocking collectives, spread_wide(): lax.all_to_all(value, ('req', 'rep'), split_axis=0, concat_axis=0, tiled=...  48.7 us
    all_to_all x2, starting transfers between devices, spread_req(): return lax.all_to_all(value, 'req', split_axis=0, concat_axis=0, tiled=True)  15 us
    all_to_all x1, blocking collectives, spread_req(): return lax.all_to_all(value, 'req', split_axis=0, concat_axis=0, tiled=True)  12.4 us
    all_to_all x2, waiting for transfers between devices, spread_req(): return lax.all_to_all(value, 'req', split_axis=0, concat_axis=0, tiled=True)  12 us
    ppermute x5, starting transfers between devices, other_core(): return lax.ppermute(value, 'rep', swap)  8.57 us
    pallas_call x1, Pallas kernels, pages_call(): call(page_kernel, [pltpu.VMEM((mine, SPAN) + pool.shape[2:], BF16), pltpu...  4.09 us
    ppermute x3, starting transfers between devices, shards(): lax.ppermute(piece, 'rep', [(p, p ^ m) for p in range(rep_count)])  3.88 us
    pallas_call x1, Pallas kernels, attention_call(): call(attention_kernel, shape_of(arrived.shape), [SM, VM, VM, VM, VM, FAR]...  3.8 us
  transfers between devices with their start and end apart: 10, of which 8 were waited for; matrix products, arithmetic and copies ran while one was open for 2% of the time, Pallas kernels for 8%

profile of v8, /device:TPU:1, one launch (start us, length us, event | category | flops | bytes accessed | tf_op | source)
XLA Modules:
  0.0 127.6 jit_solution(14080275950744443201)
XLA Ops:
  0.0 1.8 %shard_map.136 = bf16[32,8,1152]{2,1,0:T(8,128)(2,1)} custom-call(s32[4]{0:T(128)} %slots_far.1, s32[2,2,2,4]{3,2,1,0:T(2,128)} %bitcast.34, bf16[4,2,2048]{2,1,0:T(2,128)(2,1)} %tokens_far.1, f32[2,2048]{1,0:T(2,128)} %gains.3), custom_call_target="tpu_custom_call" | custom-call | tf_op jit(solution)/shard_map/pallas_call | solution.py:533
  1.8 11.2 %all-to-all-start = ((bf16[32,8,1152]{2,1,0:T(8,128)(2,1)}), bf16[32,8,1152]{2,1,0:T(8,128)(2,1)S(1)}, u32[]{:S(2)}, u32[]{:S(2)}) async-start(bf16[32,8,1152]{2,1,0:T(8,128)(2,1)} %shard_map.136), calls=%async_computation | async-start | bytes 1179648 | tf_op jit(solution)/shard_map/all_to_all | solution.py:508
  13.0 0.8 reshape.28
  13.8 0.7 convert_bitcast_fusion
  14.5 0.1 copy.24
  14.6 0.1 reshape.33
  14.7 0.8 copy.23
  15.5 0.1 eq.15
  15.5 0.1 select_reduce_fusion
  15.6 0.1 copy.25
  15.7 0.1 copy.26
  15.8 4.1 %shard_map.137 = (bf16[4,256,2,512]{3,2,1,0:T(2,128)(2,1)S(1)}, bf16[4,768,2,512]{3,2,1,0:T(2,128)(2,1)}, bf16[2,128,512]{2,1,0:T(8,128)(2,1)}) custom-call(s32[4,64]{1,0:T(4,128)} %table_far.1, s32[4]{0:T(128)} %lens.1, bf16[256,16,2,512]{3,2,1,0:T(2,128)(2,1)} %pool.1, bf16[1,128,2048]{2,1,0:T(8,128)(2,1)} %weight.4), custom_call_target="tpu_custom_call" | custom-call | tf_op jit(solution)/shard_map/pallas_call | solution.py:223
  19.9 6.1 %all-to-all-done.near = bf16[32,8,1152]{2,1,0:T(8,128)(2,1)S(1)} async-done(((bf16[32,8,1152]{2,1,0:T(8,128)(2,1)}), bf16[32,8,1152]{2,1,0:T(8,128)(2,1)S(1)}, u32[]{:S(2)}, u32[]{:S(2)}) %all-to-all-start) | async-done | bytes 589856 | tf_op jit(solution)/shard_map/all_to_all | solution.py:508
  26.0 2.2 %collective-permute-start = (bf16[32,8,1152]{2,1,0:T(8,128)(2,1)S(1)}, bf16[32,8,1152]{2,1,0:T(8,128)(2,1)S(1)}, u32[]{:S(2)}, u32[]{:S(2)}) collective-permute-start(bf16[32,8,1152]{2,1,0:T(8,128)(2,1)S(1)} %all-to-all-done.near), channel_id=1, source_target_pairs={{0,1},{1,0},{2,3},{3,2},{4,5},{5,4},{6,7},{7,6},{8,9},{9,8},{10,11... | collective-permute-start | bytes 1769480 | tf_op jit(solution)/shard_map/ppermute | solution.py:521
  28.2 1.3 %shard_map.138 = (bf16[1,2048,128]{2,1,0:T(8,128)(2,1)S(1)}, f32[256,128]{1,0:T(8,128)S(1)}) custom-call(bf16[32,8,1152]{2,1,0:T(8,128)(2,1)S(1)} %all-to-all-done.near, bf16[1,2048,128]{2,1,0:T(8,128)(2,1)} %wq_far.1), custom_call_target="tpu_custom_call" | custom-call | tf_op jit(solution)/shard_map/pallas_call | solution.py:551
  29.5 0.3 collective-permute-done.far
  29.8 1.1 shard_map.139
  30.9 3.8 %all-to-all-start.1 = ((bf16[32,8,128]{2,1,0:T(8,128)(2,1)}), bf16[32,8,128]{2,1,0:T(8,128)(2,1)S(1)}, u32[]{:S(2)}, u32[]{:S(2)}) async-start(bf16[32,8,128]{2,1,0:T(8,128)(2,1)} %get-tuple-element.37), calls=%async_computation.1 | async-start | bytes 131072 | tf_op jit(solution)/shard_map/all_to_all | solution.py:508
  34.8 0.0 copy-start.5
  34.8 2.7 %shard_map.140 = (f32[8,128]{1,0:T(8,128)S(1)}, bf16[16,512]{1,0:T(8,128)(2,1)S(1)}) custom-call(bf16[32,8,1152]{2,1,0:T(8,128)(2,1)S(1)} %all-to-all-done.near, bf16[32,8,1152]{2,1,0:T(8,128)(2,1)S(1)} %collective-permute-done.far, bf16[2048,2,512]{2,1,0:T(2,128)(2,1)} %wkv_far.1), custom_call_target="tpu_custom_call" | custom-call | tf_op jit(solution)/shard_map/pallas_call | solution.py:561
  37.5 6.0 %all-to-all-done.1.arrived = bf16[32,8,128]{2,1,0:T(8,128)(2,1)S(1)} async-done(((bf16[32,8,128]{2,1,0:T(8,128)(2,1)}), bf16[32,8,128]{2,1,0:T(8,128)(2,1)S(1)}, u32[]{:S(2)}, u32[]{:S(2)}) %all-to-all-start.1) | async-done | bytes 65568 | tf_op jit(solution)/shard_map/all_to_all | solution.py:508
  43.4 0.0 copy-done.5
  43.4 0.0 copy-start.6
  43.4 0.0 copy-start.3
  43.4 3.8 %shard_map.141 = bf16[32,8,128]{2,1,0:T(8,128)(2,1)S(1)} custom-call(s32[4]{0:T(128)S(1)} %copy-done.5, f32[8,128]{1,0:T(8,128)S(1)} %get-tuple-element.36.sel, bf16[32,8,128]{2,1,0:T(8,128)(2,1)S(1)} %all-to-all-done.1.arrived, bf16[16,512]{1,0:T(8,128)(2,1)S(1)} %get-tuple-element.38.fresh, bf16[4,256,2,512]{3,2,1,0:T(2,128)(2,1)S(1)} %get-tuple-element.39.start, ...), custom_call_target="tpu_custom_call" | custom-call | tf_op jit(solution)/shard_map/pallas_call | solution.py:370
  47.2 12.4 %all_to_all.30.returned = bf16[32,8,128]{2,1,0:T(8,128)(2,1)S(1)} all-to-all(bf16[32,8,128]{2,1,0:T(8,128)(2,1)S(1)} %shard_map.141), channel_id=1, replica_groups=mesh['req'=32,'rep'=4] {'req'}, dimensions={0} | all-to-all | bytes 131072 | tf_op jit(solution)/shard_map/all_to_all | solution.py:508
  59.7 0.0 copy-done.6
  59.7 2.7 %collective-permute-start.2 = (bf16[2,128,512]{2,1,0:T(8,128)(2,1)S(1)}, bf16[2,128,512]{2,1,0:T(8,128)(2,1)S(1)}, u32[]{:S(2)}, u32[]{:S(2)}) collective-permute-start(bf16[2,128,512]{2,1,0:T(8,128)(2,1)S(1)} %copy-done.6), channel_id=1, source_target_pairs={{0,1},{1,0},{2,3},{3,2},{4,5},{5,4},{6,7},{7,6},{8,9},{9,8},{10,11... | collective-permute-start | bytes 786440 | tf_op jit(solution)/shard_map/ppermute | solution.py:521
  62.3 0.0 collective-permute-start.1
  62.3 0.0 copy-done.3
  62.3 0.5 shard_map.142.part
  62.9 0.7 collective-permute-done.1.returned
  63.6 0.0 collective-permute-done.2.weight
  63.6 0.5 shard_map.143
  64.1 0.0 copy-start
  64.1 0.0 copy-start.1
  64.1 0.0 copy-start.4
  64.1 16.6 %all_to_all.31 = bf16[64,8,512]{2,1,0:T(8,128)(2,1)S(1)} all-to-all(bf16[64,8,512]{2,1,0:T(8,128)(2,1)S(1)} %bitcast.30), channel_id=1, replica_groups={{0,2,4,6,8,10,12,14,16,18,20,22,24,26,28,30,32,34,36,38,40,42,44,46,48,..., dimensions={0} | all-to-all | bytes 1048576 | tf_op jit(solution)/shard_map/all_to_all | solution.py:511
  80.8 0.1 convert_reduce_fusion.1
  80.9 0.1 multiply_reduce_fusion.1
  81.0 0.0 copy-start.2
  81.0 15.6 %all_to_all.32 = bf16[64,8,512]{2,1,0:T(8,128)(2,1)S(1)} all-to-all(bf16[64,8,512]{2,1,0:T(8,128)(2,1)S(1)} %broadcast_in_dim.29), channel_id=1, replica_groups={{0,2,4,6,8,10,12,14,16,18,20,22,24,26,28,30,32,34,36,38,40,42,44,46,48,..., dimensions={0} | all-to-all | bytes 1048576 | tf_op jit(solution)/shard_map/all_to_all | solution.py:511
  96.7 3.2 %collective-permute-start.3 = (bf16[64,8,512]{2,1,0:T(8,128)(2,1)S(1)}, bf16[64,8,512]{2,1,0:T(8,128)(2,1)S(1)}, u32[]{:S(2)}, u32[]{:S(2)}) collective-permute-start(bf16[64,8,512]{2,1,0:T(8,128)(2,1)S(1)} %all_to_all.32), channel_id=1, source_target_pairs={{0,1},{1,0},{2,3},{3,2},{4,5},{5,4},{6,7},{7,6},{8,9},{9,8},{10,11... | collective-permute-start | bytes 1572872 | tf_op jit(solution)/shard_map/ppermute | solution.py:521
  99.9 0.0 copy-done
  99.9 0.0 copy-done.1
  99.9 0.0 copy-done.4
  99.9 0.7 shard_map.144
  100.6 0.8 collective-permute-done.3
  101.4 0.0 copy-done.2
  101.4 1.1 shard_map.145
  102.5 0.5 collective-permute-start.4
  103.0 0.4 shard_map.146
  103.4 1.1 collective-permute-done.4
  104.5 0.2 add_convert_fusion
  104.7 16.4 %all_to_all.33 = bf16[64,8,512]{2,1,0:T(8,128)(2,1)S(1)} all-to-all(bf16[64,8,512]{2,1,0:T(8,128)(2,1)S(1)} %bitcast.32), channel_id=1, replica_groups={{0,2,4,6,8,10,12,14,16,18,20,22,24,26,28,30,32,34,36,38,40,42,44,46,48,..., dimensions={0} | all-to-all | bytes 1048576 | tf_op jit(solution)/shard_map/all_to_all | solution.py:511
  121.1 0.1 convert_reduce_fusion
  121.2 0.1 multiply_reduce_fusion
  121.3 2.2 %collective-permute-start.5 = (bf16[8,512]{1,0:T(8,128)(2,1)S(1)}, bf16[8,512]{1,0:T(8,128)(2,1)S(1)}, u32[]{:S(2)}, u32[]{:S(2)}) collective-permute-start(bf16[8,512]{1,0:T(8,128)(2,1)S(1)} %add_convert_fusion.1.refs_0_), channel_id=1, source_target_pairs={{0,1},{1,0},{2,3},{3,2},{4,5},{5,4},{6,7},{7,6},{8,9},{9,8},{10,11... | collective-permute-start | bytes 24584 | tf_op jit(solution)/shard_map/ppermute | solution.py:600
  123.5 0.4 collective-permute-start.6
  123.8 1.3 %collective-permute-start.7 = (bf16[8,512]{1,0:T(8,128)(2,1)S(1)}, bf16[8,512]{1,0:T(8,128)(2,1)S(1)}, u32[]{:S(2)}, u32[]{:S(2)}) collective-permute-start(bf16[8,512]{1,0:T(8,128)(2,1)S(1)} %add_convert_fusion.1.refs_0_), channel_id=1, source_target_pairs={{0,3},{1,2},{2,1},{3,0},{4,7},{5,6},{6,5},{7,4},{8,11},{9,10},{10,... | collective-permute-start | bytes 24584 | tf_op jit(solution)/shard_map/ppermute | solution.py:600
  125.2 0.0 collective-permute-done.5.refs_1_
  125.2 0.8 collective-permute-done.6.refs_2_
  126.0 1.0 collective-permute-done.7.refs_3_
  126.9 0.6 shard_map.147
  (5 shorter events, 0.1 us)
Async XLA Ops:
  1.8 24.2 %all-to-all-start = ((bf16[32,8,1152]{2,1,0:T(8,128)(2,1)}), bf16[32,8,1152]{2,1,0:T(8,128)(2,1)S(1)}, u32[]{:S(2)}, u32[]{:S(2)}) async-start(bf16[32,8,1152]{2,1,0:T(8,128)(2,1)} %shard_map.136), calls=%async_computation | async-start | bytes 1179648 | tf_op jit(solution)/shard_map/all_to_all | solution.py:508
  26.0 3.8 %collective-permute-start = (bf16[32,8,1152]{2,1,0:T(8,128)(2,1)S(1)}, bf16[32,8,1152]{2,1,0:T(8,128)(2,1)S(1)}, u32[]{:S(2)}, u32[]{:S(2)}) collective-permute-start(bf16[32,8,1152]{2,1,0:T(8,128)(2,1)S(1)} %all-to-all-done.near), channel_id=1, source_target_pairs={{0,1},{1,0},{2,3},{3,2},{4,5},{5,4},{6,7},{7,6},{8,9},{9,8},{10,11... | collective-permute-start | bytes 1769480 | tf_op jit(solution)/shard_map/ppermute | solution.py:521
  30.9 12.5 %all-to-all-start.1 = ((bf16[32,8,128]{2,1,0:T(8,128)(2,1)}), bf16[32,8,128]{2,1,0:T(8,128)(2,1)S(1)}, u32[]{:S(2)}, u32[]{:S(2)}) async-start(bf16[32,8,128]{2,1,0:T(8,128)(2,1)} %get-tuple-element.37), calls=%async_computation.1 | async-start | bytes 131072 | tf_op jit(solution)/shard_map/all_to_all | solution.py:508
  34.8 8.6 %copy-start.5 = (s32[4]{0:T(128)S(1)}, s32[4]{0:T(128)}, u32[]{:S(2)}) copy-start(s32[4]{0:T(128)} %lens.1) | copy-start | bytes 52
  43.4 16.2 %copy-start.6 = (bf16[2,128,512]{2,1,0:T(8,128)(2,1)S(1)}, bf16[2,128,512]{2,1,0:T(8,128)(2,1)}, u32[]{:S(2)}) copy-start(bf16[2,128,512]{2,1,0:T(8,128)(2,1)} %get-tuple-element.43) | copy-start | bytes 786436
  43.4 18.9 %copy-start.3 = (bf16[1,128,2048]{2,1,0:T(8,128)(2,1)S(1)}, bf16[1,128,2048]{2,1,0:T(8,128)(2,1)}, u32[]{:S(2)}) copy-start(bf16[1,128,2048]{2,1,0:T(8,128)(2,1)} %weight.4) | copy-start | bytes 1572868
  59.7 3.9 %collective-permute-start.2 = (bf16[2,128,512]{2,1,0:T(8,128)(2,1)S(1)}, bf16[2,128,512]{2,1,0:T(8,128)(2,1)S(1)}, u32[]{:S(2)}, u32[]{:S(2)}) collective-permute-start(bf16[2,128,512]{2,1,0:T(8,128)(2,1)S(1)} %copy-done.6), channel_id=1, source_target_pairs={{0,1},{1,0},{2,3},{3,2},{4,5},{5,4},{6,7},{7,6},{8,9},{9,8},{10,11... | collective-permute-start | bytes 786440 | tf_op jit(solution)/shard_map/ppermute | solution.py:521
  62.3 1.3 collective-permute-start.1
  64.1 35.8 %copy-start = (bf16[1,2048,352]{1,2,0:T(8,128)(2,1)S(1)}, bf16[1,2048,352]{1,2,0:T(8,128)(2,1)}, u32[]{:S(2)}) copy-start(bf16[1,2048,352]{1,2,0:T(8,128)(2,1)} %param.19) | copy-start | bytes 4325380
  64.1 35.8 %copy-start.1 = (bf16[1,2048,352]{1,2,0:T(8,128)(2,1)S(1)}, bf16[1,2048,352]{1,2,0:T(8,128)(2,1)}, u32[]{:S(2)}) copy-start(bf16[1,2048,352]{1,2,0:T(8,128)(2,1)} %param.20) | copy-start | bytes 4325380
  64.1 35.7 %copy-start.4 = (f32[2,2048]{1,0:T(2,128)S(1)}, f32[2,2048]{1,0:T(2,128)}, u32[]{:S(2)}) copy-start(f32[2,2048]{1,0:T(2,128)} %gains.3) | copy-start | bytes 49156
  81.0 20.4 %copy-start.2 = (bf16[1,352,2048]{2,1,0:T(8,128)(2,1)S(1)}, bf16[1,352,2048]{2,1,0:T(8,128)(2,1)}, u32[]{:S(2)}) copy-start(bf16[1,352,2048]{2,1,0:T(8,128)(2,1)} %weight.5) | copy-start | bytes 4325380
  96.7 4.8 %collective-permute-start.3 = (bf16[64,8,512]{2,1,0:T(8,128)(2,1)S(1)}, bf16[64,8,512]{2,1,0:T(8,128)(2,1)S(1)}, u32[]{:S(2)}, u32[]{:S(2)}) collective-permute-start(bf16[64,8,512]{2,1,0:T(8,128)(2,1)S(1)} %all_to_all.32), channel_id=1, source_target_pairs={{0,1},{1,0},{2,3},{3,2},{4,5},{5,4},{6,7},{7,6},{8,9},{9,8},{10,11... | collective-permute-start | bytes 1572872 | tf_op jit(solution)/shard_map/ppermute | solution.py:521
  102.5 2.0 %collective-permute-start.4 = (bf16[32,2,8,512]{3,2,1,0:T(8,128)(2,1)S(1)}, bf16[32,2,8,512]{3,2,1,0:T(8,128)(2,1)S(1)}, u32[]{:S(2)}, u32[]{:S(2)}) collective-permute-start(bf16[32,2,8,512]{3,2,1,0:T(8,128)(2,1)S(1)} %get-tuple-element.49), channel_id=1, source_target_pairs={{0,1},{1,0},{2,3},{3,2},{4,5},{5,4},{6,7},{7,6},{8,9},{9,8},{10,11... | collective-permute-start | bytes 1572872 | tf_op jit(solution)/shard_map/ppermute | solution.py:521
  121.3 3.9 %collective-permute-start.5 = (bf16[8,512]{1,0:T(8,128)(2,1)S(1)}, bf16[8,512]{1,0:T(8,128)(2,1)S(1)}, u32[]{:S(2)}, u32[]{:S(2)}) collective-permute-start(bf16[8,512]{1,0:T(8,128)(2,1)S(1)} %add_convert_fusion.1.refs_0_), channel_id=1, source_target_pairs={{0,1},{1,0},{2,3},{3,2},{4,5},{5,4},{6,7},{7,6},{8,9},{9,8},{10,11... | collective-permute-start | bytes 24584 | tf_op jit(solution)/shard_map/ppermute | solution.py:600
  123.5 2.5 %collective-permute-start.6 = (bf16[8,512]{1,0:T(8,128)(2,1)S(1)}, bf16[8,512]{1,0:T(8,128)(2,1)S(1)}, u32[]{:S(2)}, u32[]{:S(2)}) collective-permute-start(bf16[8,512]{1,0:T(8,128)(2,1)S(1)} %add_convert_fusion.1.refs_0_), channel_id=1, source_target_pairs={{0,2},{1,3},{2,0},{3,1},{4,6},{5,7},{6,4},{7,5},{8,10},{9,11},{10,... | collective-permute-start | bytes 24584 | tf_op jit(solution)/shard_map/ppermute | solution.py:600
  123.8 3.1 %collective-permute-start.7 = (bf16[8,512]{1,0:T(8,128)(2,1)S(1)}, bf16[8,512]{1,0:T(8,128)(2,1)S(1)}, u32[]{:S(2)}, u32[]{:S(2)}) collective-permute-start(bf16[8,512]{1,0:T(8,128)(2,1)S(1)} %add_convert_fusion.1.refs_0_), channel_id=1, source_target_pairs={{0,3},{1,2},{2,1},{3,0},{4,7},{5,6},{6,5},{7,4},{8,11},{9,10},{10,... | collective-permute-start | bytes 24584 | tf_op jit(solution)/shard_map/ppermute | solution.py:600
